TPU v7x, 32 devices: a whole 2x2x4 slice. The times are simulated.
32 devices in a mesh: shard: 8 (over y, x, core), group: 4 (over z).
Axes of the slice: x: 2, y: 2, z: 4, core: 2. Of those that a mesh axis runs over, the one named last changes fastest.
Arguments:
- layer_input_rows: bfloat16 [32768, 1472], P(('shard', 'group')), may hold values from -6 to 6
- gain_attn: bfloat16 [1472], P('group'), may hold values from 0.5 to 1.5
- w_query: bfloat16 [1472, 384], P('group'), may hold values from -0.0390625 to 0.0390625
- w_key: bfloat16 [1472, 384], P('group'), may hold values from -0.15625 to 0.15625
- w_value: bfloat16 [1472, 384], P('group'), may hold values from -0.15625 to 0.15625
- w_out: bfloat16 [384, 1472], P('group'), may hold values from -1.75 to 1.75
- gain_ff: bfloat16 [1472], P('group'), may hold values from 0.5 to 1.5
- gate_weight: bfloat16 [1472, 3584], P('group'), may hold values from -0.15625 to 0.15625
- w_up: bfloat16 [1472, 3584], P('group'), may hold values from -0.15625 to 0.15625
- w_down: bfloat16 [3584, 1472], P('group'), may hold values from -0.09375 to 0.09375
- bucket_head_bias: bfloat16 [32, 6], P('group'), may hold values from -4 to 4
- positions: int32 [32768], P(('shard', 'group')), may hold values from 0 to 766, as said below
- rel_bucket: int32 [1024], replicated, may hold values from 0 to 31, as said below
- out_grad: bfloat16 [32768, 1472], P(('shard', 'group')), may hold values from -6 to 6
Outputs:
- block_output: bfloat16 [32768, 1472], P(('shard', 'group'))
- input_grad: bfloat16 [32768, 1472], P(('shard', 'group'))
- grad_gain_attn: float32 [1472], P('group')
- grad_query: float32 [1472, 384], P('group')
- grad_key: float32 [1472, 384], P('group')
- grad_value: float32 [1472, 384], P('group')
- grad_out_proj: float32 [384, 1472], P('group')
- grad_gain_ff: float32 [1472], P('group')
- grad_gate: float32 [1472, 3584], P('group')
- grad_up: float32 [1472, 3584], P('group')
- grad_down: float32 [3584, 1472], P('group')
- grad_bias_table: float32 [32, 6], P('group')
Inputs may be any that keep to these rules, and one draw needn't show every extreme that they name: Each run of 512 tokens is one sequence whose positions rise by one from a start of 0 to 255; some sequence starts at 0 and some at 255. `rel_bucket`: entry r + 512 is the bucket of relative distance r (key minus query position): 0 at r = 0, not falling with |r|, 16 or more exactly where r > 0.
All inputs are finite; a program needn't handle non-finite values.
Results may differ from a plain program's by a relative error of at most 0.019.
Values may be sent and summed in bfloat16 or wider, within the bound.
No kernel may reach another device: no remote copies, remote signals or barrier semaphores. Data moves between devices by JAX's collectives and lax.ppermute only.
A program may use at most 320 MiB of HBM per device.

v0:
```python
import functools

import jax
import jax.numpy as jnp
from jax import lax
from jax.experimental import pallas as pl
from jax.experimental.pallas import tpu as pltpu
from jax.sharding import PartitionSpec as P

H = 6
DK = 64
SEQ = 512
BLOCK = 256
FLOOR = 1e-06
ROOT = 0.7978845608028654
CUBIC = 0.044715
RB = 128
MB = 512
VMEM_LIMIT = 60 << 20
NT = (((1,), (1,)), ((), ()))
TN = (((0,), (0,)), ((), ()))
ANY = pl.BlockSpec(memory_space=pl.ANY)
bf16 = jnp.bfloat16
f32 = jnp.float32
CORE, XBIT, YBIT = 1, 2, 4


def kernel_cost(us):
    return pl.CostEstimate(flops=int(us * 1.15e9), bytes_accessed=int(us * 1e6), transcendentals=0)


def skew_bias(off_ref, bias_ref):
    rows = jnp.broadcast_to(off_ref[0], (SEQ, 2 * SEQ))
    bias_ref[0] = pltpu.roll(rows, SEQ, 1, stride=1, stride_axis=0)[:, :SEQ].astype(bias_ref.dtype)


def bias_matrix(offsets):
    return pl.pallas_call(
        skew_bias,
        grid=(H,),
        in_specs=[pl.BlockSpec((1, 1, 2 * SEQ), lambda h: (h, 0, 0))],
        out_specs=pl.BlockSpec((1, SEQ, SEQ), lambda h: (h, 0, 0)),
        out_shape=jax.ShapeDtypeStruct((H, SEQ, SEQ), bf16),
        cost_estimate=kernel_cost(4),
        name="bias_matrix",
    )(offsets)


def half_lanes(v, side):
    lane = lax.broadcasted_iota(jnp.int32, v.shape, 1)
    return jnp.where((lane < DK) == (side == 0), v, jnp.zeros_like(v))


def attend_kernel(q_ref, k_ref, v_ref, bias_ref, row_ref, col_ref, attend_ref, ctx_ref):
    keys = k_ref[...]
    values = v_ref[...]
    col = col_ref[0]
    for b in range(SEQ // RB):
        rows = pl.ds(b * RB, RB)
        allowed = col <= row_ref[0, rows]
        ctx = None
        for side in range(2):
            s = lax.dot_general(half_lanes(q_ref[rows], side), keys, NT, preferred_element_type=f32)
            s = jnp.where(allowed, s + bias_ref[side, rows].astype(f32), -1e30)
            p = jnp.exp(s - jnp.max(s, axis=-1, keepdims=True))
            p = (p * (1.0 / jnp.sum(p, axis=-1, keepdims=True))).astype(bf16)
            attend_ref[0, side, rows] = p
            part = half_lanes(jnp.dot(p, values, preferred_element_type=f32), side)
            ctx = part if ctx is None else ctx + part
        ctx_ref[rows] = ctx.astype(bf16)


def pair(which):
    return pl.BlockSpec((SEQ, 2 * DK), lambda h, s: (s, which * (H // 2) + h))


def attend_forward(qkv, bias, row, col):
    n = qkv.shape[0] // SEQ
    return pl.pallas_call(
        attend_kernel,
        grid=(H // 2, n),
        in_specs=[
            pair(0),
            pair(1),
            pair(2),
            pl.BlockSpec((2, SEQ, SEQ), lambda h, s: (h, 0, 0)),
            pl.BlockSpec((1, SEQ, 1), lambda h, s: (s, 0, 0)),
            pl.BlockSpec((1, 1, SEQ), lambda h, s: (s, 0, 0)),
        ],
        out_specs=[pl.BlockSpec((1, 2, SEQ, SEQ), lambda h, s: (s, h, 0, 0)), pair(0)],
        out_shape=[jax.ShapeDtypeStruct((n, H, SEQ, SEQ), bf16), jax.ShapeDtypeStruct((n * SEQ, H * DK), bf16)],
        cost_estimate=kernel_cost(20),
        name="attend_forward",
    )(qkv, qkv, qkv, bias, row, col)


def attend_back_kernel(q_ref, k_ref, v_ref, attend_ref, dctx_ref, dq_ref, dk_ref, dv_ref, skew_ref, ds_ref, skew_sum):
    keys = k_ref[...]
    values = v_ref[...]

    @pl.when(pl.program_id(1) == 0)
    def _():
        skew_sum[...] = jnp.zeros_like(skew_sum)

    for b in range(SEQ // RB):
        rows = pl.ds(b * RB, RB)
        start = SEQ - RB * b
        dq = None
        for side in range(2):
            p = attend_ref[0, side, rows].astype(f32)
            da = lax.dot_general(half_lanes(dctx_ref[rows], side), values, NT, preferred_element_type=f32)
            ds = (p * (da - jnp.sum(p * da, axis=-1, keepdims=True))).astype(bf16)
            ds_ref[side, rows] = ds
            part = half_lanes(jnp.dot(ds, keys, preferred_element_type=f32), side)
            dq = part if dq is None else dq + part
            skew_sum[side, :, start : start + SEQ] += ds.astype(f32)
        dq_ref[rows] = dq.astype(bf16)
    dk, dv = None, None
    for side in range(2):
        part = half_lanes(lax.dot_general(ds_ref[side], q_ref[...], TN, preferred_element_type=f32), side)
        dk = part if dk is None else dk + part
        part = half_lanes(lax.dot_general(attend_ref[0, side], dctx_ref[...], TN, preferred_element_type=f32), side)
        dv = part if dv is None else dv + part
    dk_ref[...] = dk.astype(bf16)
    dv_ref[...] = dv.astype(bf16)

    @pl.when(pl.program_id(1) == pl.num_programs(1) - 1)
    def _():
        for side in range(2):
            total = skew_sum[side, 0:8]
            for u in range(1, RB // 8):
                total += pltpu.roll(skew_sum[side, 8 * u : 8 * u + 8], 2 * SEQ - 8 * u, 1)
            row = lax.broadcasted_iota(jnp.int32, total.shape, 0)
            for bit in (1, 2, 4):
                total = jnp.where((row & bit) != 0, pltpu.roll(total, 2 * SEQ - bit, 1), total)
            skew_ref[side] = jnp.sum(total, axis=0, keepdims=True)


def attend_backward(qkv, attend, dctx):
    n = qkv.shape[0] // SEQ
    out = jax.ShapeDtypeStruct(dctx.shape, bf16)
    return pl.pallas_call(
        attend_back_kernel,
        grid=(H // 2, n),
        in_specs=[pair(0), pair(1), pair(2), pl.BlockSpec((1, 2, SEQ, SEQ), lambda h, s: (s, h, 0, 0)), pair(0)],
        out_specs=[pair(0), pair(0), pair(0), pl.BlockSpec((2, 1, 2 * SEQ), lambda h, s: (h, 0, 0))],
        out_shape=[out, out, out, jax.ShapeDtypeStruct((H, 1, 2 * SEQ), f32)],
        scratch_shapes=[pltpu.VMEM((2, SEQ, SEQ), bf16), pltpu.VMEM((2, RB, 2 * SEQ), f32)],
        cost_estimate=kernel_cost(22),
        name="attend_backward",
    )(qkv, qkv, qkv, attend, dctx)


class Copies:
    def __init__(self, sems):
        self.sems = sems; self.count = 0
    def start(self, src, dst):
        copy = pltpu.make_async_copy(src, dst, self.sems.at[self.count])
        self.count += 1
        copy.start()
        return copy

def wait(copies):
    for c in copies: c.wait()

def load_gate_up(copies, scal, wgu, own_gate, own_up, mine, other, groups):
    z, chunk, core = scal[0], scal[1], scal[2]
    block = own_gate.shape[1]
    started = []
    if other is None:
        for side in range(2):
            for at in range(groups):
                started.append(copies.start(mine.at[side, at], wgu.at[side, at * block : (at + 1) * block]))
        return started
    here = pl.ds(pl.multiple_of(z * block, 16), block)
    started.append(copies.start(own_gate.at[chunk], wgu.at[0, here]))
    started.append(copies.start(own_up.at[chunk], wgu.at[1, here]))
    for k in range(1, groups):
        at = lax.rem(z - k + groups, groups) * block
        for parts, side in ((mine, core), (other, 1 - core)):
            base = 0
            for part in parts:
                n = part.shape[1]
                started.append(copies.start(part.at[k - 1], wgu.at[side, pl.ds(pl.multiple_of(at + base, 8), n)]))
                base += n
    return started

def load_down(copies, scal, wd, own_down, mine, other, groups):
    z, chunk, core = scal[0], scal[1], scal[2]
    block = own_down.shape[1]
    if other is None:
        started = []
        half = block // 2
        for side in range(2):
            for at in range(groups):
                base = at * block + side * half
                started.append(copies.start(mine.at[side, at], wd.at[base : base + half]))
        return started
    started = [copies.start(own_down.at[chunk], wd.at[pl.ds(pl.multiple_of(z * block, 8), block)])]
    for k in range(1, groups):
        at = lax.rem(z - k + groups, groups) * block
        for parts, side in ((mine, core), (other, 1 - core)):
            base = at + side * (block // 2)
            for part in parts:
                n = part.shape[1]
                started.append(copies.start(part.at[k - 1], wd.at[pl.ds(pl.multiple_of(base, 8), n)]))
                base = base + n
    return started

def take_parts(it, n):
    if n == 0:
        return next(it), None
    return [next(it) for _ in range(n)], [next(it) for _ in range(n)]


def parts_of(source):
    if not isinstance(source, tuple):
        return 0, [source], source.shape[0] * source.shape[1]
    mine, other = source
    return len(mine), [*mine, *other], 2 + 2 * len(mine) * mine[0].shape[0]


def ffn_kernel(groups, nparts, *refs):
    it = iter(refs)
    scal = next(it); x_h, xt_h, g_h, own_gate, own_up, own_down = [next(it) for _ in range(6)]
    mine, other = take_parts(it, nparts[0])
    mine_d, other_d = take_parts(it, nparts[1])
    hid_h, dg_h, du_h, gm_h, go_h, gdm_h, gdo_h = [next(it) for _ in range(7)]
    x, xt, g, wgu, wd, hid, dga, dup, hidt, ggu, gd, sems = [next(it) for _ in range(12)]
    copies = Copies(sems)
    core = scal[2]
    c_x = copies.start(x_h, x)
    c_gu = load_gate_up(copies, scal, wgu, own_gate, own_up, mine, other, groups)
    c_g = copies.start(g_h, g)
    c_d = load_down(copies, scal, wd, own_down, mine_d, other_d, groups)
    c_xt = copies.start(xt_h, xt)
    c_x.wait(); wait(c_gu); c_g.wait(); wait(c_d)
    tokens = x.shape[0]
    mb = MB
    def rows_step(m, _):
        rows = pl.ds(pl.multiple_of(m * mb, mb), mb)
        xm = x[rows]
        v = jnp.dot(xm, wgu[0], preferred_element_type=f32).astype(bf16).astype(f32)
        u = jnp.dot(xm, wgu[1], preferred_element_type=f32).astype(bf16).astype(f32)
        dh = lax.dot_general(g[rows], wd[...], NT, preferred_element_type=f32)
        sq = v * v
        half = 0.5 + 0.5 * jnp.tanh(v * (ROOT + (ROOT * 0.044715) * sq))
        act = v * half
        slope = half + (2.0 * v * half) * ((1.0 - half) * (ROOT + (3 * 0.044715 * ROOT) * sq))
        h = (act * u).astype(bf16)
        hid[rows] = h
        dga[rows] = (dh * u * slope).astype(bf16)
        dup[rows] = (dh * act).astype(bf16)
        hidt[:, rows] = h.T
        return 0
    lax.fori_loop(0, tokens // mb, rows_step, 0)
    c_out = [copies.start(hid, hid_h), copies.start(dga, dg_h), copies.start(dup, du_h)]
    block = own_down.shape[1]
    half_block = block // 2
    def down_step(b, _):
        rows = pl.ds(pl.multiple_of(b * block, 16), block)
        gd[rows] = jnp.dot(hidt[rows], g[...], preferred_element_type=f32).astype(bf16)
        return 0
    lax.fori_loop(0, groups, down_step, 0)
    for b in range(groups):
        for side, dst in ((core, gdm_h), (1 - core, gdo_h)):
            c_out.append(copies.start(gd.at[pl.ds(pl.multiple_of(b * block + side * half_block, 8), half_block)], dst.at[b]))
    c_xt.wait()
    block = own_gate.shape[1]
    for i, act in ((0, dga), (1, dup)):
        def gate_step(b, _, i=i, act=act):
            rows = pl.ds(pl.multiple_of(b * block, 16), block)
            ggu[i, rows] = jnp.dot(xt[rows], act[...], preferred_element_type=f32).astype(bf16)
            return 0
        lax.fori_loop(0, groups, gate_step, 0)
    c_out.append(copies.start(ggu.at[core], gm_h))
    c_out.append(copies.start(ggu.at[1 - core], go_h))
    wait(c_out)

def ffn_chunk(scal, x, xt, g, own_gate, own_up, own_down, gate_up, down):
    tokens, d = x.shape
    groups = d // own_gate.shape[1]
    f = own_gate.shape[2]
    n_gu, arrays_gu, copies_gu = parts_of(gate_up)
    n_d, arrays_d, copies_d = parts_of(down)
    nparts = (n_gu, n_d)
    act = jax.ShapeDtypeStruct((tokens, f), bf16)
    gu = jax.ShapeDtypeStruct((d, f), bf16)
    gdn = jax.ShapeDtypeStruct((groups, own_down.shape[1] // 2, d), bf16)
    ins = [x, xt, g, own_gate, own_up, own_down, *arrays_gu, *arrays_d]
    ncop = 3 + copies_gu + copies_d + 3 + 2 * groups + 2
    V = lambda s: pltpu.VMEM(s, bf16)
    return pl.pallas_call(
        functools.partial(ffn_kernel, groups, nparts),
        in_specs=[pl.BlockSpec(memory_space=pltpu.SMEM)] + [ANY] * len(ins),
        out_specs=[ANY] * 7,
        out_shape=[act, act, act, gu, gu, gdn, gdn],
        scratch_shapes=[V((tokens, d)), V((d, tokens)), V((tokens, d)), V((2, d, f)), V((f, d)), V((tokens, f)), V((tokens, f)), V((tokens, f)), V((f, tokens)), V((2, d, f)), V((f, d)), pltpu.SemaphoreType.DMA((ncop,))],
        compiler_params=pltpu.CompilerParams(vmem_limit_bytes=VMEM_LIMIT),
        cost_estimate=kernel_cost(30),
        name="ffn_chunk",
    )(scal, *ins)

TB = 256


def norm_back_columns(values, gain, grad):
    r = lax.rsqrt(jnp.mean(values * values, axis=0, keepdims=True) + FLOOR)
    scaled = gain * grad
    back = r * scaled - values * ((r * r * r) * jnp.mean(scaled * values, axis=0, keepdims=True))
    return back, jnp.sum(grad * values * r, axis=1, keepdims=True)


def dx_kernel(groups, counts, *refs):
    it = iter(refs)
    scal = next(it)
    gain_h, middle_h, g_h = next(it), next(it), next(it)
    own_gate, own_up = next(it), next(it)
    chunks = []
    for n in counts:
        dg, du = next(it), next(it)
        chunks.append((dg, du, *take_parts(it, n)))
    dm_h, da_h, gg_h = next(it), next(it), next(it)
    acc, wgu, dga, dup, middle, g, gain, gg, sems = [next(it) for _ in range(9)]
    copies = Copies(sems)
    tokens = acc.shape[1]

    def load(j):
        dg, du, mine, other = chunks[j]
        s = (scal[0], scal[1] ^ j, scal[2])
        out = load_gate_up(copies, s, wgu.at[j % 2], own_gate, own_up, mine, other, groups)
        return out + [copies.start(dg, dga.at[j % 2]), copies.start(du, dup.at[j % 2])]

    pending = load(0)
    extra = [copies.start(gain_h, gain), copies.start(middle_h, middle), copies.start(g_h, g)]
    for j in range(len(chunks)):
        following = load(j + 1) if j + 1 < len(chunks) else []
        wait(pending)
        pending = following
        b = j % 2

        def step(m, _, j=j, b=b):
            at = pl.ds(pl.multiple_of(m * MB, MB), MB)
            part = lax.dot_general(wgu[b, 0], dga[b, at], NT, preferred_element_type=f32)
            part += lax.dot_general(wgu[b, 1], dup[b, at], NT, preferred_element_type=f32)
            acc[:, at] = part if j == 0 else acc[:, at] + part
            return 0

        lax.fori_loop(0, tokens // MB, step, 0)
    wait(extra)
    gg[...] = jnp.zeros_like(gg)

    def finish(m, _):
        at = pl.ds(pl.multiple_of(m * TB, TB), TB)
        back, part = norm_back_columns(middle[:, at], gain[...], acc[:, at])
        total = g[:, at].astype(f32) + back
        acc[:, at] = total
        g[:, at] = total.astype(bf16)
        gg[...] += part
        return 0

    lax.fori_loop(0, tokens // TB, finish, 0)
    wait([copies.start(g, da_h), copies.start(acc, dm_h), copies.start(gg, gg_h)])


def ffn_dx(scal, gain, middle_t, g_t, own_gate, own_up, chunks):
    tokens, f = chunks[0][0].shape
    d = middle_t.shape[0]
    groups = d // own_gate.shape[1]
    ins = [gain, middle_t, g_t, own_gate, own_up]
    ncop = 6
    counts = []
    for dg, du, source in chunks:
        n, arrays, copies = parts_of(source)
        counts.append(n)
        ins += [dg, du, *arrays]
        ncop += 2 + copies
    V = lambda s: pltpu.VMEM(s, bf16)
    F = lambda s: pltpu.VMEM(s, f32)
    return pl.pallas_call(
        functools.partial(dx_kernel, groups, tuple(counts)),
        in_specs=[pl.BlockSpec(memory_space=pltpu.SMEM)] + [ANY] * len(ins),
        out_specs=[ANY, ANY, ANY],
        out_shape=[jax.ShapeDtypeStruct((d, tokens), f32), jax.ShapeDtypeStruct((d, tokens), bf16), jax.ShapeDtypeStruct((d, 1), f32)],
        scratch_shapes=[F((d, tokens)), V((2, 2, d, f)), V((2, tokens, f)), V((2, tokens, f)), F((d, tokens)), V((d, tokens)), F((d, 1)), F((d, 1)), pltpu.SemaphoreType.DMA((ncop,))],
        compiler_params=pltpu.CompilerParams(vmem_limit_bytes=VMEM_LIMIT),
        cost_estimate=kernel_cost(35),
        name="ffn_dx",
    )(scal, *ins)


def middle_kernel(ctx_ref, w_ref, x_ref, gain_ref, mid_ref, nt_ref, n_ref):
    mid = x_ref[...].astype(f32) + lax.dot_general(w_ref[...], ctx_ref[...], NT, preferred_element_type=f32)
    mid_ref[...] = mid
    normed = mid * lax.rsqrt(jnp.mean(mid * mid, axis=0, keepdims=True) + FLOOR) * gain_ref[...]
    nt_ref[...] = normed.astype(bf16)
    n_ref[...] = normed.T.astype(bf16)


def middle_norm(context, wo_t, x_t, gain):
    d, tokens = x_t.shape
    width = context.shape[1]
    cols = pl.BlockSpec((d, TB), lambda i: (0, i))
    return pl.pallas_call(
        middle_kernel,
        grid=(tokens // TB,),
        in_specs=[pl.BlockSpec((TB, width), lambda i: (i, 0)), pl.BlockSpec((d, width), lambda i: (0, 0)), cols, pl.BlockSpec((d, 1), lambda i: (0, 0))],
        out_specs=[cols, cols, pl.BlockSpec((TB, d), lambda i: (i, 0))],
        out_shape=[jax.ShapeDtypeStruct((d, tokens), f32), jax.ShapeDtypeStruct((d, tokens), bf16), jax.ShapeDtypeStruct((tokens, d), bf16)],
        compiler_params=pltpu.CompilerParams(vmem_limit_bytes=VMEM_LIMIT),
        cost_estimate=kernel_cost(7),
        name="middle_norm",
    )(context, wo_t, x_t, gain)


def input_kernel(dq_ref, dk_ref, dv_ref, w_ref, x_ref, dm_ref, gain_ref, out_ref, gg_ref):
    grads = jnp.concatenate([dq_ref[...], dk_ref[...], dv_ref[...]], axis=1)
    d_normed = lax.dot_general(w_ref[...], grads, NT, preferred_element_type=f32)
    back, part = norm_back_columns(x_ref[...].astype(f32), gain_ref[...], d_normed)
    out_ref[...] = (dm_ref[...] + back).astype(bf16)

    @pl.when(pl.program_id(0) == 0)
    def _():
        gg_ref[...] = jnp.zeros_like(gg_ref)

    gg_ref[...] += part


def input_gradient(dq, dk, dv, wqkv, x_t, dm_t, gain):
    d, tokens = x_t.shape
    width = dq.shape[1]
    head = pl.BlockSpec((TB, width), lambda i: (i, 0))
    cols = pl.BlockSpec((d, TB), lambda i: (0, i))
    one = pl.BlockSpec((d, 1), lambda i: (0, 0))
    return pl.pallas_call(
        input_kernel,
        grid=(tokens // TB,),
        in_specs=[head, head, head, pl.BlockSpec((d, 3 * width), lambda i: (0, 0)), cols, cols, one],
        out_specs=[cols, one],
        out_shape=[jax.ShapeDtypeStruct((d, tokens), bf16), jax.ShapeDtypeStruct((d, 1), f32)],
        compiler_params=pltpu.CompilerParams(vmem_limit_bytes=VMEM_LIMIT),
        cost_estimate=kernel_cost(8),
        name="input_gradient",
    )(dq, dk, dv, wqkv, x_t, dm_t, gain)


def matrices_kernel(groups, *refs):
    scal, nt_h, dq_h, dk_h, dv_h, ctx_h, da_h, small_h, mine_h, other_h = refs[:10]
    nt, dqkv, ctx, ctx_t, da, small, buf, sems = refs[10:]
    d, tokens = nt.shape
    width = ctx.shape[1]
    rows = d // groups
    half = width // 2
    copies = Copies(sems)
    c_out = [copies.start(ctx_h, ctx), copies.start(da_h, da)]
    c_in = [copies.start(nt_h, nt), copies.start(small_h, small)]
    c_in += [copies.start(src, dqkv.at[m]) for m, src in enumerate((dq_h, dk_h, dv_h))]
    wait(c_out)
    ctx_t[...] = ctx[...].T
    grad_out = lax.dot_general(ctx_t[...], da[...], NT, preferred_element_type=f32).astype(bf16)
    n = width // groups
    for z in range(groups):
        for i in range(4):
            block = grad_out[z * n : (z + 1) * n, i * width : min(d, (i + 1) * width)]
            if block.shape[1] < width:
                block = jnp.concatenate([block, jnp.zeros((n, width - block.shape[1]), bf16)], axis=1)
            buf[i // 2, 3, z, (i % 2) * n : (i % 2 + 1) * n] = block
    wait(c_in)
    for m in range(3):

        def step(z, _, m=m):
            part = jnp.dot(nt[pl.ds(pl.multiple_of(z * rows, 16), rows)], dqkv[m], preferred_element_type=f32).astype(bf16)
            buf[0, m, z] = part[:half]
            buf[1, m, z, : rows - half] = part[half:]
            buf[1, m, z, rows - half :] = small[z]
            return 0

        lax.fori_loop(0, groups, step, 0)
    wait([copies.start(buf.at[scal[2]], mine_h), copies.start(buf.at[1 - scal[2]], other_h)])


def attention_matrices(scal, normed_t, dq, dk, dv, ctx, da_t, small):
    d, tokens = normed_t.shape
    groups = small.shape[0]
    width = dq.shape[1]
    out = jax.ShapeDtypeStruct((4, groups, width // 2, width), bf16)
    V = lambda s: pltpu.VMEM(s, bf16)
    return pl.pallas_call(
        functools.partial(matrices_kernel, groups),
        in_specs=[pl.BlockSpec(memory_space=pltpu.SMEM)] + [ANY] * 7,
        out_specs=[ANY, ANY],
        out_shape=[out, out],
        scratch_shapes=[V((d, tokens)), V((3, tokens, width)), V((tokens, width)), V((width, tokens)), V((d, tokens)), V(small.shape), V((2, *out.shape)), pltpu.SemaphoreType.DMA((9,))],
        compiler_params=pltpu.CompilerParams(vmem_limit_bytes=VMEM_LIMIT),
        cost_estimate=kernel_cost(9),
        name="attention_matrices",
    )(scal, normed_t, dq, dk, dv, ctx, da_t, small)


def out_kernel(groups, counts, *refs):
    it = iter(refs)
    scal = next(it)
    middle, own_down = next(it), next(it)
    chunks = []
    for n in counts:
        hid = next(it)
        chunks.append((hid, *take_parts(it, n)))
    out_h = next(it)
    acc, mid, out, wd, act, sems = [next(it) for _ in range(6)]
    copies = Copies(sems)

    def load(j):
        hid, mine, other = chunks[j]
        s = (scal[0], scal[1] ^ j, scal[2])
        return load_down(copies, s, wd.at[j % 2], own_down, mine, other, groups) + [copies.start(hid, act.at[j % 2])]

    c_middle = copies.start(middle, mid)
    pending = load(0)
    for j in range(len(chunks)):
        following = load(j + 1) if j + 1 < len(chunks) else []
        wait(pending)
        pending = following
        b = j % 2

        def step(m, _, j=j, b=b):
            rows = pl.ds(pl.multiple_of(m * MB, MB), MB)
            part = jnp.dot(act[b, rows], wd[b], preferred_element_type=f32)
            acc[rows] = part if j == 0 else acc[rows] + part
            return 0

        lax.fori_loop(0, acc.shape[0] // MB, step, 0)
    c_middle.wait()

    def finish(m, _):
        at = pl.ds(pl.multiple_of(m * TB, TB), TB)
        out[:, at] = (mid[:, at] + acc[at].T).astype(bf16)
        return 0

    lax.fori_loop(0, acc.shape[0] // TB, finish, 0)
    done = copies.start(out, out_h)
    done.wait()


def ffn_out(scal, middle, own_down, chunks):
    d, tokens = middle.shape
    f = chunks[0][0].shape[1]
    groups = f // own_down.shape[1]
    ins = [middle, own_down]
    ncop = 2
    counts = []
    for hid, source in chunks:
        n, arrays, copies = parts_of(source)
        counts.append(n)
        ins += [hid, *arrays]
        ncop += 1 + copies
    V = lambda s: pltpu.VMEM(s, bf16)
    return pl.pallas_call(
        functools.partial(out_kernel, groups, tuple(counts)),
        in_specs=[pl.BlockSpec(memory_space=pltpu.SMEM)] + [ANY] * len(ins),
        out_specs=ANY,
        out_shape=jax.ShapeDtypeStruct((d, tokens), bf16),
        scratch_shapes=[pltpu.VMEM((tokens, d), f32), pltpu.VMEM((d, tokens), f32), V((d, tokens)), V((2, f, d)), V((2, tokens, f)), pltpu.SemaphoreType.DMA((ncop,))],
        compiler_params=pltpu.CompilerParams(vmem_limit_bytes=VMEM_LIMIT),
        cost_estimate=kernel_cost(21),
        name="ffn_out",
    )(scal, *ins)


def split_kernel(gate_ref, up_ref, og_ref, ou_ref):
    quarter = og_ref.shape[0]
    width = og_ref.shape[2] // quarter
    for src, dst in ((gate_ref, og_ref), (up_ref, ou_ref)):
        for p in range(quarter):
            for b in range(quarter):
                at = (b * quarter + p) * width
                dst[p, :, b * width : (b + 1) * width] = src[:, at : at + width]


def split_columns(gate, up):
    rows, ff = gate.shape
    tile = rows // 2
    out = jax.ShapeDtypeStruct((4, rows, ff // 4), bf16)
    return pl.pallas_call(
        split_kernel,
        grid=(2,),
        in_specs=[pl.BlockSpec((tile, ff), lambda i: (i, 0))] * 2,
        out_specs=[pl.BlockSpec((4, tile, ff // 4), lambda i: (0, i, 0))] * 2,
        out_shape=[out, out],
        cost_estimate=kernel_cost(5),
        name="split_columns",
    )(gate, up)


def join_kernel(scal, *refs):
    mine, other, gate_ref, up_ref = refs
    me, core = scal[1], scal[2]
    width = mine.shape[2] // 4

    def put(p, j, side):
        for src, dst in ((mine, (gate_ref, up_ref)[side]), (other, (gate_ref, up_ref)[1 - side])):
            for b in range(4):
                at = (b * 4 + p) * width
                dst[:, at : at + width] = src[j, :, b * width : (b + 1) * width].astype(f32)

    for own in range(4):
        for side in range(2):

            @pl.when(jnp.logical_and(me == own, core == side))
            def _(own=own, side=side):
                for j in range(4):
                    put(own ^ j, j, side)


def join_columns(scal, mine, other):
    _, rows, f = mine.shape
    tile = rows // 2
    out = jax.ShapeDtypeStruct((rows, 4 * f), f32)
    return pl.pallas_call(
        join_kernel,
        grid=(2,),
        in_specs=[pl.BlockSpec(memory_space=pltpu.SMEM)] + [pl.BlockSpec((4, tile, f), lambda i: (0, i, 0))] * 2,
        out_specs=[pl.BlockSpec((tile, 4 * f), lambda i: (i, 0))] * 2,
        out_shape=[out, out],
        cost_estimate=kernel_cost(6.5),
        compiler_params=pltpu.CompilerParams(vmem_limit_bytes=VMEM_LIMIT),
        name="join_columns",
    )(scal, mine, other)


def weights_kernel(groups, *refs):
    scal = refs[0]
    mine, other = refs[1:5], refs[5:9]
    wqkv, wo, smalls, buf, flat, sems = refs[9:]
    rows = wqkv.shape[0] // groups
    width = buf.shape[-1]
    half = width // 2
    out_rows = width // groups
    d = wo.shape[0]
    copies = Copies(sems)
    done = []
    for j in range(4):
        for side, arrays in ((scal[2], mine), (1 - scal[2], other)):
            for k in range(groups):
                z = lax.rem(scal[0] - k + groups, groups)
                done.append(copies.start(arrays[j].at[k], buf.at[scal[1] ^ j, z, pl.ds(pl.multiple_of(side * half, 16), half)]))
    wait(done)
    for z in range(groups):
        for m in range(3):
            wqkv[z * rows : (z + 1) * rows, m * width : (m + 1) * width] = buf[m, z, :rows]
        for i in range(-(-d // width)):
            n = min(width, d - i * width)
            flat[z * out_rows : (z + 1) * out_rows, i * width : i * width + n] = buf[3, z, i * out_rows : (i + 1) * out_rows, :n]
        smalls[z] = buf[0, z, rows:]
    wo[...] = flat[...].T


def attention_weights(scal, mine, other, rows, d):
    groups, half, width = mine[0].shape
    V = pl.BlockSpec(memory_space=pltpu.VMEM)
    return pl.pallas_call(
        functools.partial(weights_kernel, groups),
        in_specs=[pl.BlockSpec(memory_space=pltpu.SMEM)] + [ANY] * 8,
        out_specs=[V, V, V],
        out_shape=[
            jax.ShapeDtypeStruct((groups * rows, 3 * width), bf16),
            jax.ShapeDtypeStruct((d, width), bf16),
            jax.ShapeDtypeStruct((groups, width - rows, width), bf16),
        ],
        scratch_shapes=[pltpu.VMEM((4, groups, width, width), bf16), pltpu.VMEM((width, d), bf16), pltpu.SemaphoreType.DMA((8 * groups,))],
        cost_estimate=kernel_cost(5.8),
        compiler_params=pltpu.CompilerParams(vmem_limit_bytes=VMEM_LIMIT),
        name="attention_weights",
    )(scal, *mine, *other)


def gradients_kernel(*refs):
    scal = refs[0]
    mine, other = refs[1:3]
    grads, grad_out, small, buf, sems = refs[3], refs[4], refs[5], refs[6], refs[7]
    rows = grads.shape[1]
    width = buf.shape[-1]
    half = width // 2
    out_rows, d = grad_out.shape
    copies = Copies(sems)
    done = []
    for j in range(4):
        for side, arrays in ((scal[2], mine), (1 - scal[2], other)):
            done.append(copies.start(arrays.at[j], buf.at[scal[1] ^ j, pl.ds(pl.multiple_of(side * half, 16), half)]))
    wait(done)
    for m in range(3):
        grads[m] = buf[m, :rows].astype(f32)
    for i in range(-(-d // width)):
        n = min(width, d - i * width)
        grad_out[:, i * width : i * width + n] = buf[3, i * out_rows : (i + 1) * out_rows, :n].astype(f32)
    small[...] = buf[0, rows:].astype(f32)


def attention_gradients(scal, mine, other, rows, out_rows, d):
    _, half, width = mine.shape
    V = pl.BlockSpec(memory_space=pltpu.VMEM)
    return pl.pallas_call(
        gradients_kernel,
        in_specs=[pl.BlockSpec(memory_space=pltpu.SMEM)] + [ANY] * 2,
        out_specs=[V, V, V],
        out_shape=[
            jax.ShapeDtypeStruct((3, rows, width), f32),
            jax.ShapeDtypeStruct((out_rows, d), f32),
            jax.ShapeDtypeStruct((width - rows, width), f32),
        ],
        scratch_shapes=[pltpu.VMEM((4, width, width), bf16), pltpu.SemaphoreType.DMA((8,))],
        cost_estimate=kernel_cost(3.5),
        compiler_params=pltpu.CompilerParams(vmem_limit_bytes=VMEM_LIMIT),
        name="attention_gradients",
    )(scal, mine, other)


def down_kernel(*refs):
    scal = refs[0]
    mine, other = refs[1:3]
    out, buf, sems = refs[3:]
    half = buf.shape[0] // 8
    copies = Copies(sems)
    done = []
    for j in range(4):
        for side, arrays in ((scal[2], mine), (1 - scal[2], other)):
            at = ((scal[1] ^ j) * 2 + side) * half
            done.append(copies.start(arrays.at[j], buf.at[pl.ds(pl.multiple_of(at, 16), half)]))
    wait(done)
    for i in range(buf.shape[0] // 128):
        rows = slice(i * 128, (i + 1) * 128)
        out[:, rows] = buf[rows].astype(f32).T


def down_gradient(scal, mine, other):
    _, half, d = mine.shape
    return pl.pallas_call(
        down_kernel,
        in_specs=[pl.BlockSpec(memory_space=pltpu.SMEM)] + [ANY] * 2,
        out_specs=pl.BlockSpec(memory_space=pltpu.VMEM),
        out_shape=jax.ShapeDtypeStruct((d, 8 * half), f32),
        scratch_shapes=[pltpu.VMEM((8 * half, d), bf16), pltpu.SemaphoreType.DMA((8,))],
        cost_estimate=kernel_cost(5.6),
        compiler_params=pltpu.CompilerParams(vmem_limit_bytes=VMEM_LIMIT),
        name="down_gradient",
    )(scal, mine, other)


def dot(left, right, form):
    return jnp.einsum(form, left, right, preferred_element_type=f32)


def add(*terms):
    total = terms[0].astype(f32)
    for term in terms[1:]:
        total = total + term.astype(f32)
    return total.astype(bf16)


def after(v, *others):
    return lax.optimization_barrier((v, others))[0]


def pick(stack, i):
    return lax.dynamic_index_in_dim(stack, i, 0, keepdims=False)


SHARD = ("outer", "chip", "core")


class Links:
    def __init__(self, shards, groups):
        self.shards, self.groups = shards, groups
        self.z = lax.axis_index("group")
        self.index = lax.axis_index(SHARD)
        self.core = self.index & 1
        self.chip = (self.index >> 1) & 3

    def swap(self, v, bit):
        return lax.ppermute(v, SHARD, [(i, i ^ bit) for i in range(self.shards)])

    def turn(self, v, k):
        return lax.ppermute(v, "group", [(i, (i + k) % self.groups) for i in range(self.groups)])

    def ring_gather(self, v):
        return [v] + [self.turn(v, k) for k in range(1, self.groups)]

    def others(self, v):
        return jnp.stack([pick(v, (self.z - k) % self.groups) for k in range(1, self.groups)])

    def ring_reduce(self, v, *others):
        at = lambda k: pick(v, (self.z + k) % self.groups)
        total = at(0).astype(f32)
        for k in range(1, self.groups):
            total = total + after(self.turn(at(k), k), *others).astype(f32)
        return total

    def beyond(self, total):
        bit = 8
        while bit < self.shards:
            total = total + self.swap(total, bit)
            bit *= 2
        return total


def local(
    layer_input_rows,
    gain_attn,
    w_query,
    w_key,
    w_value,
    w_out,
    gain_ff,
    gate_weight,
    w_up,
    w_down,
    bucket_head_bias,
    positions,
    rel_bucket,
    out_grad,
    *,
    shards,
    groups,
):
    links = Links(shards, groups)
    z, core, chip = links.z, links.core, links.chip
    tokens, d = layer_input_rows.shape
    seqs = tokens // SEQ
    width = w_query.shape[1]
    rows = w_query.shape[0]
    buckets = bucket_head_bias.shape[0] * groups
    scals = [jnp.stack([z, chip ^ j, core]).astype(jnp.int32) for j in range(4)]
    scal = scals[0]

    small = jnp.concatenate([gain_attn, gain_ff, bucket_head_bias.reshape(-1)])
    spare = width - rows
    small = jnp.pad(small, (0, spare * width - small.shape[0])).reshape(spare, width)
    out_blocks = -(-d // width)
    wo_block = jnp.pad(w_out, ((0, 0), (0, out_blocks * width - d)))
    wo_block = jnp.concatenate([wo_block[:, i * width : (i + 1) * width] for i in range(out_blocks)])
    tall = lambda w: jnp.concatenate([w, small])
    four = jnp.stack([tall(w_query), tall(w_key), tall(w_value), wo_block])
    half = width // 2
    piece = lax.dynamic_slice(four, (chip, core * half, 0), (1, half, width))[0]
    slots = links.ring_gather(piece)
    own_gate, own_up = split_columns(gate_weight, w_up)
    slots[1:] = after(slots[1:], own_gate)
    mine = [jnp.stack(slots)]
    x_t, g_t = layer_input_rows.T, out_grad.T
    g = lax.optimization_barrier(out_grad)
    arrived = [links.swap(mine[0], bit) for bit in (XBIT, YBIT, XBIT | YBIT)]
    mine += [after(a, g) for a in arrived]
    wqkv, wo_t, smalls = attention_weights(scal, mine, [links.swap(a, CORE) for a in mine], rows, d)
    smalls = smalls.reshape(groups, -1)
    gains = [smalls[:, i * rows : (i + 1) * rows].reshape(d, 1).astype(f32) for i in range(2)]
    bias_table = smalls[:, 2 * rows : 2 * rows + bucket_head_bias.size].reshape(buckets, H)

    own_down = w_down.reshape(4, -1, d)
    half_down = own_down.shape[1] // 2
    whole = lambda v: lax.all_gather(v, ("core", "group")).reshape(2, groups, *v.shape)
    gate_up_of = lambda p: jnp.where(core == 0, pick(own_gate, p), pick(own_up, p))
    down_of = lambda p: lax.dynamic_slice(own_down, (p, core * half_down, 0), (1, half_down, d))[0]
    near_gu = whole(after(gate_up_of(chip), *slots[1:]))

    inputs = x_t.astype(f32)
    r_attn = lax.rsqrt(jnp.mean(inputs * inputs, axis=0, keepdims=True) + FLOOR)
    normed_t = (inputs * r_attn * gains[0]).astype(bf16)
    qkv = dot(normed_t, wqkv, "dt,dc->tc").astype(bf16)
    onehot = (rel_bucket[:, None] == jnp.arange(buckets, dtype=jnp.int32)[None, :]).astype(f32)
    offsets = jnp.dot(onehot, bias_table.astype(f32), precision=lax.Precision.HIGHEST).T
    bias = bias_matrix(offsets[:, None, :])
    near_dn = whole(after(down_of(chip), bias))
    places = (positions // BLOCK).reshape(seqs, SEQ)
    attend, context = attend_forward(qkv, after(bias, near_gu), places[:, :, None], places[:, None, :])
    gu = links.others(pick(after(near_gu, context), core))
    gu_x, gu_y = links.swap(gu, XBIT), links.swap(gu, YBIT)
    middle_t, normed_ff_t, normed_ff = middle_norm(context, wo_t, x_t, gains[1])
    dn = links.others(pick(after(near_dn, context), core))
    dn_x, dn_y = links.swap(dn, XBIT), links.swap(dn, YBIT)
    far_gu, far_dn = whole(after(gate_up_of(chip ^ 3), qkv)), whole(after(down_of(chip ^ 3), context))
    gus, dns = [near_gu], [near_dn]
    both = lambda parts: (parts, [links.swap(a, CORE) for a in parts])

    acts, sums_gu, sums_dn = [None] * 4, [None] * 4, [None] * 4

    def chunk(j, *deps):
        hid, dg, du, gm, go, dm, do = ffn_chunk(
            after(scals[j], *deps), normed_ff, normed_ff_t, g, own_gate, own_up, own_down, gus[j], dns[j]
        )
        acts[j] = (hid, dg, du)
        sums_gu[j] = add(gm, links.swap(go, CORE))
        sums_dn[j] = add(dm, links.swap(do, CORE))
        return hid

    n = d // 2
    scatter = lambda v: lax.psum_scatter(v, "group", scatter_dimension=0)
    done = chunk(0)
    gu_x, gu_y, dn_x, dn_y = after((gu_x, gu_y, dn_x, dn_y), done)
    gus += [both([gu_x]), both([gu_y])]
    dns += [both([dn_x]), both([dn_y])]
    gus.append(far_gu)
    dns.append(far_dn)
    rings = [None] * 4
    rings[0] = scatter(sums_dn[0])
    done = chunk(1, done, sums_dn[0], far_gu)
    rings[1] = scatter(sums_dn[1])
    done = chunk(2, done, sums_gu[0], sums_dn[1], rings[0], far_dn)
    rings[2] = scatter(sums_dn[2])
    done = chunk(3, done, sums_gu[1], sums_dn[2], rings[1])
    from_x = [links.swap(sums_gu[1][:n], XBIT), links.swap(sums_gu[1][n:], XBIT)]
    from_y = [links.swap(sums_gu[2][:n], YBIT), links.swap(sums_gu[2][n:], YBIT)]
    rings[3] = scatter(sums_dn[3])
    far_sum = scatter(sums_gu[3].reshape(groups, rows, -1))
    d_middle_t, d_attn_t, grad_gain_ff = ffn_dx(
        after(scal, done, rings[2], sums_gu[2], sums_gu[3], sums_dn[2], sums_dn[3]),
        gains[1],
        middle_t,
        g_t,
        own_gate,
        own_up,
        [(acts[j][1], acts[j][2], gus[j]) for j in range(4)],
    )
    d_attn_t = after(d_attn_t, from_x[0], from_y[0], rings[3])
    d_context = dot(d_attn_t, wo_t, "dt,dc->tc").astype(bf16)
    d_q, d_k, d_v, per_offset = attend_backward(qkv, attend, d_context)
    far = after([links.swap(rings[j], j << 1) for j in (1, 2, 3)], d_q)
    from_x[1], from_y[1] = after((from_x[1], from_y[1]), d_q)
    red_dn = rings[0].astype(f32)
    for part in far:
        red_dn = red_dn + part.astype(f32)
    red_dn = links.beyond(red_dn).astype(bf16)
    red_gu = jnp.concatenate([add(sums_gu[0][:n], from_x[0], from_y[0]), add(sums_gu[0][n:], from_x[1], from_y[1])])
    d_q = after(d_q, red_dn, red_gu)
    red_gu = scatter(red_gu.reshape(groups, rows, -1))
    grad_table = jnp.dot(onehot.T, per_offset[:, 0, :].T, precision=lax.Precision.HIGHEST)
    input_grad_t, grad_gain_attn = input_gradient(d_q, d_k, d_v, wqkv, x_t, d_middle_t, gains[0])

    small = [grad_gain_attn.reshape(groups, -1), grad_gain_ff.reshape(groups, -1), grad_table.reshape(groups, -1)]
    small = jnp.concatenate(small, axis=1).astype(bf16)
    small = jnp.pad(small, ((0, 0), (0, spare * width - small.shape[1]))).reshape(groups, spare, width)
    mine, other = attention_matrices(after(scal, input_grad_t), normed_t, d_q, d_k, d_v, context, d_attn_t, small)
    sums = add(mine, links.swap(other, CORE))

    def spread(v, *others):
        received = [after(links.swap(v, j << 1), *others) for j in (1, 2, 3)]
        mine = jnp.stack([v, *received])
        return mine, links.swap(mine, CORE)

    spread_dn = spread(red_dn, mine)
    far_sum = links.swap(far_sum, XBIT | YBIT)
    red_gu = links.beyond(red_gu.astype(f32) + after(far_sum, mine).astype(f32)).astype(bf16)
    gu_x, gu_y = links.swap(red_gu, XBIT), links.swap(red_gu, YBIT)
    output_t = ffn_out(after(scal, sums, spread_dn[1], red_gu), middle_t, own_down, [(acts[j][0], dns[j]) for j in range(4)])
    gu_x, gu_y = after((gu_x, gu_y), output_t)
    red_plane = add(pick(sums, chip), *(after(links.swap(pick(sums, chip ^ j), j << 1), output_t) for j in (1, 2, 3)))
    red = links.beyond(scatter(red_plane).astype(f32)).astype(bf16)
    mid = rows // 2
    gu_d = jnp.concatenate([links.swap(gu_x[:mid], YBIT), links.swap(gu_y[mid:], XBIT)])
    spread_gu = jnp.stack([red_gu, gu_x, gu_y, gu_d])
    grad_gate, grad_up = join_columns(scal, spread_gu, links.swap(spread_gu, CORE))
    grad_down = down_gradient(scal, *after(spread_dn, red_plane)).T
    wide, grad_out, small = attention_gradients(scal, *spread(red), rows, *w_out.shape)
    small = small.reshape(-1)
    return (
        output_t.T,
        input_grad_t.T,
        small[:rows],
        wide[0],
        wide[1],
        wide[2],
        grad_out,
        small[rows : 2 * rows],
        grad_gate,
        grad_up,
        grad_down,
        small[2 * rows : 2 * rows + bucket_head_bias.size].reshape(bucket_head_bias.shape),
    )


def solution(mesh):
    shards, groups = mesh.shape["shard"], mesh.shape["group"]
    mesh = jax.sharding.Mesh(mesh.devices.reshape(shards // 8, 4, 2, groups), (*SHARD, "group"))
    split = P((*SHARD, "group"), None)
    rows = P("group", None)
    in_specs = (split, P("group"), rows, rows, rows, rows, P("group"), rows, rows, rows, rows, P((*SHARD, "group")), P(), split)
    out_specs = (split, split, P("group"), rows, rows, rows, rows, P("group"), rows, rows, rows, rows)
    body = functools.partial(local, shards=shards, groups=groups)
    return jax.shard_map(body, mesh=mesh, in_specs=in_specs, out_specs=out_specs, check_vma=False)
```

profile of v0, /device:TPU:0, one launch (start us, length us, event | category | flops | bytes accessed | tf_op | source)
XLA Modules:
  0.0 581.4 jit_solution(8094752143446310891)
XLA Ops:
  11.2 3.1 collective-permute-start
  18.3 5.2 split_columns.1
  23.4 2.9 select_bitcast_fusion
  30.4 12.8 %collective-permute-done.3.refs_2_ = bf16[4,192,384]{2,1,0:T(8,128)(2,1)} collective-permute-done((bf16[4,192,384]{2,1,0:T(8,128)(2,1)S(1)}, bf16[4,192,384]{2,1,0:T(8,128)(2,1)}, u32[]{:S(2)}, u32[]{:S(2)}) %collective-permute-start.3) | collective-permute-done | bytes 589856 | tf_op jit(solution)/shard_map/ppermute | solution.py:779
  43.2 12.8 %collective-permute-done.4.refs_3_ = bf16[4,192,384]{2,1,0:T(8,128)(2,1)} collective-permute-done((bf16[4,192,384]{2,1,0:T(8,128)(2,1)S(1)}, bf16[4,192,384]{2,1,0:T(8,128)(2,1)}, u32[]{:S(2)}, u32[]{:S(2)}) %collective-permute-start.4) | collective-permute-done | bytes 589856 | tf_op jit(solution)/shard_map/ppermute | solution.py:779
  56.5 3.3 copy.33
  61.6 6.0 %attention_weights.1 = (bf16[1472,1152]{1,0:T(8,128)(2,1)}, bf16[1472,384]{1,0:T(8,128)(2,1)}, bf16[4,16,384]{2,1,0:T(8,128)(2,1)}) custom-call(s32[3]{0:T(128)} %add_add_fusion.refs_0_.scal, bf16[4,192,384]{2,1,0:T(8,128)(2,1)} %copy-done.13, bf16[4,192,384]{2,1,0:T(8,128)(2,1)} %collective-permute-done.3.refs_2_, ...), custom_call_target="tpu_custom_call" | custom-call | flops 6670000128 | bytes 5800000 | tf_op jit(solution)/shard_map/attention_weights/pallas_call | solution.py:660
  69.5 4.3 bias_matrix.1.bias_ref
  77.4 5.6 convolution_convert_fusion.q_ref.k_ref.v_ref
  83.5 2.9 copy.34.refs_3_
  88.9 20.4 %attend_forward.1 = (bf16[2,6,512,512]{3,2,1,0:T(8,128)(2,1)}, bf16[1024,384]{1,0:T(8,128)(2,1)}) custom-call(bf16[1024,1152]{1,0:T(8,128)(2,1)} %convolution_convert_fusion.q_ref.k_ref.v_ref, bf16[1024,1152]{1,0:T(8,128)(2,1)} %convolution_convert_fusion.q_ref.k_ref.v_ref, bf16[1024,1152]{1,0:T(8,128)(2,1)} %convolution_convert_fusion.q_ref.k_ref.v_ref, ...), custom_call_target="tpu_custom_call" | custom-call | flops 23000000512 | bytes 20000000 | tf_op jit(solution)/shard_map/attend_forward/pallas_call | solution.py:79
  113.4 8.0 %all-gather.11.cloned.1.call-done = bf16[896,1472]{1,0:T(8,128)(2,1)} async-done(((bf16[112,1472]{1,0:T(8,128)(2,1)}), bf16[896,1472]{1,0:T(8,128)(2,1)}) %all-gather.11.cloned.1.call-update) | async-done | bytes 2637840 | tf_op jit(solution)/shard_map/all_gather | solution.py:859
  125.8 8.9 %middle_norm.1 = (f32[1472,1024]{1,0:T(8,128)}, bf16[1472,1024]{1,0:T(8,128)(2,1)}, bf16[1024,1472]{1,0:T(8,128)(2,1)}) custom-call(bf16[1024,384]{1,0:T(8,128)(2,1)} %get-tuple-element.120.ctx_ref.refs_5_, bf16[1472,384]{1,0:T(8,128)(2,1)} %get-tuple-element.121.w_ref, bf16[1472,1024]{1,0:T(8,128)(2,1)} %bitcast.104, f32[1472,1]{1,0:T(8,128)} %reshape.166.gain_ref.refs_1_), custom_call_target="tpu_custom_call" | custom-call | flops 8049999872 | bytes 7000000 | tf_op jit(solution)/shard_map/middle_norm/pallas_call | solution.py:404
  134.7 29.9 %ffn_chunk.4 = (bf16[1024,896]{1,0:T(8,128)(2,1)}, bf16[1024,896]{1,0:T(8,128)(2,1)}, bf16[1024,896]{1,0:T(8,128)(2,1)}, bf16[1472,896]{1,0:T(8,128)(2,1)}, bf16...) custom-call(s32[3]{0:T(128)} %add_add_fusion.refs_0_.scal, ...), custom_call_target="tpu_custom_call" | custom-call | flops 34500001792 | bytes 30000000 | tf_op jit(solution)/shard_map/ffn_chunk/pallas_call | solution.py:293
  164.6 14.3 %collective-permute-done.13.refs_9_.refs_6_ = bf16[3,112,1472]{2,1,0:T(8,128)(2,1)} collective-permute-done((bf16[3,112,1472]{2,1,0:T(8,128)(2,1)S(1)}, bf16[3,112,1472]{2,1,0:T(8,128)(2,1)}, u32[]{:S(2)}, u32[]{:S(2)}) %collective-permute-start.13) | collective-permute-done | bytes 989216 | tf_op jit(solution)/shard_map/ppermute | solution.py:779
  181.8 5.9 %collective-permute-done.10 = bf16[4,112,1472]{2,1,0:T(8,128)(2,1)S(1)} collective-permute-done((bf16[4,112,1472]{2,1,0:T(8,128)(2,1)}, bf16[4,112,1472]{2,1,0:T(8,128)(2,1)S(1)}, u32[]{:S(2)}, u32[]{:S(2)}) %collective-permute-start.10) | collective-permute-done | bytes 1318944 | tf_op jit(solution)/shard_map/ppermute | solution.py:779
  187.7 2.8 add_convert_fusion.8
  190.9 29.8 %ffn_chunk.5 = (bf16[1024,896]{1,0:T(8,128)(2,1)}, bf16[1024,896]{1,0:T(8,128)(2,1)}, bf16[1024,896]{1,0:T(8,128)(2,1)}, bf16[1472,896]{1,0:T(8,128)(2,1)}, bf16...) custom-call(s32[3]{0:T(128)} %add_add_fusion.3.refs_0_, ...), custom_call_target="tpu_custom_call" | custom-call | flops 34500001792 | bytes 30000000 | tf_op jit(solution)/shard_map/ffn_chunk/pallas_call | solution.py:293
  221.9 4.0 add_convert_fusion.3
  226.1 2.8 add_convert_fusion.7
  229.0 29.9 %ffn_chunk.6 = (bf16[1024,896]{1,0:T(8,128)(2,1)}, bf16[1024,896]{1,0:T(8,128)(2,1)}, bf16[1024,896]{1,0:T(8,128)(2,1)}, bf16[1472,896]{1,0:T(8,128)(2,1)}, bf16...) custom-call(s32[3]{0:T(128)} %add_add_fusion.2.refs_0_, ...), custom_call_target="tpu_custom_call" | custom-call | flops 34500001792 | bytes 30000000 | tf_op jit(solution)/shard_map/ffn_chunk/pallas_call | solution.py:293
  262.2 2.8 add_convert_fusion.6
  266.8 3.2 add_convert_fusion.2
  270.1 30.0 %ffn_chunk.7 = (bf16[1024,896]{1,0:T(8,128)(2,1)}, bf16[1024,896]{1,0:T(8,128)(2,1)}, bf16[1024,896]{1,0:T(8,128)(2,1)}, bf16[1472,896]{1,0:T(8,128)(2,1)}, bf16...) custom-call(s32[3]{0:T(128)} %add_add_fusion.1.refs_0_, ...), custom_call_target="tpu_custom_call" | custom-call | flops 34500001792 | bytes 30000000 | tf_op jit(solution)/shard_map/ffn_chunk/pallas_call | solution.py:293
  300.4 3.0 collective-permute-done.25
  303.5 2.8 add_convert_fusion.5
  319.0 4.0 add_convert_fusion
  323.5 40.6 %ffn_dx.1 = (f32[1472,1024]{1,0:T(8,128)}, bf16[1472,1024]{1,0:T(8,128)(2,1)}, f32[1472,1]{1,0:T(8,128)}) custom-call(s32[3]{0:T(128)} %add_add_fusion.refs_0_.scal, f32[1472,1]{1,0:T(8,128)} %reshape.166.gain_ref.refs_1_, f32[1472,1024]{1,0:T(8,128)} %get-tuple-element.157.refs_2_.refs_1_, bf16[1472,1024]{1,0:T(8,128)(2,1)} %bitcast.114, ...), custom_call_target="tpu_custom_call" | custom-call | flops 40249999360 | bytes 35000000 | tf_op jit(solution)/shard_map/ffn_dx/pallas_call | solution.py:380
  368.6 4.9 convolution_convert_fusion.1.dctx_ref
  373.5 22.1 %attend_backward.1 = (bf16[1024,384]{1,0:T(8,128)(2,1)}, bf16[1024,384]{1,0:T(8,128)(2,1)}, bf16[1024,384]{1,0:T(8,128)(2,1)}, f32[6,1,1024]{2,1,0:T(1,128)}) custom-call(bf16[1024,1152]{1,0:T(8,128)(2,1)} %convolution_convert_fusion.q_ref.k_ref.v_ref, bf16[1024,1152]{1,0:T(8,128)(2,1)} %convolution_convert_fusion.q_ref.k_ref.v_ref, ...), custom_call_target="tpu_custom_call" | custom-call | flops 25300000768 | bytes 22000000 | tf_op jit(solution)/shard_map/attend_backward/pallas_call | solution.py:142
  395.7 5.0 add_convert_fusion.10
  401.2 3.4 pad_maximum_fusion
  406.0 12.0 %input_gradient.1 = (bf16[1472,1024]{1,0:T(8,128)(2,1)}, f32[1472,1]{1,0:T(8,128)}) custom-call(bf16[1024,384]{1,0:T(8,128)(2,1)} %get-tuple-element.174.dq_ref.refs_2_, bf16[1024,384]{1,0:T(8,128)(2,1)} %get-tuple-element.175.dk_ref.refs_3_, bf16[1024,384]{1,0:T(8,128)(2,1)} %get-tuple-element.176.dv_ref.refs_4_, ...), custom_call_target="tpu_custom_call" | custom-call | flops 9200000000 | bytes 8000000 | tf_op jit(solution)/shard_map/input_gradient/pallas_call | solution.py:435
  420.3 13.2 %attention_matrices.1 = (bf16[4,4,192,384]{3,2,1,0:T(8,128)(2,1)}, bf16[4,4,192,384]{3,2,1,0:T(8,128)(2,1)}) custom-call(s32[3]{0:T(128)} %add_add_fusion.refs_0_.scal, bf16[1472,1024]{1,0:T(8,128)(2,1)} %copy-done.4, bf16[1024,384]{1,0:T(8,128)(2,1)} %get-tuple-element.174.dq_ref.refs_2_, bf16[1024,384]{1,0:T(8,128)(2,1)} %get-tuple-element.175.dk_ref.refs_3_, ...), custom_call_target="tpu_custom_call" | custom-call | flops 10350000128 | bytes 9000000 | tf_op jit(solution)/shard_map/attention_matrices/pallas_call | solution.py:488
  437.1 8.3 %collective-permute-done.36 = bf16[112,1472]{1,0:T(8,128)(2,1)S(1)} collective-permute-done((bf16[112,1472]{1,0:T(8,128)(2,1)S(1)}, bf16[112,1472]{1,0:T(8,128)(2,1)S(1)}, u32[]{:S(2)}, u32[]{:S(2)}) %collective-permute-start.36) | collective-permute-done | bytes 329760 | tf_op jit(solution)/shard_map/ppermute | solution.py:779
  445.5 6.9 %collective-permute-done.35 = bf16[112,1472]{1,0:T(8,128)(2,1)S(1)} collective-permute-done((bf16[112,1472]{1,0:T(8,128)(2,1)S(1)}, bf16[112,1472]{1,0:T(8,128)(2,1)S(1)}, u32[]{:S(2)}, u32[]{:S(2)}) %collective-permute-start.35) | collective-permute-done | bytes 329760 | tf_op jit(solution)/shard_map/ppermute | solution.py:779
  455.4 3.0 add_convert_fusion.4
  463.2 9.4 %collective-permute-done.38 = bf16[368,896]{1,0:T(8,128)(2,1)S(1)} collective-permute-done((bf16[368,896]{1,0:T(8,128)(2,1)}, bf16[368,896]{1,0:T(8,128)(2,1)S(1)}, u32[]{:S(2)}, u32[]{:S(2)}) %collective-permute-start.38) | collective-permute-done | bytes 659488 | tf_op jit(solution)/shard_map/ppermute | solution.py:779
  473.5 8.7 %reduce-scatter.16.cloned.1.call-done = bf16[1,368,896]{2,1,0:T(8,128)(2,1)} async-done(((bf16[4,368,896]{2,1,0:T(8,128)(2,1)}), bf16[1,368,896]{2,1,0:T(8,128)(2,1)}) %reduce-scatter.16.cloned.1.call-update) | async-done | bytes 659472 | tf_op jit(solution)/shard_map/reduce_scatter | solution.py:895
  486.6 23.2 %ffn_out.1 = bf16[1472,1024]{1,0:T(8,128)(2,1)} custom-call(s32[3]{0:T(128)} %add_add_fusion.refs_0_.scal, f32[1472,1024]{1,0:T(8,128)} %get-tuple-element.157.refs_2_.refs_1_, bf16[4,224,1472]{2,1,0:T(8,128)(2,1)} %bitcast.113, bf16[1024,896]{1,0:T(8,128)(2,1)} %get-tuple-element.125.refs_3_, bf16[2,4,112,1472]{3,2,1,0:T(8,128)(2,1)} %bitcast.125, ...), custom_call_target="tpu_custom_call" | custom-call | flops 24149999616 | bytes 21000000 | tf_op jit(solution)/shard_map/ffn_out/pallas_call | solution.py:557
  519.7 3.4 collective-permute-done.49
  526.4 3.2 pad_maximum_fusion.1.refs_0_
  529.6 12.5 %reduce-scatter.20.cloned.1.call-done = bf16[1,192,384]{2,1,0:T(8,128)(2,1)} async-done(((bf16[4,192,384]{2,1,0:T(8,128)(2,1)}), bf16[1,192,384]{2,1,0:T(8,128)(2,1)}) %reduce-scatter.20.cloned.1.call-update) | async-done | bytes 147472 | tf_op jit(solution)/shard_map/reduce_scatter | solution.py:895
  545.5 3.6 collective-permute-done.44
  551.7 5.6 down_gradient.1
  558.2 3.5 attention_gradients.1
  563.8 2.6 slice_bitcast_fusion
  568.0 6.6 %join_columns.1 = (f32[368,3584]{1,0:T(8,128)}, f32[368,3584]{1,0:T(8,128)}) custom-call(s32[3]{0:T(128)} %add_add_fusion.refs_0_.scal, bf16[4,368,896]{2,1,0:T(8,128)(2,1)} %pad_maximum_fusion.1.refs_0_, bf16[4,368,896]{2,1,0:T(8,128)(2,1)} %copy-done.19), custom_call_target="tpu_custom_call" | custom-call | flops 7474999808 | bytes 6500000 | tf_op jit(solution)/shard_map/join_columns/pallas_call | solution.py:618
  (226 shorter events, 103.5 us)
Async XLA Ops:
  7.2 81.7 %all-gather.9.cloned.1.call-start = ((), (), s32[]{:S(2)}) async-start(), calls=%async_computation.14 | async-start | bytes 5935104 | tf_op jit(solution)/shard_map/all_gather | solution.py:859
  11.2 15.1 %collective-permute-start = (bf16[192,384]{1,0:T(8,128)(2,1)S(1)}, bf16[192,384]{1,0:T(8,128)(2,1)S(1)}, u32[]{:S(2)}, u32[]{:S(2)}) collective-permute-start(bf16[192,384]{1,0:T(8,128)(2,1)S(1)} %bitcast.120), channel_id=1, source_target_pairs={{0,1},{1,2},{2,3},{3,0},{4,5},{5,6},{6,7},{7,4},{8,9},{9,10},{10,1... | collective-permute-start | bytes 442376 | tf_op jit(solution)/shard_map/ppermute | solution.py:782
  14.3 12.3 %collective-permute-start.1 = (bf16[192,384]{1,0:T(8,128)(2,1)S(1)}, bf16[192,384]{1,0:T(8,128)(2,1)S(1)}, u32[]{:S(2)}, u32[]{:S(2)}) collective-permute-start(bf16[192,384]{1,0:T(8,128)(2,1)S(1)} %bitcast.121), channel_id=1, source_target_pairs={{0,2},{1,3},{2,0},{3,1},{4,6},{5,7},{6,4},{7,5},{8,10},{9,11},{10,... | collective-permute-start | bytes 442376 | tf_op jit(solution)/shard_map/ppermute | solution.py:782
  26.6 94.8 %all-gather.11.cloned.1.call-start = ((), (), s32[]{:S(2)}) async-start(), calls=%async_computation.15 | async-start | bytes 3096576 | tf_op jit(solution)/shard_map/all_gather | solution.py:859
  26.8 16.4 %collective-permute-start.3 = (bf16[4,192,384]{2,1,0:T(8,128)(2,1)S(1)}, bf16[4,192,384]{2,1,0:T(8,128)(2,1)}, u32[]{:S(2)}, u32[]{:S(2)}) collective-permute-start(bf16[4,192,384]{2,1,0:T(8,128)(2,1)S(1)} %pad_maximum_fusion.5.refs_1_), channel_id=1, source_target_pairs={{0,8},{4,12},{8,0},{12,4},{16,24},{20,28},{24,16},{28,20},{1,9},{5... | collective-permute-start | bytes 1769480 | tf_op jit(solution)/shard_map/ppermute | solution.py:779
  28.4 27.6 %collective-permute-start.4 = (bf16[4,192,384]{2,1,0:T(8,128)(2,1)S(1)}, bf16[4,192,384]{2,1,0:T(8,128)(2,1)}, u32[]{:S(2)}, u32[]{:S(2)}) collective-permute-start(bf16[4,192,384]{2,1,0:T(8,128)(2,1)S(1)} %pad_maximum_fusion.5.refs_1_), channel_id=1, source_target_pairs={{0,16},{4,20},{8,24},{12,28},{16,0},{20,4},{24,8},{28,12},{1,17},{... | collective-permute-start | bytes 1769480 | tf_op jit(solution)/shard_map/ppermute | solution.py:779
  29.9 26.1 %collective-permute-start.5 = (bf16[4,192,384]{2,1,0:T(8,128)(2,1)S(1)}, bf16[4,192,384]{2,1,0:T(8,128)(2,1)}, u32[]{:S(2)}, u32[]{:S(2)}) collective-permute-start(bf16[4,192,384]{2,1,0:T(8,128)(2,1)S(1)} %pad_maximum_fusion.5.refs_1_), channel_id=1, source_target_pairs={{0,24},{4,28},{8,16},{12,20},{16,8},{20,12},{24,0},{28,4},{1,25},{... | collective-permute-start | bytes 1769480 | tf_op jit(solution)/shard_map/ppermute | solution.py:779
  30.4 31.2 %collective-permute-start.6 = (bf16[4,192,384]{2,1,0:T(8,128)(2,1)S(1)}, bf16[4,192,384]{2,1,0:T(8,128)(2,1)}, u32[]{:S(2)}, u32[]{:S(2)}) collective-permute-start(bf16[4,192,384]{2,1,0:T(8,128)(2,1)S(1)} %pad_maximum_fusion.5.refs_1_), channel_id=1, source_target_pairs={{0,4},{4,0},{8,12},{12,8},{16,20},{20,16},{24,28},{28,24},{1,5},{5... | collective-permute-start | bytes 1769480 | tf_op jit(solution)/shard_map/ppermute | solution.py:779
  73.9 116.6 %all-gather.13.cloned.1.call-start = ((), (), s32[]{:S(2)}) async-start(), calls=%async_computation.16 | async-start | bytes 5935104 | tf_op jit(solution)/shard_map/all_gather | solution.py:859
  83.0 145.9 %all-gather.15.cloned.1.call-start = ((), (), s32[]{:S(2)}) async-start(), calls=%async_computation.17 | async-start | bytes 3096576 | tf_op jit(solution)/shard_map/all_gather | solution.py:859
  111.2 68.7 %collective-permute-start.11 = (bf16[3,368,896]{2,1,0:T(8,128)(2,1)S(1)}, bf16[3,368,896]{2,1,0:T(8,128)(2,1)}, u32[]{:S(2)}, u32[]{:S(2)}) collective-permute-start(bf16[3,368,896]{2,1,0:T(8,128)(2,1)S(1)} %pad_maximum_fusion.2), channel_id=1, source_target_pairs={{0,8},{4,12},{8,0},{12,4},{16,24},{20,28},{24,16},{28,20},{1,9},{5... | collective-permute-start | bytes 5935112 | tf_op jit(solution)/shard_map/ppermute | solution.py:779
  112.5 67.5 %collective-permute-start.12 = (bf16[3,368,896]{2,1,0:T(8,128)(2,1)S(1)}, bf16[3,368,896]{2,1,0:T(8,128)(2,1)}, u32[]{:S(2)}, u32[]{:S(2)}) collective-permute-start(bf16[3,368,896]{2,1,0:T(8,128)(2,1)S(1)} %pad_maximum_fusion.2), channel_id=1, source_target_pairs={{0,16},{4,20},{8,24},{12,28},{16,0},{20,4},{24,8},{28,12},{1,17},{... | collective-permute-start | bytes 5935112 | tf_op jit(solution)/shard_map/ppermute | solution.py:779
  122.8 56.1 %collective-permute-start.13 = (bf16[3,112,1472]{2,1,0:T(8,128)(2,1)S(1)}, bf16[3,112,1472]{2,1,0:T(8,128)(2,1)}, u32[]{:S(2)}, u32[]{:S(2)}) collective-permute-start(bf16[3,112,1472]{2,1,0:T(8,128)(2,1)S(1)} %pad_maximum_fusion.4), channel_id=1, source_target_pairs={{0,8},{4,12},{8,0},{12,4},{16,24},{20,28},{24,16},{28,20},{1,9},{5... | collective-permute-start | bytes 2967560 | tf_op jit(solution)/shard_map/ppermute | solution.py:779
  124.4 55.6 %collective-permute-start.14 = (bf16[3,112,1472]{2,1,0:T(8,128)(2,1)S(1)}, bf16[3,112,1472]{2,1,0:T(8,128)(2,1)}, u32[]{:S(2)}, u32[]{:S(2)}) collective-permute-start(bf16[3,112,1472]{2,1,0:T(8,128)(2,1)S(1)} %pad_maximum_fusion.4), channel_id=1, source_target_pairs={{0,16},{4,20},{8,24},{12,28},{16,0},{20,4},{24,8},{28,12},{1,17},{... | collective-permute-start | bytes 2967560 | tf_op jit(solution)/shard_map/ppermute | solution.py:779
  179.9 11.0 %collective-permute-start.15 = (bf16[3,368,896]{2,1,0:T(8,128)(2,1)}, bf16[3,368,896]{2,1,0:T(8,128)(2,1)}, u32[]{:S(2)}, u32[]{:S(2)}) collective-permute-start(bf16[3,368,896]{2,1,0:T(8,128)(2,1)} %collective-permute-done.11.refs_7_.refs_11_), channel_id=1, source_target_pairs={{0,4},{4,0},{8,12},{12,8},{16,20},{20,16},{24,28},{28,24},{1,5},{5... | collective-permute-start | bytes 5935112 | tf_op jit(solution)/shard_map/ppermute | solution.py:779
  180.4 10.4 %collective-permute-start.16 = (bf16[3,112,1472]{2,1,0:T(8,128)(2,1)}, bf16[3,112,1472]{2,1,0:T(8,128)(2,1)}, u32[]{:S(2)}, u32[]{:S(2)}) collective-permute-start(bf16[3,112,1472]{2,1,0:T(8,128)(2,1)} %collective-permute-done.13.refs_9_.refs_6_), channel_id=1, source_target_pairs={{0,4},{4,0},{8,12},{12,8},{16,20},{20,16},{24,28},{28,24},{1,5},{5... | collective-permute-start | bytes 2967560 | tf_op jit(solution)/shard_map/ppermute | solution.py:779
  181.1 40.8 %collective-permute-start.17 = (bf16[1472,896]{1,0:T(8,128)(2,1)}, bf16[1472,896]{1,0:T(8,128)(2,1)}, u32[]{:S(2)}, u32[]{:S(2)}) collective-permute-start(bf16[1472,896]{1,0:T(8,128)(2,1)} %get-tuple-element.136), channel_id=1, source_target_pairs={{0,4},{4,0},{8,12},{12,8},{16,20},{20,16},{24,28},{28,24},{1,5},{5... | collective-permute-start | bytes 7913480 | tf_op jit(solution)/shard_map/ppermute | solution.py:779
  181.6 88.5 %reduce-scatter.10.cloned.1.call-start = ((), (), s32[]{:S(2)}) async-start(), calls=%async_computation.8 | async-start | bytes 1720320 | tf_op jit(solution)/shard_map/reduce_scatter | solution.py:895
  190.5 38.5 %collective-permute-start.19 = (bf16[3,368,896]{2,1,0:T(8,128)(2,1)}, bf16[3,368,896]{2,1,0:T(8,128)(2,1)}, u32[]{:S(2)}, u32[]{:S(2)}) collective-permute-start(bf16[3,368,896]{2,1,0:T(8,128)(2,1)} %collective-permute-done.12.refs_7_.refs_15_), channel_id=1, source_target_pairs={{0,4},{4,0},{8,12},{12,8},{16,20},{20,16},{24,28},{28,24},{1,5},{5... | collective-permute-start | bytes 5935112 | tf_op jit(solution)/shard_map/ppermute | solution.py:779
  225.9 39.5 %collective-permute-start.21 = (bf16[1472,896]{1,0:T(8,128)(2,1)}, bf16[1472,896]{1,0:T(8,128)(2,1)S(1)}, u32[]{:S(2)}, u32[]{:S(2)}) collective-permute-start(bf16[1472,896]{1,0:T(8,128)(2,1)} %get-tuple-element.145), channel_id=1, source_target_pairs={{0,4},{4,0},{8,12},{12,8},{16,20},{20,16},{24,28},{28,24},{1,5},{5... | collective-permute-start | bytes 7913480 | tf_op jit(solution)/shard_map/ppermute | solution.py:779
  228.9 94.1 %reduce-scatter.12.cloned.1.call-start = ((), (), s32[]{:S(2)}) async-start(), calls=%async_computation.9 | async-start | bytes 1720320 | tf_op jit(solution)/shard_map/reduce_scatter | solution.py:895
  265.1 102.2 %reduce-scatter.14.cloned.1.call-start = ((), (), s32[]{:S(2)}) async-start(), calls=%async_computation.10 | async-start | bytes 1720320 | tf_op jit(solution)/shard_map/reduce_scatter | solution.py:895
  306.3 98.5 %reduce-scatter.8.cloned.1.call-start = ((), (), s32[]{:S(2)}) async-start(), calls=%async_computation.7 | async-start | bytes 1720320 | tf_op jit(solution)/shard_map/reduce_scatter | solution.py:895
  306.7 11.9 %collective-permute-start.24 = (bf16[1472,896]{1,0:T(8,128)(2,1)}, bf16[1472,896]{1,0:T(8,128)(2,1)}, u32[]{:S(2)}, u32[]{:S(2)}) collective-permute-start(bf16[1472,896]{1,0:T(8,128)(2,1)} %get-tuple-element.153), channel_id=1, source_target_pairs={{0,4},{4,0},{8,12},{12,8},{16,20},{20,16},{24,28},{28,24},{1,5},{5... | collective-permute-start | bytes 7913480 | tf_op jit(solution)/shard_map/ppermute | solution.py:779
  307.0 146.7 %reduce-scatter.18.cloned.1.call-start = ((), (), s32[]{:S(2)}) async-start(), calls=%async_computation.12 | async-start | bytes 3297280 | tf_op jit(solution)/shard_map/reduce_scatter | solution.py:895
  310.0 55.6 %collective-permute-start.26 = (bf16[736,896]{1,0:T(8,128)(2,1)}, bf16[736,896]{1,0:T(8,128)(2,1)S(1)}, u32[]{:S(2)}, u32[]{:S(2)}) collective-permute-start(bf16[736,896]{1,0:T(8,128)(2,1)} %get-tuple-element.217), channel_id=1, source_target_pairs={{0,8},{4,12},{8,0},{12,4},{16,24},{20,28},{24,16},{28,20},{1,9},{5... | collective-permute-start | bytes 3956744 | tf_op jit(solution)/shard_map/ppermute | solution.py:779
  310.7 84.9 %collective-permute-start.31 = (bf16[736,896]{1,0:T(8,128)(2,1)}, bf16[736,896]{1,0:T(8,128)(2,1)}, u32[]{:S(2)}, u32[]{:S(2)}) collective-permute-start(bf16[736,896]{1,0:T(8,128)(2,1)} %get-tuple-element.216), channel_id=1, source_target_pairs={{0,8},{4,12},{8,0},{12,4},{16,24},{20,28},{24,16},{28,20},{1,9},{5... | collective-permute-start | bytes 3956744 | tf_op jit(solution)/shard_map/ppermute | solution.py:779
  312.0 92.7 %collective-permute-start.28 = (bf16[112,1472]{1,0:T(8,128)(2,1)}, bf16[112,1472]{1,0:T(8,128)(2,1)S(1)}, u32[]{:S(2)}, u32[]{:S(2)}) collective-permute-start(bf16[112,1472]{1,0:T(8,128)(2,1)} %bitcast.32), channel_id=1, source_target_pairs={{0,8},{4,12},{8,0},{12,4},{16,24},{20,28},{24,16},{28,20},{1,9},{5... | collective-permute-start | bytes 989192 | tf_op jit(solution)/shard_map/ppermute | solution.py:779
  317.0 50.3 %collective-permute-start.27 = (bf16[736,896]{1,0:T(8,128)(2,1)}, bf16[736,896]{1,0:T(8,128)(2,1)S(1)}, u32[]{:S(2)}, u32[]{:S(2)}) collective-permute-start(bf16[736,896]{1,0:T(8,128)(2,1)} %get-tuple-element.215), channel_id=1, source_target_pairs={{0,16},{4,20},{8,24},{12,28},{16,0},{20,4},{24,8},{28,12},{1,17},{... | collective-permute-start | bytes 3956744 | tf_op jit(solution)/shard_map/ppermute | solution.py:779
  318.6 77.1 %collective-permute-start.32 = (bf16[736,896]{1,0:T(8,128)(2,1)}, bf16[736,896]{1,0:T(8,128)(2,1)}, u32[]{:S(2)}, u32[]{:S(2)}) collective-permute-start(bf16[736,896]{1,0:T(8,128)(2,1)} %get-tuple-element.214), channel_id=1, source_target_pairs={{0,16},{4,20},{8,24},{12,28},{16,0},{20,4},{24,8},{28,12},{1,17},{... | collective-permute-start | bytes 3956744 | tf_op jit(solution)/shard_map/ppermute | solution.py:779
  323.0 159.1 %reduce-scatter.16.cloned.1.call-start = ((), (), s32[]{:S(2)}) async-start(), calls=%async_computation.11 | async-start | bytes 3297280 | tf_op jit(solution)/shard_map/reduce_scatter | solution.py:895
  365.6 39.1 %collective-permute-start.29 = (bf16[112,1472]{1,0:T(8,128)(2,1)}, bf16[112,1472]{1,0:T(8,128)(2,1)S(1)}, u32[]{:S(2)}, u32[]{:S(2)}) collective-permute-start(bf16[112,1472]{1,0:T(8,128)(2,1)} %bitcast.149), channel_id=1, source_target_pairs={{0,16},{4,20},{8,24},{12,28},{16,0},{20,4},{24,8},{28,12},{1,17},{... | collective-permute-start | bytes 989192 | tf_op jit(solution)/shard_map/ppermute | solution.py:779
  367.2 37.5 %collective-permute-start.30 = (bf16[112,1472]{1,0:T(8,128)(2,1)}, bf16[112,1472]{1,0:T(8,128)(2,1)}, u32[]{:S(2)}, u32[]{:S(2)}) collective-permute-start(bf16[112,1472]{1,0:T(8,128)(2,1)} %bitcast.150), channel_id=1, source_target_pairs={{0,24},{4,28},{8,16},{12,20},{16,8},{20,12},{24,0},{28,4},{1,25},{... | collective-permute-start | bytes 989192 | tf_op jit(solution)/shard_map/ppermute | solution.py:779
  404.7 137.4 %reduce-scatter.20.cloned.1.call-start = ((), (), s32[]{:S(2)}) async-start(), calls=%async_computation.13 | async-start | bytes 737280 | tf_op jit(solution)/shard_map/reduce_scatter | solution.py:895
  433.5 21.8 %collective-permute-start.33 = (bf16[4,4,192,384]{3,2,1,0:T(8,128)(2,1)}, bf16[4,4,192,384]{3,2,1,0:T(8,128)(2,1)}, u32[]{:S(2)}, u32[]{:S(2)}) collective-permute-start(bf16[4,4,192,384]{3,2,1,0:T(8,128)(2,1)} %get-tuple-element.184), channel_id=1, source_target_pairs={{0,4},{4,0},{8,12},{12,8},{16,20},{20,16},{24,28},{28,24},{1,5},{5... | collective-permute-start | bytes 7077896 | tf_op jit(solution)/shard_map/ppermute | solution.py:779
  433.6 11.9 %collective-permute-start.36 = (bf16[112,1472]{1,0:T(8,128)(2,1)S(1)}, bf16[112,1472]{1,0:T(8,128)(2,1)S(1)}, u32[]{:S(2)}, u32[]{:S(2)}) collective-permute-start(bf16[112,1472]{1,0:T(8,128)(2,1)S(1)} %add_convert_fusion.11), channel_id=1, source_target_pairs={{0,24},{4,28},{8,16},{12,20},{16,8},{20,12},{24,0},{28,4},{1,25},{... | collective-permute-start | bytes 989192 | tf_op jit(solution)/shard_map/ppermute | solution.py:779
  435.2 17.1 %collective-permute-start.35 = (bf16[112,1472]{1,0:T(8,128)(2,1)S(1)}, bf16[112,1472]{1,0:T(8,128)(2,1)S(1)}, u32[]{:S(2)}, u32[]{:S(2)}) collective-permute-start(bf16[112,1472]{1,0:T(8,128)(2,1)S(1)} %add_convert_fusion.11), channel_id=1, source_target_pairs={{0,16},{4,20},{8,24},{12,28},{16,0},{20,4},{24,8},{28,12},{1,17},{... | collective-permute-start | bytes 989192 | tf_op jit(solution)/shard_map/ppermute | solution.py:779
  435.7 16.6 %collective-permute-start.34 = (bf16[112,1472]{1,0:T(8,128)(2,1)S(1)}, bf16[112,1472]{1,0:T(8,128)(2,1)S(1)}, u32[]{:S(2)}, u32[]{:S(2)}) collective-permute-start(bf16[112,1472]{1,0:T(8,128)(2,1)S(1)} %add_convert_fusion.11), channel_id=1, source_target_pairs={{0,8},{4,12},{8,0},{12,4},{16,24},{20,28},{24,16},{28,20},{1,9},{5... | collective-permute-start | bytes 989192 | tf_op jit(solution)/shard_map/ppermute | solution.py:779
  453.6 31.5 %collective-permute-start.37 = (bf16[4,112,1472]{2,1,0:T(8,128)(2,1)}, bf16[4,112,1472]{2,1,0:T(8,128)(2,1)}, u32[]{:S(2)}, u32[]{:S(2)}) collective-permute-start(bf16[4,112,1472]{2,1,0:T(8,128)(2,1)} %pad_maximum_fusion.3.refs_1_), channel_id=1, source_target_pairs={{0,4},{4,0},{8,12},{12,8},{16,20},{20,16},{24,28},{28,24},{1,5},{5... | collective-permute-start | bytes 3956744 | tf_op jit(solution)/shard_map/ppermute | solution.py:779
  453.8 18.9 %collective-permute-start.38 = (bf16[368,896]{1,0:T(8,128)(2,1)}, bf16[368,896]{1,0:T(8,128)(2,1)S(1)}, u32[]{:S(2)}, u32[]{:S(2)}) collective-permute-start(bf16[368,896]{1,0:T(8,128)(2,1)} %bitcast.148), channel_id=1, source_target_pairs={{0,24},{4,28},{8,16},{12,20},{16,8},{20,12},{24,0},{28,4},{1,25},{... | collective-permute-start | bytes 1978376 | tf_op jit(solution)/shard_map/ppermute | solution.py:779
  459.7 57.4 %collective-permute-start.41 = (bf16[4,192,384]{2,1,0:T(8,128)(2,1)}, bf16[4,192,384]{2,1,0:T(8,128)(2,1)}, u32[]{:S(2)}, u32[]{:S(2)}) collective-permute-start(bf16[4,192,384]{2,1,0:T(8,128)(2,1)} %get-tuple-element.219), channel_id=1, source_target_pairs={{0,24},{4,28},{8,16},{12,20},{16,8},{20,12},{24,0},{28,4},{1,25},{... | collective-permute-start | bytes 1769480 | tf_op jit(solution)/shard_map/ppermute | solution.py:779
  461.1 56.0 %collective-permute-start.40 = (bf16[4,192,384]{2,1,0:T(8,128)(2,1)}, bf16[4,192,384]{2,1,0:T(8,128)(2,1)}, u32[]{:S(2)}, u32[]{:S(2)}) collective-permute-start(bf16[4,192,384]{2,1,0:T(8,128)(2,1)} %get-tuple-element.220), channel_id=1, source_target_pairs={{0,16},{4,20},{8,24},{12,28},{16,0},{20,4},{24,8},{28,12},{1,17},{... | collective-permute-start | bytes 1769480 | tf_op jit(solution)/shard_map/ppermute | solution.py:779
  461.8 55.3 %collective-permute-start.39 = (bf16[4,192,384]{2,1,0:T(8,128)(2,1)}, bf16[4,192,384]{2,1,0:T(8,128)(2,1)}, u32[]{:S(2)}, u32[]{:S(2)}) collective-permute-start(bf16[4,192,384]{2,1,0:T(8,128)(2,1)} %get-tuple-element.218), channel_id=1, source_target_pairs={{0,8},{4,12},{8,0},{12,4},{16,24},{20,28},{24,16},{28,20},{1,9},{5... | collective-permute-start | bytes 1769480 | tf_op jit(solution)/shard_map/ppermute | solution.py:779
  483.6 27.3 %collective-permute-start.46 = (bf16[368,896]{1,0:T(8,128)(2,1)S(1)}, bf16[368,896]{1,0:T(8,128)(2,1)}, u32[]{:S(2)}, u32[]{:S(2)}) collective-permute-start(bf16[368,896]{1,0:T(8,128)(2,1)S(1)} %fusion.3), channel_id=1, source_target_pairs={{0,8},{4,12},{8,0},{12,4},{16,24},{20,28},{24,16},{28,20},{1,9},{5... | collective-permute-start | bytes 1978376 | tf_op jit(solution)/shard_map/ppermute | solution.py:779
  485.1 26.3 %collective-permute-start.47 = (bf16[368,896]{1,0:T(8,128)(2,1)S(1)}, bf16[368,896]{1,0:T(8,128)(2,1)}, u32[]{:S(2)}, u32[]{:S(2)}) collective-permute-start(bf16[368,896]{1,0:T(8,128)(2,1)S(1)} %fusion.3), channel_id=1, source_target_pairs={{0,16},{4,20},{8,24},{12,28},{16,0},{20,4},{24,8},{28,12},{1,17},{... | collective-permute-start | bytes 1978376 | tf_op jit(solution)/shard_map/ppermute | solution.py:779
  513.2 9.9 %collective-permute-start.49 = (bf16[184,896]{1,0:T(8,128)(2,1)}, bf16[184,896]{1,0:T(8,128)(2,1)S(1)}, u32[]{:S(2)}, u32[]{:S(2)}) collective-permute-start(bf16[184,896]{1,0:T(8,128)(2,1)} %slice.85), channel_id=1, source_target_pairs={{0,8},{4,12},{8,0},{12,4},{16,24},{20,28},{24,16},{28,20},{1,9},{5... | collective-permute-start | bytes 989192 | tf_op jit(solution)/shard_map/ppermute | solution.py:779
  515.7 9.7 %collective-permute-start.48 = (bf16[184,896]{1,0:T(8,128)(2,1)}, bf16[184,896]{1,0:T(8,128)(2,1)}, u32[]{:S(2)}, u32[]{:S(2)}) collective-permute-start(bf16[184,896]{1,0:T(8,128)(2,1)} %slice.84), channel_id=1, source_target_pairs={{0,16},{4,20},{8,24},{12,28},{16,0},{20,4},{24,8},{28,12},{1,17},{... | collective-permute-start | bytes 989192 | tf_op jit(solution)/shard_map/ppermute | solution.py:779
  529.6 36.9 %collective-permute-start.50 = (bf16[4,368,896]{2,1,0:T(8,128)(2,1)}, bf16[4,368,896]{2,1,0:T(8,128)(2,1)S(1)}, u32[]{:S(2)}, u32[]{:S(2)}) collective-permute-start(bf16[4,368,896]{2,1,0:T(8,128)(2,1)} %pad_maximum_fusion.1.refs_0_), channel_id=1, source_target_pairs={{0,4},{4,0},{8,12},{12,8},{16,20},{20,16},{24,28},{28,24},{1,5},{5... | collective-permute-start | bytes 7913480 | tf_op jit(solution)/shard_map/ppermute | solution.py:779
  (39 other events, 263.4 us)
Sparse Core Ops, SparseCore 0:
  26.8 58.6 all-gather.8
  87.6 33.7 all-gather.10
  123.0 55.2 all-gather.12
  181.7 35.7 all-gather.14
  229.0 32.9 reduce-scatter.9
  265.2 33.0 reduce-scatter.11
  306.4 32.8 reduce-scatter.13
  341.7 31.0 reduce-scatter.7
  375.7 51.4 reduce-scatter.17
  429.9 52.1 reduce-scatter.15
  519.8 22.2 reduce-scatter.19
where the time goes:
time: 589 us; the launch traced here: 581 us
  Pallas kernels  291 us (49%)
  waiting for transfers between devices  119 us (20%)
  other arithmetic  60.4 us (10%)
  starting transfers between devices  46.9 us (8%)
  local copies, waits for them, and re-layouts  37.7 us (6%)
  between operations  14.7 us (2%)
  matrix products  11.2 us (2%)
    pallas_call x4, Pallas kernels, ffn_chunk(): pl.pallas_call(functools.partial(ffn_kernel, groups, nparts), in_specs=[p...  120 us
    ppermute x48, waiting for transfers between devices, swap(): return lax.ppermute(v, SHARD, [(i, i ^ bit) for i in range(self.shards)])  89.5 us
    pallas_call x1, Pallas kernels, ffn_dx(): pl.pallas_call(functools.partial(dx_kernel, groups, tuple(counts)), in_sp...  40.6 us
    ppermute x48, starting transfers between devices, swap(): return lax.ppermute(v, SHARD, [(i, i ^ bit) for i in range(self.shards)])  38.1 us
    convert_element_type x11, other arithmetic, add(): return total.astype(bf16)  35.4 us
    pallas_call x1, Pallas kernels, ffn_out(): pl.pallas_call(functools.partial(out_kernel, groups, tuple(counts)), in_s...  23.2 us
    pallas_call x1, Pallas kernels, attend_backward(): pl.pallas_call(attend_back_kernel, grid=(H // 2, n), in_specs=[pair(0), p...  22.1 us
    reduce_scatter x7, waiting for transfers between devices, local(): scatter = lambda v: lax.psum_scatter(v, 'group', scatter_dimension=0)  21.2 us
  transfers between devices with their start and end apart: 62, of which 20 were waited for; matrix products, arithmetic and copies ran while one was open for 17% of the time, Pallas kernels for 49%

commit v1 on v0

--- a/solution.py
+++ b/solution.py
@@ -89,7 +89,7 @@
         ],
         out_specs=[pl.BlockSpec((1, 2, SEQ, SEQ), lambda h, s: (s, h, 0, 0)), pair(0)],
         out_shape=[jax.ShapeDtypeStruct((n, H, SEQ, SEQ), bf16), jax.ShapeDtypeStruct((n * SEQ, H * DK), bf16)],
-        cost_estimate=kernel_cost(20),
+        cost_estimate=kernel_cost(0.5),
         name="attend_forward",
     )(qkv, qkv, qkv, bias, row, col)
 
@@ -234,25 +234,36 @@
     c_g = copies.start(g_h, g)
     c_d = load_down(copies, scal, wd, own_down, mine_d, other_d, groups)
     c_xt = copies.start(xt_h, xt)
-    c_x.wait(); wait(c_gu); c_g.wait(); wait(c_d)
     tokens = x.shape[0]
     mb = MB
+    c_x.wait()
+    wait(c_gu)
+
+    def gate_rows(m, _):
+        rows = pl.ds(pl.multiple_of(m * mb, mb), mb)
+        dga[rows] = jnp.dot(x[rows], wgu[0], preferred_element_type=f32).astype(bf16)
+        return 0
+
+    lax.fori_loop(0, tokens // mb, gate_rows, 0)
+    c_g.wait()
+    wait(c_d)
+
     def rows_step(m, _):
         rows = pl.ds(pl.multiple_of(m * mb, mb), mb)
-        xm = x[rows]
-        v = jnp.dot(xm, wgu[0], preferred_element_type=f32).astype(bf16).astype(f32)
-        u = jnp.dot(xm, wgu[1], preferred_element_type=f32).astype(bf16).astype(f32)
+        v = dga[rows].astype(f32)
+        u = jnp.dot(x[rows], wgu[1], preferred_element_type=f32).astype(bf16).astype(f32)
         dh = lax.dot_general(g[rows], wd[...], NT, preferred_element_type=f32)
         sq = v * v
-        half = 0.5 + 0.5 * jnp.tanh(v * (ROOT + (ROOT * 0.044715) * sq))
+        half = 0.5 + 0.5 * jnp.tanh(v * (ROOT + (ROOT * CUBIC) * sq))
         act = v * half
-        slope = half + (2.0 * v * half) * ((1.0 - half) * (ROOT + (3 * 0.044715 * ROOT) * sq))
+        slope = half + (2.0 * v * half) * ((1.0 - half) * (ROOT + (3 * CUBIC * ROOT) * sq))
         h = (act * u).astype(bf16)
         hid[rows] = h
         dga[rows] = (dh * u * slope).astype(bf16)
         dup[rows] = (dh * act).astype(bf16)
         hidt[:, rows] = h.T
         return 0
+
     lax.fori_loop(0, tokens // mb, rows_step, 0)
     c_out = [copies.start(hid, hid_h), copies.start(dga, dg_h), copies.start(dup, du_h)]
     block = own_down.shape[1]
@@ -273,9 +284,14 @@
             ggu[i, rows] = jnp.dot(xt[rows], act[...], preferred_element_type=f32).astype(bf16)
             return 0
         lax.fori_loop(0, groups, gate_step, 0)
-    c_out.append(copies.start(ggu.at[core], gm_h))
-    c_out.append(copies.start(ggu.at[1 - core], go_h))
+        sem = sems.at[copies.count]
+        copies.count += 1
+        last = [pltpu.make_async_copy(ggu.at[i], dst, sem) for dst in (gm_h, go_h)]
+        pl.when(core == i)(last[0].start)
+        pl.when(core != i)(last[1].start)
+        c_out.append(last[0])
     wait(c_out)
+
 
 def ffn_chunk(scal, x, xt, g, own_gate, own_up, own_down, gate_up, down):
     tokens, d = x.shape
@@ -408,7 +424,7 @@
         out_specs=[cols, cols, pl.BlockSpec((TB, d), lambda i: (i, 0))],
         out_shape=[jax.ShapeDtypeStruct((d, tokens), f32), jax.ShapeDtypeStruct((d, tokens), bf16), jax.ShapeDtypeStruct((tokens, d), bf16)],
         compiler_params=pltpu.CompilerParams(vmem_limit_bytes=VMEM_LIMIT),
-        cost_estimate=kernel_cost(7),
+        cost_estimate=kernel_cost(0.5),
         name="middle_norm",
     )(context, wo_t, x_t, gain)
 
@@ -758,6 +774,10 @@
 
 def after(v, *others):
     return lax.optimization_barrier((v, others))[0]
+
+
+def tie(*values):
+    return lax.optimization_barrier(values)
 
 
 def pick(stack, i):
@@ -870,10 +890,12 @@
     bias = bias_matrix(offsets[:, None, :])
     near_dn = whole(after(down_of(chip), bias))
     places = (positions // BLOCK).reshape(seqs, SEQ)
-    attend, context = attend_forward(qkv, after(bias, near_gu), places[:, :, None], places[:, None, :])
-    gu = links.others(pick(after(near_gu, context), core))
+    bias, near_gu = tie(bias, near_gu)
+    gu = links.others(pick(near_gu, core))
     gu_x, gu_y = links.swap(gu, XBIT), links.swap(gu, YBIT)
+    attend, context = attend_forward(qkv, bias, places[:, :, None], places[:, None, :])
     middle_t, normed_ff_t, normed_ff = middle_norm(context, wo_t, x_t, gains[1])
+    normed_ff, gu_x, gu_y = tie(normed_ff, gu_x, gu_y)
     dn = links.others(pick(after(near_dn, context), core))
     dn_x, dn_y = links.swap(dn, XBIT), links.swap(dn, YBIT)
     far_gu, far_dn = whole(after(gate_up_of(chip ^ 3), qkv)), whole(after(down_of(chip ^ 3), context))
@@ -891,7 +913,6 @@
         sums_dn[j] = add(dm, links.swap(do, CORE))
         return hid
 
-    n = d // 2
     scatter = lambda v: lax.psum_scatter(v, "group", scatter_dimension=0)
     done = chunk(0)
     gu_x, gu_y, dn_x, dn_y = after((gu_x, gu_y, dn_x, dn_y), done)
@@ -903,15 +924,16 @@
     rings[0] = scatter(sums_dn[0])
     done = chunk(1, done, sums_dn[0], far_gu)
     rings[1] = scatter(sums_dn[1])
-    done = chunk(2, done, sums_gu[0], sums_dn[1], rings[0], far_dn)
-    rings[2] = scatter(sums_dn[2])
-    done = chunk(3, done, sums_gu[1], sums_dn[2], rings[1])
-    from_x = [links.swap(sums_gu[1][:n], XBIT), links.swap(sums_gu[1][n:], XBIT)]
-    from_y = [links.swap(sums_gu[2][:n], YBIT), links.swap(sums_gu[2][n:], YBIT)]
-    rings[3] = scatter(sums_dn[3])
+    done, rings[0] = tie(done, rings[0])
+    done = chunk(2, done, sums_gu[0], sums_dn[1], far_dn)
+    done, rings[1] = tie(done, rings[1])
+    done = chunk(3, done, sums_gu[1], sums_dn[2])
+    from_x, from_y = links.swap(sums_gu[1], XBIT), links.swap(sums_gu[2], YBIT)
+    pair = scatter(jnp.stack([sums_dn[2], sums_dn[3]], axis=1))
+    rings[2:] = pair[0], pair[1]
     far_sum = scatter(sums_gu[3].reshape(groups, rows, -1))
     d_middle_t, d_attn_t, grad_gain_ff = ffn_dx(
-        after(scal, done, rings[2], sums_gu[2], sums_gu[3], sums_dn[2], sums_dn[3]),
+        after(scal, done, sums_gu[2], sums_gu[3], sums_dn[2], sums_dn[3]),
         gains[1],
         middle_t,
         g_t,
@@ -919,46 +941,51 @@
         own_up,
         [(acts[j][1], acts[j][2], gus[j]) for j in range(4)],
     )
-    d_attn_t = after(d_attn_t, from_x[0], from_y[0], rings[3])
     d_context = dot(d_attn_t, wo_t, "dt,dc->tc").astype(bf16)
+    d_context, from_x, from_y, *rings = tie(d_context, from_x, from_y, *rings)
     d_q, d_k, d_v, per_offset = attend_backward(qkv, attend, d_context)
     far = after([links.swap(rings[j], j << 1) for j in (1, 2, 3)], d_q)
-    from_x[1], from_y[1] = after((from_x[1], from_y[1]), d_q)
     red_dn = rings[0].astype(f32)
     for part in far:
         red_dn = red_dn + part.astype(f32)
     red_dn = links.beyond(red_dn).astype(bf16)
-    red_gu = jnp.concatenate([add(sums_gu[0][:n], from_x[0], from_y[0]), add(sums_gu[0][n:], from_x[1], from_y[1])])
-    d_q = after(d_q, red_dn, red_gu)
-    red_gu = scatter(red_gu.reshape(groups, rows, -1))
+    red_gu = scatter(add(sums_gu[0], from_x, from_y).reshape(groups, rows, -1))
+    d_q, red_dn = tie(d_q, red_dn)
     grad_table = jnp.dot(onehot.T, per_offset[:, 0, :].T, precision=lax.Precision.HIGHEST)
     input_grad_t, grad_gain_attn = input_gradient(d_q, d_k, d_v, wqkv, x_t, d_middle_t, gains[0])
+
+    def spread(v, *others):
+        received = [after(links.swap(v, j << 1), *others) for j in (1, 2, 3)]
+        mine = jnp.stack([v, *received])
+        return mine, links.swap(mine, CORE)
+
+    received = [links.swap(red_dn, j << 1) for j in (1, 2, 3)]
+    input_grad_t, far_sum, *received = tie(input_grad_t, far_sum, *received)
+    dn_mine = jnp.stack([red_dn, *received])
+    dn_other = links.swap(dn_mine, CORE)
+    far_sum = links.swap(far_sum, XBIT | YBIT)
 
     small = [grad_gain_attn.reshape(groups, -1), grad_gain_ff.reshape(groups, -1), grad_table.reshape(groups, -1)]
     small = jnp.concatenate(small, axis=1).astype(bf16)
     small = jnp.pad(small, ((0, 0), (0, spare * width - small.shape[1]))).reshape(groups, spare, width)
     mine, other = attention_matrices(after(scal, input_grad_t), normed_t, d_q, d_k, d_v, context, d_attn_t, small)
+    mine, dn_other = tie(mine, dn_other)
     sums = add(mine, links.swap(other, CORE))
-
-    def spread(v, *others):
-        received = [after(links.swap(v, j << 1), *others) for j in (1, 2, 3)]
-        mine = jnp.stack([v, *received])
-        return mine, links.swap(mine, CORE)
-
-    spread_dn = spread(red_dn, mine)
-    far_sum = links.swap(far_sum, XBIT | YBIT)
-    red_gu = links.beyond(red_gu.astype(f32) + after(far_sum, mine).astype(f32)).astype(bf16)
+    output_t = ffn_out(after(scal, sums), middle_t, own_down, [(acts[j][0], dns[j]) for j in range(4)])
+    plane = [links.swap(pick(sums, chip ^ j), j << 1) for j in (1, 2, 3)]
+    output_t, far_sum, red_gu, *plane = tie(output_t, far_sum, red_gu, *plane)
+    red_plane = add(pick(sums, chip), *plane)
+    red_gu = links.beyond(red_gu.astype(f32) + far_sum.astype(f32)).astype(bf16)
+    red_gu, red_plane = tie(red_gu, red_plane)
+    red = scatter(red_plane)
     gu_x, gu_y = links.swap(red_gu, XBIT), links.swap(red_gu, YBIT)
-    output_t = ffn_out(after(scal, sums, spread_dn[1], red_gu), middle_t, own_down, [(acts[j][0], dns[j]) for j in range(4)])
-    gu_x, gu_y = after((gu_x, gu_y), output_t)
-    red_plane = add(pick(sums, chip), *(after(links.swap(pick(sums, chip ^ j), j << 1), output_t) for j in (1, 2, 3)))
-    red = links.beyond(scatter(red_plane).astype(f32)).astype(bf16)
+    grad_down = down_gradient(scal, dn_mine, after(dn_other, red_gu)).T
+    gu_x, gu_y, red, grad_down = tie(gu_x, gu_y, red, grad_down)
     mid = rows // 2
     gu_d = jnp.concatenate([links.swap(gu_x[:mid], YBIT), links.swap(gu_y[mid:], XBIT)])
     spread_gu = jnp.stack([red_gu, gu_x, gu_y, gu_d])
     grad_gate, grad_up = join_columns(scal, spread_gu, links.swap(spread_gu, CORE))
-    grad_down = down_gradient(scal, *after(spread_dn, red_plane)).T
-    wide, grad_out, small = attention_gradients(scal, *spread(red), rows, *w_out.shape)
+    wide, grad_out, small = attention_gradients(scal, *spread(links.beyond(red.astype(f32)).astype(bf16)), rows, *w_out.shape)
     small = small.reshape(-1)
     return (
         output_t.T,

time: 589 us -> 548 us (0.930)
  waiting for transfers between devices: 119 us -> 93.8 us
    reduce_scatter x7 -> x6, waiting for transfers between devices: 21.2 us -> 3.87 us  [local(): scatter = lambda v: lax.psum_scatter(v, 'group', scatter_dimension=0)]
    ppermute x48 -> x46, waiting for transfers between devices: 89.5 us -> 78.8 us  [swap(): return lax.ppermute(v, SHARD, [(i, i ^ bit) for i in range(self.shards)])]
    ppermute x48 -> x46, starting transfers between devices: 38.1 us -> 37.4 us  [swap(): return lax.ppermute(v, SHARD, [(i, i ^ bit) for i in range(self.shards)])]
  transfers between devices with their start and end apart: 62 -> 59, of which waited for: 20 -> 24; matrix products, arithmetic and copies ran while one was open for 17% -> 15% of each run, Pallas kernels for 49% -> 52%
where the time goes in v1:
time: 548 us; the launch traced here: 541 us
  Pallas kernels  286 us (52%)
  waiting for transfers between devices  93.8 us (17%)
  other arithmetic  56.7 us (10%)
  starting transfers between devices  45.2 us (8%)
  local copies, waits for them, and re-layouts  32.2 us (6%)
  between operations  15.2 us (3%)
  matrix products  11.2 us (2%)
    pallas_call x4, Pallas kernels, ffn_chunk(): pl.pallas_call(functools.partial(ffn_kernel, groups, nparts), in_specs=[p...  115 us
    ppermute x46, waiting for transfers between devices, swap(): return lax.ppermute(v, SHARD, [(i, i ^ bit) for i in range(self.shards)])  78.8 us
    pallas_call x1, Pallas kernels, ffn_dx(): pl.pallas_call(functools.partial(dx_kernel, groups, tuple(counts)), in_sp...  40.5 us
    ppermute x46, starting transfers between devices, swap(): return lax.ppermute(v, SHARD, [(i, i ^ bit) for i in range(self.shards)])  37.4 us
    convert_element_type x11, other arithmetic, add(): return total.astype(bf16)  36.5 us
    pallas_call x1, Pallas kernels, ffn_out(): pl.pallas_call(functools.partial(out_kernel, groups, tuple(counts)), in_s...  23.3 us
    pallas_call x1, Pallas kernels, attend_backward(): pl.pallas_call(attend_back_kernel, grid=(H // 2, n), in_specs=[pair(0), p...  22.1 us
    pallas_call x1, Pallas kernels, attend_forward(): pl.pallas_call(attend_kernel, grid=(H // 2, n), in_specs=[pair(0), pair(1...  20.3 us
  transfers between devices with their start and end apart: 59, of which 24 were waited for; matrix products, arithmetic and copies ran while one was open for 15% of the time, Pallas kernels for 52%

profile of v1, /device:TPU:0, one launch (start us, length us, event | category | flops | bytes accessed | tf_op | source)
XLA Modules:
  0.0 540.5 jit_solution(1768321242992632706)
XLA Ops:
  11.2 5.1 collective-permute-start.2
  17.4 5.1 split_columns.1
  22.5 2.9 select_bitcast_fusion
  25.4 3.4 collective-permute-done.1
  29.0 2.5 collective-permute-start.5
  32.6 13.8 %collective-permute-done.5.refs_4_ = bf16[4,192,384]{2,1,0:T(8,128)(2,1)} collective-permute-done((bf16[4,192,384]{2,1,0:T(8,128)(2,1)S(1)}, bf16[4,192,384]{2,1,0:T(8,128)(2,1)}, u32[]{:S(2)}, u32[]{:S(2)}) %collective-permute-start.5) | collective-permute-done | bytes 589856 | tf_op jit(solution)/shard_map/ppermute | solution.py:799
  46.4 11.0 %collective-permute-done.4.refs_3_ = bf16[4,192,384]{2,1,0:T(8,128)(2,1)} collective-permute-done((bf16[4,192,384]{2,1,0:T(8,128)(2,1)S(1)}, bf16[4,192,384]{2,1,0:T(8,128)(2,1)}, u32[]{:S(2)}, u32[]{:S(2)}) %collective-permute-start.4) | collective-permute-done | bytes 589856 | tf_op jit(solution)/shard_map/ppermute | solution.py:799
  57.9 3.3 copy.33
  63.0 6.0 %attention_weights.1 = (bf16[1472,1152]{1,0:T(8,128)(2,1)}, bf16[1472,384]{1,0:T(8,128)(2,1)}, bf16[4,16,384]{2,1,0:T(8,128)(2,1)}) custom-call(s32[3]{0:T(128)} %add_add_fusion.refs_0_.scal, bf16[4,192,384]{2,1,0:T(8,128)(2,1)} %copy-done.15, bf16[4,192,384]{2,1,0:T(8,128)(2,1)} %collective-permute-done.3.refs_2_, ...), custom_call_target="tpu_custom_call" | custom-call | flops 6670000128 | bytes 5800000 | tf_op jit(solution)/shard_map/attention_weights/pallas_call | solution.py:676
  70.9 4.3 bias_matrix.1.bias_ref
  78.8 5.6 %convolution_convert_fusion.q_ref.k_ref.v_ref = bf16[1024,1152]{1,0:T(8,128)(2,1)} fusion(bf16[1472,1024]{1,0:T(8,128)(2,1)S(1)} %fusion.2.refs_1_, bf16[1472,1152]{1,0:T(8,128)(2,1)S(1)} %copy-done.32), kind=kOutput, calls=%fused_computation.11 | convolution fusion | flops 3474063360 | bytes 8765440 | tf_op jit(solution)/shard_map/dt,dc->tc/dot_general | solution.py:765
  91.9 2.9 copy.34.refs_3_
  97.2 20.3 %attend_forward.1 = (bf16[2,6,512,512]{3,2,1,0:T(8,128)(2,1)}, bf16[1024,384]{1,0:T(8,128)(2,1)}) custom-call(bf16[1024,1152]{1,0:T(8,128)(2,1)} %convolution_convert_fusion.q_ref.k_ref.v_ref, bf16[1024,1152]{1,0:T(8,128)(2,1)} %convolution_convert_fusion.q_ref.k_ref.v_ref, bf16[1024,1152]{1,0:T(8,128)(2,1)} %convolution_convert_fusion.q_ref.k_ref.v_ref, ...), custom_call_target="tpu_custom_call" | custom-call | flops 575000000 | bytes 500000 | tf_op jit(solution)/shard_map/attend_forward/pallas_call | solution.py:79
  117.5 4.2 all-gather.11.cloned.1.call-done
  126.1 8.9 %middle_norm.1 = (f32[1472,1024]{1,0:T(8,128)}, bf16[1472,1024]{1,0:T(8,128)(2,1)}, bf16[1024,1472]{1,0:T(8,128)(2,1)}) custom-call(bf16[1024,384]{1,0:T(8,128)(2,1)} %get-tuple-element.139.ctx_ref.refs_5_, bf16[1472,384]{1,0:T(8,128)(2,1)} %get-tuple-element.140.w_ref, bf16[1472,1024]{1,0:T(8,128)(2,1)} %bitcast.106, f32[1472,1]{1,0:T(8,128)} %reshape.166.gain_ref.refs_1_), custom_call_target="tpu_custom_call" | custom-call | flops 575000000 | bytes 500000 | tf_op jit(solution)/shard_map/middle_norm/pallas_call | solution.py:420
  136.7 28.6 %ffn_chunk.4 = (bf16[1024,896]{1,0:T(8,128)(2,1)}, bf16[1024,896]{1,0:T(8,128)(2,1)}, bf16[1024,896]{1,0:T(8,128)(2,1)}, bf16[1472,896]{1,0:T(8,128)(2,1)}, bf16...) custom-call(s32[3]{0:T(128)} %add_add_fusion.refs_0_.scal, ...), custom_call_target="tpu_custom_call" | custom-call | flops 34500001792 | bytes 30000000 | tf_op jit(solution)/shard_map/ffn_chunk/pallas_call | solution.py:309
  168.2 7.6 %collective-permute-done.12 = bf16[4,112,1472]{2,1,0:T(8,128)(2,1)S(1)} collective-permute-done((bf16[4,112,1472]{2,1,0:T(8,128)(2,1)}, bf16[4,112,1472]{2,1,0:T(8,128)(2,1)S(1)}, u32[]{:S(2)}, u32[]{:S(2)}) %collective-permute-start.12) | collective-permute-done | bytes 1318944 | tf_op jit(solution)/shard_map/ppermute | solution.py:799
  175.8 2.8 add_convert_fusion.9
  181.5 28.7 %ffn_chunk.5 = (bf16[1024,896]{1,0:T(8,128)(2,1)}, bf16[1024,896]{1,0:T(8,128)(2,1)}, bf16[1024,896]{1,0:T(8,128)(2,1)}, bf16[1472,896]{1,0:T(8,128)(2,1)}, bf16...) custom-call(s32[3]{0:T(128)} %add_add_fusion.2.refs_0_, ...), custom_call_target="tpu_custom_call" | custom-call | flops 34500001792 | bytes 30000000 | tf_op jit(solution)/shard_map/ffn_chunk/pallas_call | solution.py:309
  211.7 4.0 add_convert_fusion.3
  215.7 2.8 add_convert_fusion.8
  219.1 28.7 %ffn_chunk.6 = (bf16[1024,896]{1,0:T(8,128)(2,1)}, bf16[1024,896]{1,0:T(8,128)(2,1)}, bf16[1024,896]{1,0:T(8,128)(2,1)}, bf16[1472,896]{1,0:T(8,128)(2,1)}, bf16...) custom-call(s32[3]{0:T(128)} %add_add_fusion.3.refs_0_, ...), custom_call_target="tpu_custom_call" | custom-call | flops 34500001792 | bytes 30000000 | tf_op jit(solution)/shard_map/ffn_chunk/pallas_call | solution.py:309
  249.0 4.0 add_convert_fusion.4
  254.7 28.5 %ffn_chunk.7 = (bf16[1024,896]{1,0:T(8,128)(2,1)}, bf16[1024,896]{1,0:T(8,128)(2,1)}, bf16[1024,896]{1,0:T(8,128)(2,1)}, bf16[1472,896]{1,0:T(8,128)(2,1)}, bf16...) custom-call(s32[3]{0:T(128)} %add_add_fusion.1.refs_0_, ...), custom_call_target="tpu_custom_call" | custom-call | flops 34500001792 | bytes 30000000 | tf_op jit(solution)/shard_map/ffn_chunk/pallas_call | solution.py:309
  283.6 3.1 collective-permute-done.25
  295.5 4.8 add_convert_fusion.2
  301.3 4.0 add_convert_fusion.1
  305.8 40.5 %ffn_dx.1 = (f32[1472,1024]{1,0:T(8,128)}, bf16[1472,1024]{1,0:T(8,128)(2,1)}, f32[1472,1]{1,0:T(8,128)}) custom-call(s32[3]{0:T(128)} %add_add_fusion.refs_0_.scal, f32[1472,1]{1,0:T(8,128)} %reshape.166.gain_ref.refs_1_, f32[1472,1024]{1,0:T(8,128)} %get-tuple-element.177.refs_2_.refs_1_, bf16[1472,1024]{1,0:T(8,128)(2,1)} %bitcast.118, ...), custom_call_target="tpu_custom_call" | custom-call | flops 40249999360 | bytes 35000000 | tf_op jit(solution)/shard_map/ffn_dx/pallas_call | solution.py:396
  347.8 4.9 convolution_convert_fusion.1.dctx_ref
  353.9 6.2 %collective-permute-done.27 = bf16[1472,896]{1,0:T(8,128)(2,1)} collective-permute-done((bf16[1472,896]{1,0:T(8,128)(2,1)}, bf16[1472,896]{1,0:T(8,128)(2,1)}, u32[]{:S(2)}, u32[]{:S(2)}) %collective-permute-start.27) | collective-permute-done | bytes 2637856 | tf_op jit(solution)/shard_map/ppermute | solution.py:799
  363.6 22.1 %attend_backward.1 = (bf16[1024,384]{1,0:T(8,128)(2,1)}, bf16[1024,384]{1,0:T(8,128)(2,1)}, bf16[1024,384]{1,0:T(8,128)(2,1)}, f32[6,1,1024]{2,1,0:T(1,128)}) custom-call(bf16[1024,1152]{1,0:T(8,128)(2,1)} %convolution_convert_fusion.q_ref.k_ref.v_ref, bf16[1024,1152]{1,0:T(8,128)(2,1)} %convolution_convert_fusion.q_ref.k_ref.v_ref, ...), custom_call_target="tpu_custom_call" | custom-call | flops 25300000768 | bytes 22000000 | tf_op jit(solution)/shard_map/attend_backward/pallas_call | solution.py:142
  385.7 5.0 add_convert_fusion
  396.7 12.2 %input_gradient.1 = (bf16[1472,1024]{1,0:T(8,128)(2,1)}, f32[1472,1]{1,0:T(8,128)}) custom-call(bf16[1024,384]{1,0:T(8,128)(2,1)} %get-tuple-element.200.dq_ref.refs_2_, bf16[1024,384]{1,0:T(8,128)(2,1)} %get-tuple-element.201.dk_ref.refs_3_, bf16[1024,384]{1,0:T(8,128)(2,1)} %get-tuple-element.202.dv_ref.refs_4_, ...), custom_call_target="tpu_custom_call" | custom-call | flops 9200000000 | bytes 8000000 | tf_op jit(solution)/shard_map/input_gradient/pallas_call | solution.py:451
  411.1 13.3 %attention_matrices.1 = (bf16[4,4,192,384]{3,2,1,0:T(8,128)(2,1)}, bf16[4,4,192,384]{3,2,1,0:T(8,128)(2,1)}) custom-call(s32[3]{0:T(128)} %add_add_fusion.refs_0_.scal, bf16[1472,1024]{1,0:T(8,128)(2,1)} %copy-done.4, bf16[1024,384]{1,0:T(8,128)(2,1)} %get-tuple-element.200.dq_ref.refs_2_, bf16[1024,384]{1,0:T(8,128)(2,1)} %get-tuple-element.201.dk_ref.refs_3_, ...), custom_call_target="tpu_custom_call" | custom-call | flops 10350000128 | bytes 9000000 | tf_op jit(solution)/shard_map/attention_matrices/pallas_call | solution.py:504
  426.9 4.1 collective-permute-done.34.refs_2_
  432.1 3.1 add_convert_fusion.5
  439.9 23.3 %ffn_out.1 = bf16[1472,1024]{1,0:T(8,128)(2,1)} custom-call(s32[3]{0:T(128)} %add_add_fusion.refs_0_.scal, f32[1472,1024]{1,0:T(8,128)} %get-tuple-element.177.refs_2_.refs_1_, bf16[4,224,1472]{2,1,0:T(8,128)(2,1)} %bitcast.117, bf16[1024,896]{1,0:T(8,128)(2,1)} %get-tuple-element.146.refs_3_, bf16[2,4,112,1472]{3,2,1,0:T(8,128)(2,1)} %bitcast.132, ...), custom_call_target="tpu_custom_call" | custom-call | flops 24149999616 | bytes 21000000 | tf_op jit(solution)/shard_map/ffn_out/pallas_call | solution.py:573
  463.2 5.3 collective-permute-done.38
  470.8 2.6 fusion.5
  475.7 5.6 %down_gradient.1 = f32[1472,896]{1,0:T(8,128)} custom-call(s32[3]{0:T(128)} %add_add_fusion.refs_0_.scal, bf16[4,112,1472]{2,1,0:T(8,128)(2,1)} %copy-done.12, bf16[4,112,1472]{2,1,0:T(8,128)(2,1)} %copy-done.24), custom_call_target="tpu_custom_call" | custom-call | flops 6440000000 | bytes 5600000 | tf_op jit(solution)/shard_map/down_gradient/pallas_call | solution.py:752
  481.3 8.9 %collective-permute-done.41 = bf16[368,896]{1,0:T(8,128)(2,1)S(1)} collective-permute-done((bf16[368,896]{1,0:T(8,128)(2,1)S(1)}, bf16[368,896]{1,0:T(8,128)(2,1)S(1)}, u32[]{:S(2)}, u32[]{:S(2)}) %collective-permute-start.41) | collective-permute-done | bytes 659488 | tf_op jit(solution)/shard_map/ppermute | solution.py:799
  490.7 3.8 reduce-scatter.17.cloned.1.call-done
  497.5 4.5 collective-permute-done.47
  508.7 4.1 collective-permute-done.44
  512.8 2.6 collective-permute-done.43
  518.5 3.5 attention_gradients.1
  524.2 2.6 slice_bitcast_fusion
  526.8 6.6 %join_columns.1 = (f32[368,3584]{1,0:T(8,128)}, f32[368,3584]{1,0:T(8,128)}) custom-call(s32[3]{0:T(128)} %add_add_fusion.refs_0_.scal, bf16[4,368,896]{2,1,0:T(8,128)(2,1)} %copy-done.6, bf16[4,368,896]{2,1,0:T(8,128)(2,1)} %collective-permute-done.48.refs_1_), custom_call_target="tpu_custom_call" | custom-call | flops 7474999808 | bytes 6500000 | tf_op jit(solution)/shard_map/join_columns/pallas_call | solution.py:634
  (234 shorter events, 93.4 us)
Async XLA Ops:
  7.2 78.6 %all-gather.9.cloned.1.call-start = ((), (), s32[]{:S(2)}) async-start(), calls=%async_computation.12 | async-start | bytes 5935104 | tf_op jit(solution)/shard_map/all_gather | solution.py:879
  11.2 14.2 %collective-permute-start.2 = (bf16[192,384]{1,0:T(8,128)(2,1)S(1)}, bf16[192,384]{1,0:T(8,128)(2,1)S(1)}, u32[]{:S(2)}, u32[]{:S(2)}) collective-permute-start(bf16[192,384]{1,0:T(8,128)(2,1)S(1)} %bitcast.127), channel_id=1, source_target_pairs={{0,3},{1,0},{2,1},{3,2},{4,7},{5,4},{6,5},{7,6},{8,11},{9,8},{10,9... | collective-permute-start | bytes 442376 | tf_op jit(solution)/shard_map/ppermute | solution.py:802
  16.3 12.5 %collective-permute-start.1 = (bf16[192,384]{1,0:T(8,128)(2,1)S(1)}, bf16[192,384]{1,0:T(8,128)(2,1)S(1)}, u32[]{:S(2)}, u32[]{:S(2)}) collective-permute-start(bf16[192,384]{1,0:T(8,128)(2,1)S(1)} %bitcast.128), channel_id=1, source_target_pairs={{0,2},{1,3},{2,0},{3,1},{4,6},{5,7},{6,4},{7,5},{8,10},{9,11},{10,... | collective-permute-start | bytes 442376 | tf_op jit(solution)/shard_map/ppermute | solution.py:802
  16.3 12.5 %collective-permute-start = (bf16[192,384]{1,0:T(8,128)(2,1)S(1)}, bf16[192,384]{1,0:T(8,128)(2,1)S(1)}, u32[]{:S(2)}, u32[]{:S(2)}) collective-permute-start(bf16[192,384]{1,0:T(8,128)(2,1)S(1)} %bitcast.129), channel_id=1, source_target_pairs={{0,1},{1,2},{2,3},{3,0},{4,5},{5,6},{6,7},{7,4},{8,9},{9,10},{10,1... | collective-permute-start | bytes 442376 | tf_op jit(solution)/shard_map/ppermute | solution.py:802
  28.9 92.9 %all-gather.11.cloned.1.call-start = ((), (), s32[]{:S(2)}) async-start(), calls=%async_computation.13 | async-start | bytes 3096576 | tf_op jit(solution)/shard_map/all_gather | solution.py:879
  29.0 17.4 %collective-permute-start.5 = (bf16[4,192,384]{2,1,0:T(8,128)(2,1)S(1)}, bf16[4,192,384]{2,1,0:T(8,128)(2,1)}, u32[]{:S(2)}, u32[]{:S(2)}) collective-permute-start(bf16[4,192,384]{2,1,0:T(8,128)(2,1)S(1)} %pad_maximum_fusion.5.refs_1_), channel_id=1, source_target_pairs={{0,24},{4,28},{8,16},{12,20},{16,8},{20,12},{24,0},{28,4},{1,25},{... | collective-permute-start | bytes 1769480 | tf_op jit(solution)/shard_map/ppermute | solution.py:799
  31.5 25.8 %collective-permute-start.4 = (bf16[4,192,384]{2,1,0:T(8,128)(2,1)S(1)}, bf16[4,192,384]{2,1,0:T(8,128)(2,1)}, u32[]{:S(2)}, u32[]{:S(2)}) collective-permute-start(bf16[4,192,384]{2,1,0:T(8,128)(2,1)S(1)} %pad_maximum_fusion.5.refs_1_), channel_id=1, source_target_pairs={{0,16},{4,20},{8,24},{12,28},{16,0},{20,4},{24,8},{28,12},{1,17},{... | collective-permute-start | bytes 1769480 | tf_op jit(solution)/shard_map/ppermute | solution.py:799
  32.0 25.4 %collective-permute-start.3 = (bf16[4,192,384]{2,1,0:T(8,128)(2,1)S(1)}, bf16[4,192,384]{2,1,0:T(8,128)(2,1)}, u32[]{:S(2)}, u32[]{:S(2)}) collective-permute-start(bf16[4,192,384]{2,1,0:T(8,128)(2,1)S(1)} %pad_maximum_fusion.5.refs_1_), channel_id=1, source_target_pairs={{0,8},{4,12},{8,0},{12,4},{16,24},{20,28},{24,16},{28,20},{1,9},{5... | collective-permute-start | bytes 1769480 | tf_op jit(solution)/shard_map/ppermute | solution.py:799
  32.6 30.4 %collective-permute-start.6 = (bf16[4,192,384]{2,1,0:T(8,128)(2,1)S(1)}, bf16[4,192,384]{2,1,0:T(8,128)(2,1)}, u32[]{:S(2)}, u32[]{:S(2)}) collective-permute-start(bf16[4,192,384]{2,1,0:T(8,128)(2,1)S(1)} %pad_maximum_fusion.5.refs_1_), channel_id=1, source_target_pairs={{0,4},{4,0},{8,12},{12,8},{16,20},{20,16},{24,28},{28,24},{1,5},{5... | collective-permute-start | bytes 1769480 | tf_op jit(solution)/shard_map/ppermute | solution.py:799
  46.4 16.6 %collective-permute-start.9 = (bf16[4,192,384]{2,1,0:T(8,128)(2,1)}, bf16[4,192,384]{2,1,0:T(8,128)(2,1)}, u32[]{:S(2)}, u32[]{:S(2)}) collective-permute-start(bf16[4,192,384]{2,1,0:T(8,128)(2,1)} %collective-permute-done.5.refs_4_), channel_id=1, source_target_pairs={{0,4},{4,0},{8,12},{12,8},{16,20},{20,16},{24,28},{28,24},{1,5},{5... | collective-permute-start | bytes 1769480 | tf_op jit(solution)/shard_map/ppermute | solution.py:799
  75.3 105.2 %all-gather.13.cloned.1.call-start = ((), (), s32[]{:S(2)}) async-start(), calls=%async_computation.14 | async-start | bytes 5935104 | tf_op jit(solution)/shard_map/all_gather | solution.py:879
  84.4 134.7 %all-gather.15.cloned.1.call-start = ((), (), s32[]{:S(2)}) async-start(), calls=%async_computation.15 | async-start | bytes 3096576 | tf_op jit(solution)/shard_map/all_gather | solution.py:879
  89.0 46.2 %collective-permute-start.11 = (bf16[3,368,896]{2,1,0:T(8,128)(2,1)}, bf16[3,368,896]{2,1,0:T(8,128)(2,1)}, u32[]{:S(2)}, u32[]{:S(2)}) collective-permute-start(bf16[3,368,896]{2,1,0:T(8,128)(2,1)} %pad_maximum_fusion.2), channel_id=1, source_target_pairs={{0,16},{4,20},{8,24},{12,28},{16,0},{20,4},{24,8},{28,12},{1,17},{... | collective-permute-start | bytes 5935112 | tf_op jit(solution)/shard_map/ppermute | solution.py:799
  90.4 46.3 %collective-permute-start.10 = (bf16[3,368,896]{2,1,0:T(8,128)(2,1)}, bf16[3,368,896]{2,1,0:T(8,128)(2,1)}, u32[]{:S(2)}, u32[]{:S(2)}) collective-permute-start(bf16[3,368,896]{2,1,0:T(8,128)(2,1)} %pad_maximum_fusion.2), channel_id=1, source_target_pairs={{0,8},{4,12},{8,0},{12,4},{16,24},{20,28},{24,16},{28,20},{1,9},{5... | collective-permute-start | bytes 5935112 | tf_op jit(solution)/shard_map/ppermute | solution.py:799
  123.1 42.2 %collective-permute-start.14 = (bf16[3,112,1472]{2,1,0:T(8,128)(2,1)S(1)}, bf16[3,112,1472]{2,1,0:T(8,128)(2,1)S(1)}, u32[]{:S(2)}, u32[]{:S(2)}) collective-permute-start(bf16[3,112,1472]{2,1,0:T(8,128)(2,1)S(1)} %pad_maximum_fusion.4), channel_id=1, source_target_pairs={{0,16},{4,20},{8,24},{12,28},{16,0},{20,4},{24,8},{28,12},{1,17},{... | collective-permute-start | bytes 2967560 | tf_op jit(solution)/shard_map/ppermute | solution.py:799
  124.7 40.7 %collective-permute-start.13 = (bf16[3,112,1472]{2,1,0:T(8,128)(2,1)S(1)}, bf16[3,112,1472]{2,1,0:T(8,128)(2,1)S(1)}, u32[]{:S(2)}, u32[]{:S(2)}) collective-permute-start(bf16[3,112,1472]{2,1,0:T(8,128)(2,1)S(1)} %pad_maximum_fusion.4), channel_id=1, source_target_pairs={{0,8},{4,12},{8,0},{12,4},{16,24},{20,28},{24,16},{28,20},{1,9},{5... | collective-permute-start | bytes 2967560 | tf_op jit(solution)/shard_map/ppermute | solution.py:799
  165.4 16.1 %collective-permute-start.15 = (bf16[3,368,896]{2,1,0:T(8,128)(2,1)}, bf16[3,368,896]{2,1,0:T(8,128)(2,1)}, u32[]{:S(2)}, u32[]{:S(2)}) collective-permute-start(bf16[3,368,896]{2,1,0:T(8,128)(2,1)} %collective-permute-done.10.refs_7_.refs_11_), channel_id=1, source_target_pairs={{0,4},{4,0},{8,12},{12,8},{16,20},{20,16},{24,28},{28,24},{1,5},{5... | collective-permute-start | bytes 5935112 | tf_op jit(solution)/shard_map/ppermute | solution.py:799
  166.3 9.5 %collective-permute-start.12 = (bf16[4,112,1472]{2,1,0:T(8,128)(2,1)}, bf16[4,112,1472]{2,1,0:T(8,128)(2,1)S(1)}, u32[]{:S(2)}, u32[]{:S(2)}) collective-permute-start(bf16[4,112,1472]{2,1,0:T(8,128)(2,1)} %get-tuple-element.148), channel_id=1, source_target_pairs={{0,4},{4,0},{8,12},{12,8},{16,20},{20,16},{24,28},{28,24},{1,5},{5... | collective-permute-start | bytes 3956744 | tf_op jit(solution)/shard_map/ppermute | solution.py:799
  166.3 14.2 %collective-permute-start.16 = (bf16[3,112,1472]{2,1,0:T(8,128)(2,1)S(1)}, bf16[3,112,1472]{2,1,0:T(8,128)(2,1)S(1)}, u32[]{:S(2)}, u32[]{:S(2)}) collective-permute-start(bf16[3,112,1472]{2,1,0:T(8,128)(2,1)S(1)} %collective-permute-done.13.refs_9_.refs_6_), channel_id=1, source_target_pairs={{0,4},{4,0},{8,12},{12,8},{16,20},{20,16},{24,28},{28,24},{1,5},{5... | collective-permute-start | bytes 2967560 | tf_op jit(solution)/shard_map/ppermute | solution.py:799
  166.8 125.2 %reduce-scatter.7.cloned.1.call-start = ((), (), s32[]{:S(2)}) async-start(), calls=%async_computation.6 | async-start | bytes 1720320 | tf_op jit(solution)/shard_map/reduce_scatter | solution.py:916
  167.7 51.4 %collective-permute-start.20 = (bf16[3,368,896]{2,1,0:T(8,128)(2,1)}, bf16[3,368,896]{2,1,0:T(8,128)(2,1)}, u32[]{:S(2)}, u32[]{:S(2)}) collective-permute-start(bf16[3,368,896]{2,1,0:T(8,128)(2,1)} %collective-permute-done.11.refs_7_.refs_15_), channel_id=1, source_target_pairs={{0,4},{4,0},{8,12},{12,8},{16,20},{20,16},{24,28},{28,24},{1,5},{5... | collective-permute-start | bytes 5935112 | tf_op jit(solution)/shard_map/ppermute | solution.py:799
  167.7 44.1 %collective-permute-start.18 = (bf16[1472,896]{1,0:T(8,128)(2,1)}, bf16[1472,896]{1,0:T(8,128)(2,1)}, u32[]{:S(2)}, u32[]{:S(2)}) collective-permute-start(bf16[1472,896]{1,0:T(8,128)(2,1)} %get-tuple-element.159), channel_id=1, source_target_pairs={{0,4},{4,0},{8,12},{12,8},{16,20},{20,16},{24,28},{28,24},{1,5},{5... | collective-permute-start | bytes 7913480 | tf_op jit(solution)/shard_map/ppermute | solution.py:799
  211.1 8.0 %collective-permute-start.21 = (bf16[3,112,1472]{2,1,0:T(8,128)(2,1)}, bf16[3,112,1472]{2,1,0:T(8,128)(2,1)}, u32[]{:S(2)}, u32[]{:S(2)}) collective-permute-start(bf16[3,112,1472]{2,1,0:T(8,128)(2,1)} %copy-done.25), channel_id=1, source_target_pairs={{0,4},{4,0},{8,12},{12,8},{16,20},{20,16},{24,28},{28,24},{1,5},{5... | collective-permute-start | bytes 2967560 | tf_op jit(solution)/shard_map/ppermute | solution.py:799
  211.3 82.2 %reduce-scatter.9.cloned.1.call-start = ((), (), s32[]{:S(2)}) async-start(), calls=%async_computation.7 | async-start | bytes 1720320 | tf_op jit(solution)/shard_map/reduce_scatter | solution.py:916
  211.4 37.6 %collective-permute-start.17 = (bf16[1472,896]{1,0:T(8,128)(2,1)}, bf16[1472,896]{1,0:T(8,128)(2,1)}, u32[]{:S(2)}, u32[]{:S(2)}) collective-permute-start(bf16[1472,896]{1,0:T(8,128)(2,1)} %get-tuple-element.157), channel_id=1, source_target_pairs={{0,4},{4,0},{8,12},{12,8},{16,20},{20,16},{24,28},{28,24},{1,5},{5... | collective-permute-start | bytes 7913480 | tf_op jit(solution)/shard_map/ppermute | solution.py:799
  248.7 104.0 %reduce-scatter.11.cloned.1.call-start = ((), (), s32[]{:S(2)}) async-start(), calls=%async_computation.8 | async-start | bytes 3440640 | tf_op jit(solution)/shard_map/reduce_scatter | solution.py:916
  290.1 121.0 %reduce-scatter.13.cloned.1.call-start = ((), (), s32[]{:S(2)}) async-start(), calls=%async_computation.9 | async-start | bytes 3297280 | tf_op jit(solution)/shard_map/reduce_scatter | solution.py:916
  290.6 10.7 %collective-permute-start.24 = (bf16[1472,896]{1,0:T(8,128)(2,1)}, bf16[1472,896]{1,0:T(8,128)(2,1)}, u32[]{:S(2)}, u32[]{:S(2)}) collective-permute-start(bf16[1472,896]{1,0:T(8,128)(2,1)} %get-tuple-element.173), channel_id=1, source_target_pairs={{0,4},{4,0},{8,12},{12,8},{16,20},{20,16},{24,28},{28,24},{1,5},{5... | collective-permute-start | bytes 7913480 | tf_op jit(solution)/shard_map/ppermute | solution.py:799
  292.0 61.9 %collective-permute-start.26 = (bf16[1472,896]{1,0:T(8,128)(2,1)}, bf16[1472,896]{1,0:T(8,128)(2,1)S(1)}, u32[]{:S(2)}, u32[]{:S(2)}) collective-permute-start(bf16[1472,896]{1,0:T(8,128)(2,1)} %add_convert_fusion.4), channel_id=1, source_target_pairs={{0,8},{4,12},{8,0},{12,4},{16,24},{20,28},{24,16},{28,20},{1,9},{5... | collective-permute-start | bytes 7913480 | tf_op jit(solution)/shard_map/ppermute | solution.py:799
  300.4 59.7 %collective-permute-start.27 = (bf16[1472,896]{1,0:T(8,128)(2,1)}, bf16[1472,896]{1,0:T(8,128)(2,1)}, u32[]{:S(2)}, u32[]{:S(2)}) collective-permute-start(bf16[1472,896]{1,0:T(8,128)(2,1)} %add_convert_fusion.2), channel_id=1, source_target_pairs={{0,16},{4,20},{8,24},{12,28},{16,0},{20,4},{24,8},{28,12},{1,17},{... | collective-permute-start | bytes 7913480 | tf_op jit(solution)/shard_map/ppermute | solution.py:799
  305.3 163.2 %reduce-scatter.15.cloned.1.call-start = ((), (), s32[]{:S(2)}) async-start(), calls=%async_computation.10 | async-start | bytes 3297280 | tf_op jit(solution)/shard_map/reduce_scatter | solution.py:916
  360.1 31.3 %collective-permute-start.28 = (bf16[112,1472]{1,0:T(8,128)(2,1)}, bf16[112,1472]{1,0:T(8,128)(2,1)}, u32[]{:S(2)}, u32[]{:S(2)}) collective-permute-start(bf16[112,1472]{1,0:T(8,128)(2,1)} %bitcast.156), channel_id=1, source_target_pairs={{0,8},{4,12},{8,0},{12,4},{16,24},{20,28},{24,16},{28,20},{1,9},{5... | collective-permute-start | bytes 989192 | tf_op jit(solution)/shard_map/ppermute | solution.py:799
  361.6 29.8 %collective-permute-start.29 = (bf16[112,1472]{1,0:T(8,128)(2,1)S(1)}, bf16[112,1472]{1,0:T(8,128)(2,1)}, u32[]{:S(2)}, u32[]{:S(2)}) collective-permute-start(bf16[112,1472]{1,0:T(8,128)(2,1)S(1)} %get-tuple-element.195), channel_id=1, source_target_pairs={{0,16},{4,20},{8,24},{12,28},{16,0},{20,4},{24,8},{28,12},{1,17},{... | collective-permute-start | bytes 989192 | tf_op jit(solution)/shard_map/ppermute | solution.py:799
  362.4 29.0 %collective-permute-start.30 = (bf16[112,1472]{1,0:T(8,128)(2,1)S(1)}, bf16[112,1472]{1,0:T(8,128)(2,1)}, u32[]{:S(2)}, u32[]{:S(2)}) collective-permute-start(bf16[112,1472]{1,0:T(8,128)(2,1)S(1)} %get-tuple-element.196), channel_id=1, source_target_pairs={{0,24},{4,28},{8,16},{12,20},{16,8},{20,12},{24,0},{28,4},{1,25},{... | collective-permute-start | bytes 989192 | tf_op jit(solution)/shard_map/ppermute | solution.py:799
  391.4 103.1 %reduce-scatter.17.cloned.1.call-start = ((), (), s32[]{:S(2)}) async-start(), calls=%async_computation.11 | async-start | bytes 737280 | tf_op jit(solution)/shard_map/reduce_scatter | solution.py:916
  393.1 18.0 %collective-permute-start.33 = (bf16[112,1472]{1,0:T(8,128)(2,1)S(1)}, bf16[112,1472]{1,0:T(8,128)(2,1)S(1)}, u32[]{:S(2)}, u32[]{:S(2)}) collective-permute-start(bf16[112,1472]{1,0:T(8,128)(2,1)S(1)} %add_convert_fusion.11), channel_id=1, source_target_pairs={{0,24},{4,28},{8,16},{12,20},{16,8},{20,12},{24,0},{28,4},{1,25},{... | collective-permute-start | bytes 989192 | tf_op jit(solution)/shard_map/ppermute | solution.py:799
  394.9 16.2 %collective-permute-start.32 = (bf16[112,1472]{1,0:T(8,128)(2,1)S(1)}, bf16[112,1472]{1,0:T(8,128)(2,1)S(1)}, u32[]{:S(2)}, u32[]{:S(2)}) collective-permute-start(bf16[112,1472]{1,0:T(8,128)(2,1)S(1)} %add_convert_fusion.11), channel_id=1, source_target_pairs={{0,16},{4,20},{8,24},{12,28},{16,0},{20,4},{24,8},{28,12},{1,17},{... | collective-permute-start | bytes 989192 | tf_op jit(solution)/shard_map/ppermute | solution.py:799
  396.2 14.9 %collective-permute-start.31 = (bf16[112,1472]{1,0:T(8,128)(2,1)S(1)}, bf16[112,1472]{1,0:T(8,128)(2,1)S(1)}, u32[]{:S(2)}, u32[]{:S(2)}) collective-permute-start(bf16[112,1472]{1,0:T(8,128)(2,1)S(1)} %add_convert_fusion.11), channel_id=1, source_target_pairs={{0,8},{4,12},{8,0},{12,4},{16,24},{20,28},{24,16},{28,20},{1,9},{5... | collective-permute-start | bytes 989192 | tf_op jit(solution)/shard_map/ppermute | solution.py:799
  424.4 7.7 %collective-permute-start.35 = (bf16[4,4,192,384]{3,2,1,0:T(8,128)(2,1)}, bf16[4,4,192,384]{3,2,1,0:T(8,128)(2,1)}, u32[]{:S(2)}, u32[]{:S(2)}) collective-permute-start(bf16[4,4,192,384]{3,2,1,0:T(8,128)(2,1)} %get-tuple-element.216), channel_id=1, source_target_pairs={{0,4},{4,0},{8,12},{12,8},{16,20},{20,16},{24,28},{28,24},{1,5},{5... | collective-permute-start | bytes 7077896 | tf_op jit(solution)/shard_map/ppermute | solution.py:799
  425.2 38.0 %collective-permute-start.36 = (bf16[368,896]{1,0:T(8,128)(2,1)}, bf16[368,896]{1,0:T(8,128)(2,1)}, u32[]{:S(2)}, u32[]{:S(2)}) collective-permute-start(bf16[368,896]{1,0:T(8,128)(2,1)} %bitcast.39), channel_id=1, source_target_pairs={{0,24},{4,28},{8,16},{12,20},{16,8},{20,12},{24,0},{28,4},{1,25},{... | collective-permute-start | bytes 1978376 | tf_op jit(solution)/shard_map/ppermute | solution.py:799
  436.4 26.8 %collective-permute-start.39 = (bf16[4,192,384]{2,1,0:T(8,128)(2,1)}, bf16[4,192,384]{2,1,0:T(8,128)(2,1)}, u32[]{:S(2)}, u32[]{:S(2)}) collective-permute-start(bf16[4,192,384]{2,1,0:T(8,128)(2,1)} %get-tuple-element.250), channel_id=1, source_target_pairs={{0,24},{4,28},{8,16},{12,20},{16,8},{20,12},{24,0},{28,4},{1,25},{... | collective-permute-start | bytes 1769480 | tf_op jit(solution)/shard_map/ppermute | solution.py:799
  438.1 30.5 %collective-permute-start.38 = (bf16[4,192,384]{2,1,0:T(8,128)(2,1)}, bf16[4,192,384]{2,1,0:T(8,128)(2,1)}, u32[]{:S(2)}, u32[]{:S(2)}) collective-permute-start(bf16[4,192,384]{2,1,0:T(8,128)(2,1)} %get-tuple-element.251), channel_id=1, source_target_pairs={{0,16},{4,20},{8,24},{12,28},{16,0},{20,4},{24,8},{28,12},{1,17},{... | collective-permute-start | bytes 1769480 | tf_op jit(solution)/shard_map/ppermute | solution.py:799
  439.4 29.1 %collective-permute-start.37 = (bf16[4,192,384]{2,1,0:T(8,128)(2,1)S(1)}, bf16[4,192,384]{2,1,0:T(8,128)(2,1)S(1)}, u32[]{:S(2)}, u32[]{:S(2)}) collective-permute-start(bf16[4,192,384]{2,1,0:T(8,128)(2,1)S(1)} %get-tuple-element.252), channel_id=1, source_target_pairs={{0,8},{4,12},{8,0},{12,4},{16,24},{20,28},{24,16},{28,20},{1,9},{5... | collective-permute-start | bytes 1769480 | tf_op jit(solution)/shard_map/ppermute | solution.py:799
  473.4 16.8 %collective-permute-start.41 = (bf16[368,896]{1,0:T(8,128)(2,1)S(1)}, bf16[368,896]{1,0:T(8,128)(2,1)S(1)}, u32[]{:S(2)}, u32[]{:S(2)}) collective-permute-start(bf16[368,896]{1,0:T(8,128)(2,1)S(1)} %add_convert_fusion.10), channel_id=1, source_target_pairs={{0,16},{4,20},{8,24},{12,28},{16,0},{20,4},{24,8},{28,12},{1,17},{... | collective-permute-start | bytes 1978376 | tf_op jit(solution)/shard_map/ppermute | solution.py:799
  474.2 16.5 %collective-permute-start.40 = (bf16[368,896]{1,0:T(8,128)(2,1)S(1)}, bf16[368,896]{1,0:T(8,128)(2,1)S(1)}, u32[]{:S(2)}, u32[]{:S(2)}) collective-permute-start(bf16[368,896]{1,0:T(8,128)(2,1)S(1)} %add_convert_fusion.10), channel_id=1, source_target_pairs={{0,8},{4,12},{8,0},{12,4},{16,24},{20,28},{24,16},{28,20},{1,9},{5... | collective-permute-start | bytes 1978376 | tf_op jit(solution)/shard_map/ppermute | solution.py:799
  505.1 21.7 %collective-permute-start.48 = (bf16[4,368,896]{2,1,0:T(8,128)(2,1)S(1)}, bf16[4,368,896]{2,1,0:T(8,128)(2,1)}, u32[]{:S(2)}, u32[]{:S(2)}) collective-permute-start(bf16[4,368,896]{2,1,0:T(8,128)(2,1)S(1)} %pad_maximum_fusion.1.refs_0_), channel_id=1, source_target_pairs={{0,4},{4,0},{8,12},{12,8},{16,20},{20,16},{24,28},{28,24},{1,5},{5... | collective-permute-start | bytes 7913480 | tf_op jit(solution)/shard_map/ppermute | solution.py:799
  506.8 8.7 %collective-permute-start.43 = (bf16[192,384]{1,0:T(8,128)(2,1)S(1)}, bf16[192,384]{1,0:T(8,128)(2,1)S(1)}, u32[]{:S(2)}, u32[]{:S(2)}) collective-permute-start(bf16[192,384]{1,0:T(8,128)(2,1)S(1)} %bitcast.139), channel_id=1, source_target_pairs={{0,16},{4,20},{8,24},{12,28},{16,0},{20,4},{24,8},{28,12},{1,17},{... | collective-permute-start | bytes 442376 | tf_op jit(solution)/shard_map/ppermute | solution.py:799
  507.3 8.2 %collective-permute-start.42 = (bf16[192,384]{1,0:T(8,128)(2,1)S(1)}, bf16[192,384]{1,0:T(8,128)(2,1)S(1)}, u32[]{:S(2)}, u32[]{:S(2)}) collective-permute-start(bf16[192,384]{1,0:T(8,128)(2,1)S(1)} %bitcast.140), channel_id=1, source_target_pairs={{0,8},{4,12},{8,0},{12,4},{16,24},{20,28},{24,16},{28,20},{1,9},{5... | collective-permute-start | bytes 442376 | tf_op jit(solution)/shard_map/ppermute | solution.py:799
  (44 other events, 326.6 us)
Sparse Core Ops, SparseCore 0:
  29.0 56.7 all-gather.8
  87.9 33.7 all-gather.10
  123.3 57.0 all-gather.12
  182.5 36.5 all-gather.14
  221.2 30.8 reduce-scatter.6
  254.4 31.0 reduce-scatter.8
  290.3 52.7 reduce-scatter.10
  346.0 52.2 reduce-scatter.12
  401.2 52.2 reduce-scatter.14
  473.5 20.9 reduce-scatter.16

commit v2 on v1

--- a/solution.py
+++ b/solution.py
@@ -14,7 +14,8 @@
 FLOOR = 1e-06
 ROOT = 0.7978845608028654
 CUBIC = 0.044715
-RB = 128
+RB = 256
+RF = 256
 MB = 512
 VMEM_LIMIT = 60 << 20
 NT = (((1,), (1,)), ((), ()))
@@ -55,8 +56,8 @@
     keys = k_ref[...]
     values = v_ref[...]
     col = col_ref[0]
-    for b in range(SEQ // RB):
-        rows = pl.ds(b * RB, RB)
+    for b in range(SEQ // RF):
+        rows = pl.ds(b * RF, RF)
         allowed = col <= row_ref[0, rows]
         ctx = None
         for side in range(2):
@@ -235,7 +236,7 @@
     c_d = load_down(copies, scal, wd, own_down, mine_d, other_d, groups)
     c_xt = copies.start(xt_h, xt)
     tokens = x.shape[0]
-    mb = MB
+    mb = 256
     c_x.wait()
     wait(c_gu)
 
@@ -367,7 +368,7 @@
     gg[...] = jnp.zeros_like(gg)
 
     def finish(m, _):
-        at = pl.ds(pl.multiple_of(m * TB, TB), TB)
+        at = pl.ds(pl.multiple_of(m * MB, MB), MB)
         back, part = norm_back_columns(middle[:, at], gain[...], acc[:, at])
         total = g[:, at].astype(f32) + back
         acc[:, at] = total
@@ -375,7 +376,7 @@
         gg[...] += part
         return 0
 
-    lax.fori_loop(0, tokens // TB, finish, 0)
+    lax.fori_loop(0, tokens // MB, finish, 0)
     wait([copies.start(g, da_h), copies.start(acc, dm_h), copies.start(gg, gg_h)])
 
 
@@ -692,8 +693,8 @@
 def gradients_kernel(*refs):
     scal = refs[0]
     mine, other = refs[1:3]
-    grads, grad_out, small, buf, sems = refs[3], refs[4], refs[5], refs[6], refs[7]
-    rows = grads.shape[1]
+    grads, (grad_out, small, buf, sems) = refs[3:6], refs[6:]
+    rows = grads[0].shape[0]
     width = buf.shape[-1]
     half = width // 2
     out_rows, d = grad_out.shape
@@ -704,7 +705,7 @@
             done.append(copies.start(arrays.at[j], buf.at[scal[1] ^ j, pl.ds(pl.multiple_of(side * half, 16), half)]))
     wait(done)
     for m in range(3):
-        grads[m] = buf[m, :rows].astype(f32)
+        grads[m][...] = buf[m, :rows].astype(f32)
     for i in range(-(-d // width)):
         n = min(width, d - i * width)
         grad_out[:, i * width : i * width + n] = buf[3, i * out_rows : (i + 1) * out_rows, :n].astype(f32)
@@ -717,9 +718,9 @@
     return pl.pallas_call(
         gradients_kernel,
         in_specs=[pl.BlockSpec(memory_space=pltpu.SMEM)] + [ANY] * 2,
-        out_specs=[V, V, V],
+        out_specs=[V] * 5,
         out_shape=[
-            jax.ShapeDtypeStruct((3, rows, width), f32),
+            *[jax.ShapeDtypeStruct((rows, width), f32)] * 3,
             jax.ShapeDtypeStruct((out_rows, d), f32),
             jax.ShapeDtypeStruct((width - rows, width), f32),
         ],
@@ -898,7 +899,7 @@
     normed_ff, gu_x, gu_y = tie(normed_ff, gu_x, gu_y)
     dn = links.others(pick(after(near_dn, context), core))
     dn_x, dn_y = links.swap(dn, XBIT), links.swap(dn, YBIT)
-    far_gu, far_dn = whole(after(gate_up_of(chip ^ 3), qkv)), whole(after(down_of(chip ^ 3), context))
+    far_gu = whole(after(gate_up_of(chip ^ 3), qkv))
     gus, dns = [near_gu], [near_dn]
     both = lambda parts: (parts, [links.swap(a, CORE) for a in parts])
 
@@ -918,16 +919,18 @@
     gu_x, gu_y, dn_x, dn_y = after((gu_x, gu_y, dn_x, dn_y), done)
     gus += [both([gu_x]), both([gu_y])]
     dns += [both([dn_x]), both([dn_y])]
-    gus.append(far_gu)
-    dns.append(far_dn)
+    far_dn = links.swap(after(dn, done), XBIT | YBIT)
     rings = [None] * 4
     rings[0] = scatter(sums_dn[0])
-    done = chunk(1, done, sums_dn[0], far_gu)
+    done = chunk(1, done)
+    done, far_dn, far_gu = tie(done, far_dn, far_gu)
+    gus.append(far_gu)
+    dns.append(both([far_dn]))
+    done = chunk(2, done, sums_dn[0])
     rings[1] = scatter(sums_dn[1])
     done, rings[0] = tie(done, rings[0])
-    done = chunk(2, done, sums_gu[0], sums_dn[1], far_dn)
+    done = chunk(3, done, sums_gu[0], sums_gu[1], sums_dn[1])
     done, rings[1] = tie(done, rings[1])
-    done = chunk(3, done, sums_gu[1], sums_dn[2])
     from_x, from_y = links.swap(sums_gu[1], XBIT), links.swap(sums_gu[2], YBIT)
     pair = scatter(jnp.stack([sums_dn[2], sums_dn[3]], axis=1))
     rings[2:] = pair[0], pair[1]
@@ -985,7 +988,7 @@
     gu_d = jnp.concatenate([links.swap(gu_x[:mid], YBIT), links.swap(gu_y[mid:], XBIT)])
     spread_gu = jnp.stack([red_gu, gu_x, gu_y, gu_d])
     grad_gate, grad_up = join_columns(scal, spread_gu, links.swap(spread_gu, CORE))
-    wide, grad_out, small = attention_gradients(scal, *spread(links.beyond(red.astype(f32)).astype(bf16)), rows, *w_out.shape)
+    *wide, grad_out, small = attention_gradients(scal, *spread(links.beyond(red.astype(f32)).astype(bf16)), rows, *w_out.shape)
     small = small.reshape(-1)
     return (
         output_t.T,

time: 548 us -> 536 us (0.978)
  Pallas kernels: 286 us -> 274 us
    pallas_call x1, Pallas kernels: 20.3 us -> 14.1 us  [attend_forward(): pl.pallas_call(attend_kernel, grid=(H // 2, n), in_specs=[pair(0), pair(1...]
    ppermute x46 -> x48, waiting for transfers between devices: 78.8 us -> 73.4 us  [swap(): return lax.ppermute(v, SHARD, [(i, i ^ bit) for i in range(self.shards)])]
    all_gather x4 -> x3, waiting for transfers between devices: 7.48 us -> 11.4 us  [local(): lax.all_gather(v, ('core', 'group')).reshape(2, groups, *v.shape)]
    ppermute x46 -> x48, starting transfers between devices: 37.4 us -> 39.9 us  [swap(): return lax.ppermute(v, SHARD, [(i, i ^ bit) for i in range(self.shards)])]
    unnamed x69 -> x55, local copies, waits for them, and re-layouts: 11.6 us -> 13.7 us
  transfers between devices with their start and end apart: 59 -> 60, of which waited for: 24 -> 22; matrix products, arithmetic and copies ran while one was open for 15% -> 15% of each run, Pallas kernels for 52% -> 51%
where the time goes in v2:
time: 536 us; the launch traced here: 529 us
  Pallas kernels  274 us (51%)
  waiting for transfers between devices  92.4 us (17%)
  other arithmetic  57.6 us (11%)
  starting transfers between devices  47.2 us (9%)
  local copies, waits for them, and re-layouts  31.6 us (6%)
  between operations  14.8 us (3%)
  matrix products  11.2 us (2%)
    pallas_call x4, Pallas kernels, ffn_chunk(): pl.pallas_call(functools.partial(ffn_kernel, groups, nparts), in_specs=[p...  114 us
    ppermute x48, waiting for transfers between devices, swap(): return lax.ppermute(v, SHARD, [(i, i ^ bit) for i in range(self.shards)])  73.4 us
    ppermute x48, starting transfers between devices, swap(): return lax.ppermute(v, SHARD, [(i, i ^ bit) for i in range(self.shards)])  39.9 us
    pallas_call x1, Pallas kernels, ffn_dx(): pl.pallas_call(functools.partial(dx_kernel, groups, tuple(counts)), in_sp...  39.7 us
    convert_element_type x11, other arithmetic, add(): return total.astype(bf16)  36.2 us
    pallas_call x1, Pallas kernels, ffn_out(): pl.pallas_call(functools.partial(out_kernel, groups, tuple(counts)), in_s...  23.2 us
    pallas_call x1, Pallas kernels, attend_backward(): pl.pallas_call(attend_back_kernel, grid=(H // 2, n), in_specs=[pair(0), p...  18.3 us
    pallas_call x1, Pallas kernels, attend_forward(): pl.pallas_call(attend_kernel, grid=(H // 2, n), in_specs=[pair(0), pair(1...  14.1 us
  transfers between devices with their start and end apart: 60, of which 22 were waited for; matrix products, arithmetic and copies ran while one was open for 15% of the time, Pallas kernels for 51%

profile of v2, /device:TPU:0, one launch (start us, length us, event | category | flops | bytes accessed | tf_op | source)
XLA Modules:
  0.0 529.0 jit_solution(16475313431655152445)
XLA Ops:
  11.2 5.1 collective-permute-start.2
  17.4 5.1 split_columns.1
  22.5 2.9 select_bitcast_fusion
  25.4 3.5 collective-permute-done.1
  29.0 2.5 collective-permute-start.5
  32.6 13.8 %collective-permute-done.5.refs_4_ = bf16[4,192,384]{2,1,0:T(8,128)(2,1)} collective-permute-done((bf16[4,192,384]{2,1,0:T(8,128)(2,1)S(1)}, bf16[4,192,384]{2,1,0:T(8,128)(2,1)}, u32[]{:S(2)}, u32[]{:S(2)}) %collective-permute-start.5) | collective-permute-done | bytes 589856 | tf_op jit(solution)/shard_map/ppermute | solution.py:800
  46.4 11.0 %collective-permute-done.4.refs_3_ = bf16[4,192,384]{2,1,0:T(8,128)(2,1)} collective-permute-done((bf16[4,192,384]{2,1,0:T(8,128)(2,1)S(1)}, bf16[4,192,384]{2,1,0:T(8,128)(2,1)}, u32[]{:S(2)}, u32[]{:S(2)}) %collective-permute-start.4) | collective-permute-done | bytes 589856 | tf_op jit(solution)/shard_map/ppermute | solution.py:800
  57.9 3.3 copy.33
  62.9 6.0 %attention_weights.1 = (bf16[1472,1152]{1,0:T(8,128)(2,1)}, bf16[1472,384]{1,0:T(8,128)(2,1)}, bf16[4,16,384]{2,1,0:T(8,128)(2,1)}) custom-call(s32[3]{0:T(128)} %add_add_fusion.refs_0_.scal, bf16[4,192,384]{2,1,0:T(8,128)(2,1)} %copy-done.8, bf16[4,192,384]{2,1,0:T(8,128)(2,1)} %collective-permute-done.3.refs_2_, ...), custom_call_target="tpu_custom_call" | custom-call | flops 6670000128 | bytes 5800000 | tf_op jit(solution)/shard_map/attention_weights/pallas_call | solution.py:677
  70.8 4.3 bias_matrix.1.bias_ref
  78.7 5.6 %convolution_convert_fusion.q_ref.k_ref.v_ref = bf16[1024,1152]{1,0:T(8,128)(2,1)} fusion(bf16[1472,1024]{1,0:T(8,128)(2,1)S(1)} %fusion.2.refs_1_, bf16[1472,1152]{1,0:T(8,128)(2,1)S(1)} %copy-done.25), kind=kOutput, calls=%fused_computation.11 | convolution fusion | flops 3474063360 | bytes 8765440 | tf_op jit(solution)/shard_map/dt,dc->tc/dot_general | solution.py:766
  91.9 2.9 copy.34.refs_3_
  97.2 14.1 %attend_forward.1 = (bf16[2,6,512,512]{3,2,1,0:T(8,128)(2,1)}, bf16[1024,384]{1,0:T(8,128)(2,1)}) custom-call(bf16[1024,1152]{1,0:T(8,128)(2,1)} %convolution_convert_fusion.q_ref.k_ref.v_ref, bf16[1024,1152]{1,0:T(8,128)(2,1)} %convolution_convert_fusion.q_ref.k_ref.v_ref, bf16[1024,1152]{1,0:T(8,128)(2,1)} %convolution_convert_fusion.q_ref.k_ref.v_ref, ...), custom_call_target="tpu_custom_call" | custom-call | flops 575000000 | bytes 500000 | tf_op jit(solution)/shard_map/attend_forward/pallas_call | solution.py:80
  111.3 10.5 %all-gather.9.cloned.1.call-done = bf16[896,1472]{1,0:T(8,128)(2,1)} async-done(((bf16[112,1472]{1,0:T(8,128)(2,1)}), bf16[896,1472]{1,0:T(8,128)(2,1)}) %all-gather.9.cloned.1.call-update) | async-done | bytes 2637840 | tf_op jit(solution)/shard_map/all_gather | solution.py:880
  127.0 8.9 %middle_norm.1 = (f32[1472,1024]{1,0:T(8,128)}, bf16[1472,1024]{1,0:T(8,128)(2,1)}, bf16[1024,1472]{1,0:T(8,128)(2,1)}) custom-call(bf16[1024,384]{1,0:T(8,128)(2,1)} %get-tuple-element.143.ctx_ref.refs_5_, bf16[1472,384]{1,0:T(8,128)(2,1)} %get-tuple-element.144.w_ref, bf16[1472,1024]{1,0:T(8,128)(2,1)} %bitcast.97, f32[1472,1]{1,0:T(8,128)} %reshape.160.gain_ref.refs_1_), custom_call_target="tpu_custom_call" | custom-call | flops 575000000 | bytes 500000 | tf_op jit(solution)/shard_map/middle_norm/pallas_call | solution.py:421
  136.7 28.5 %ffn_chunk.4 = (bf16[1024,896]{1,0:T(8,128)(2,1)}, bf16[1024,896]{1,0:T(8,128)(2,1)}, bf16[1024,896]{1,0:T(8,128)(2,1)}, bf16[1472,896]{1,0:T(8,128)(2,1)}, bf16...) custom-call(s32[3]{0:T(128)} %add_add_fusion.refs_0_.scal, ...), custom_call_target="tpu_custom_call" | custom-call | flops 34500001792 | bytes 30000000 | tf_op jit(solution)/shard_map/ffn_chunk/pallas_call | solution.py:310
  169.5 5.0 collective-permute-done.12
  174.9 2.8 add_convert_fusion.9
  179.0 28.4 %ffn_chunk.6 = (bf16[1024,896]{1,0:T(8,128)(2,1)}, bf16[1024,896]{1,0:T(8,128)(2,1)}, bf16[1024,896]{1,0:T(8,128)(2,1)}, bf16[1472,896]{1,0:T(8,128)(2,1)}, bf16...) custom-call(s32[3]{0:T(128)} %add_add_fusion.3.refs_0_, ...), custom_call_target="tpu_custom_call" | custom-call | flops 34500001792 | bytes 30000000 | tf_op jit(solution)/shard_map/ffn_chunk/pallas_call | solution.py:310
  208.4 28.4 %ffn_chunk.5 = (bf16[1024,896]{1,0:T(8,128)(2,1)}, bf16[1024,896]{1,0:T(8,128)(2,1)}, bf16[1024,896]{1,0:T(8,128)(2,1)}, bf16[1472,896]{1,0:T(8,128)(2,1)}, bf16...) custom-call(s32[3]{0:T(128)} %add_add_fusion.1.refs_0_, ...), custom_call_target="tpu_custom_call" | custom-call | flops 34500001792 | bytes 30000000 | tf_op jit(solution)/shard_map/ffn_chunk/pallas_call | solution.py:310
  238.6 3.3 add_convert_fusion.3
  242.0 2.8 add_convert_fusion.8
  245.1 4.7 add_convert_fusion.2
  249.8 28.4 %ffn_chunk.7 = (bf16[1024,896]{1,0:T(8,128)(2,1)}, bf16[1024,896]{1,0:T(8,128)(2,1)}, bf16[1024,896]{1,0:T(8,128)(2,1)}, bf16[1472,896]{1,0:T(8,128)(2,1)}, bf16...) custom-call(s32[3]{0:T(128)} %add_add_fusion.2.refs_0_, ...), custom_call_target="tpu_custom_call" | custom-call | flops 34500001792 | bytes 30000000 | tf_op jit(solution)/shard_map/ffn_chunk/pallas_call | solution.py:310
  278.6 2.1 add_convert_fusion.7
  289.2 4.7 add_convert_fusion.4
  294.8 4.8 add_convert_fusion.1
  299.7 39.7 %ffn_dx.1 = (f32[1472,1024]{1,0:T(8,128)}, bf16[1472,1024]{1,0:T(8,128)(2,1)}, f32[1472,1]{1,0:T(8,128)}) custom-call(s32[3]{0:T(128)} %add_add_fusion.refs_0_.scal, f32[1472,1]{1,0:T(8,128)} %reshape.160.gain_ref.refs_1_, f32[1472,1024]{1,0:T(8,128)} %get-tuple-element.183.refs_2_.refs_1_, bf16[1472,1024]{1,0:T(8,128)(2,1)} %bitcast.109, ...), custom_call_target="tpu_custom_call" | custom-call | flops 40249999360 | bytes 35000000 | tf_op jit(solution)/shard_map/ffn_dx/pallas_call | solution.py:397
  340.9 4.9 convolution_convert_fusion.1.dctx_ref
  346.9 6.7 %collective-permute-done.29 = bf16[1472,896]{1,0:T(8,128)(2,1)} collective-permute-done((bf16[1472,896]{1,0:T(8,128)(2,1)}, bf16[1472,896]{1,0:T(8,128)(2,1)}, u32[]{:S(2)}, u32[]{:S(2)}) %collective-permute-start.29) | collective-permute-done | bytes 2637856 | tf_op jit(solution)/shard_map/ppermute | solution.py:800
  357.1 18.3 %attend_backward.1 = (bf16[1024,384]{1,0:T(8,128)(2,1)}, bf16[1024,384]{1,0:T(8,128)(2,1)}, bf16[1024,384]{1,0:T(8,128)(2,1)}, f32[6,1,1024]{2,1,0:T(1,128)}) custom-call(bf16[1024,1152]{1,0:T(8,128)(2,1)} %convolution_convert_fusion.q_ref.k_ref.v_ref, bf16[1024,1152]{1,0:T(8,128)(2,1)} %convolution_convert_fusion.q_ref.k_ref.v_ref, ...), custom_call_target="tpu_custom_call" | custom-call | flops 25300000768 | bytes 22000000 | tf_op jit(solution)/shard_map/attend_backward/pallas_call | solution.py:143
  375.4 5.0 add_convert_fusion
  386.3 12.0 %input_gradient.1 = (bf16[1472,1024]{1,0:T(8,128)(2,1)}, f32[1472,1]{1,0:T(8,128)}) custom-call(bf16[1024,384]{1,0:T(8,128)(2,1)} %get-tuple-element.206.dq_ref.refs_2_, bf16[1024,384]{1,0:T(8,128)(2,1)} %get-tuple-element.207.dk_ref.refs_3_, bf16[1024,384]{1,0:T(8,128)(2,1)} %get-tuple-element.208.dv_ref.refs_4_, ...), custom_call_target="tpu_custom_call" | custom-call | flops 9200000000 | bytes 8000000 | tf_op jit(solution)/shard_map/input_gradient/pallas_call | solution.py:452
  400.6 13.2 %attention_matrices.1 = (bf16[4,4,192,384]{3,2,1,0:T(8,128)(2,1)}, bf16[4,4,192,384]{3,2,1,0:T(8,128)(2,1)}) custom-call(s32[3]{0:T(128)} %add_add_fusion.refs_0_.scal, bf16[1472,1024]{1,0:T(8,128)(2,1)} %copy-done.3, bf16[1024,384]{1,0:T(8,128)(2,1)} %get-tuple-element.206.dq_ref.refs_2_, bf16[1024,384]{1,0:T(8,128)(2,1)} %get-tuple-element.207.dk_ref.refs_3_, ...), custom_call_target="tpu_custom_call" | custom-call | flops 10350000128 | bytes 9000000 | tf_op jit(solution)/shard_map/attention_matrices/pallas_call | solution.py:505
  414.6 2.0 collective-permute-start.38
  416.6 3.7 collective-permute-done.36.refs_2_
  421.5 3.1 add_convert_fusion.5
  429.3 23.2 %ffn_out.1 = bf16[1472,1024]{1,0:T(8,128)(2,1)} custom-call(s32[3]{0:T(128)} %add_add_fusion.refs_0_.scal, f32[1472,1024]{1,0:T(8,128)} %get-tuple-element.183.refs_2_.refs_1_, bf16[4,224,1472]{2,1,0:T(8,128)(2,1)} %bitcast.108, bf16[1024,896]{1,0:T(8,128)(2,1)} %get-tuple-element.156.refs_3_, bf16[2,4,112,1472]{3,2,1,0:T(8,128)(2,1)} %bitcast.123, ...), custom_call_target="tpu_custom_call" | custom-call | flops 24149999616 | bytes 21000000 | tf_op jit(solution)/shard_map/ffn_out/pallas_call | solution.py:574
  452.5 5.4 %collective-permute-done.40 = bf16[4,192,384]{2,1,0:T(8,128)(2,1)} collective-permute-done((bf16[4,192,384]{2,1,0:T(8,128)(2,1)}, bf16[4,192,384]{2,1,0:T(8,128)(2,1)}, u32[]{:S(2)}, u32[]{:S(2)}) %collective-permute-start.40) | collective-permute-done | bytes 589856 | tf_op jit(solution)/shard_map/ppermute | solution.py:800
  460.2 2.6 fusion.5
  465.4 5.6 %down_gradient.1 = f32[1472,896]{1,0:T(8,128)} custom-call(s32[3]{0:T(128)} %add_add_fusion.refs_0_.scal, bf16[4,112,1472]{2,1,0:T(8,128)(2,1)} %copy-done.5, bf16[4,112,1472]{2,1,0:T(8,128)(2,1)} %copy-done.18), custom_call_target="tpu_custom_call" | custom-call | flops 6440000000 | bytes 5600000 | tf_op jit(solution)/shard_map/down_gradient/pallas_call | solution.py:753
  471.0 8.5 %collective-permute-done.43 = bf16[368,896]{1,0:T(8,128)(2,1)S(1)} collective-permute-done((bf16[368,896]{1,0:T(8,128)(2,1)S(1)}, bf16[368,896]{1,0:T(8,128)(2,1)S(1)}, u32[]{:S(2)}, u32[]{:S(2)}) %collective-permute-start.43) | collective-permute-done | bytes 659488 | tf_op jit(solution)/shard_map/ppermute | solution.py:800
  480.5 4.0 reduce-scatter.17.cloned.1.call-done
  487.5 4.5 collective-permute-done.49
  498.6 4.1 collective-permute-done.46
  502.7 2.7 collective-permute-done.45
  508.5 3.5 attention_gradients.1
  515.6 6.6 %join_columns.1 = (f32[368,3584]{1,0:T(8,128)}, f32[368,3584]{1,0:T(8,128)}) custom-call(s32[3]{0:T(128)} %add_add_fusion.refs_0_.scal, bf16[4,368,896]{2,1,0:T(8,128)(2,1)} %pad_maximum_fusion.1.refs_0_, bf16[4,368,896]{2,1,0:T(8,128)(2,1)} %copy-done.17), custom_call_target="tpu_custom_call" | custom-call | flops 7474999808 | bytes 6500000 | tf_op jit(solution)/shard_map/join_columns/pallas_call | solution.py:635
  (220 shorter events, 91.6 us)
Async XLA Ops:
  7.2 78.6 %all-gather.7.cloned.1.call-start = ((), (), s32[]{:S(2)}) async-start(), calls=%async_computation.12 | async-start | bytes 5935104 | tf_op jit(solution)/shard_map/all_gather | solution.py:880
  11.2 14.1 %collective-permute-start.2 = (bf16[192,384]{1,0:T(8,128)(2,1)S(1)}, bf16[192,384]{1,0:T(8,128)(2,1)S(1)}, u32[]{:S(2)}, u32[]{:S(2)}) collective-permute-start(bf16[192,384]{1,0:T(8,128)(2,1)S(1)} %bitcast.118), channel_id=1, source_target_pairs={{0,3},{1,0},{2,1},{3,2},{4,7},{5,4},{6,5},{7,6},{8,11},{9,8},{10,9... | collective-permute-start | bytes 442376 | tf_op jit(solution)/shard_map/ppermute | solution.py:803
  16.3 12.5 %collective-permute-start.1 = (bf16[192,384]{1,0:T(8,128)(2,1)S(1)}, bf16[192,384]{1,0:T(8,128)(2,1)S(1)}, u32[]{:S(2)}, u32[]{:S(2)}) collective-permute-start(bf16[192,384]{1,0:T(8,128)(2,1)S(1)} %bitcast.119), channel_id=1, source_target_pairs={{0,2},{1,3},{2,0},{3,1},{4,6},{5,7},{6,4},{7,5},{8,10},{9,11},{10,... | collective-permute-start | bytes 442376 | tf_op jit(solution)/shard_map/ppermute | solution.py:803
  16.3 12.5 %collective-permute-start = (bf16[192,384]{1,0:T(8,128)(2,1)S(1)}, bf16[192,384]{1,0:T(8,128)(2,1)S(1)}, u32[]{:S(2)}, u32[]{:S(2)}) collective-permute-start(bf16[192,384]{1,0:T(8,128)(2,1)S(1)} %bitcast.120), channel_id=1, source_target_pairs={{0,1},{1,2},{2,3},{3,0},{4,5},{5,6},{6,7},{7,4},{8,9},{9,10},{10,1... | collective-permute-start | bytes 442376 | tf_op jit(solution)/shard_map/ppermute | solution.py:803
  28.9 92.9 %all-gather.9.cloned.1.call-start = ((), (), s32[]{:S(2)}) async-start(), calls=%async_computation.13 | async-start | bytes 3096576 | tf_op jit(solution)/shard_map/all_gather | solution.py:880
  29.0 17.4 %collective-permute-start.5 = (bf16[4,192,384]{2,1,0:T(8,128)(2,1)S(1)}, bf16[4,192,384]{2,1,0:T(8,128)(2,1)}, u32[]{:S(2)}, u32[]{:S(2)}) collective-permute-start(bf16[4,192,384]{2,1,0:T(8,128)(2,1)S(1)} %pad_maximum_fusion.5.refs_1_), channel_id=1, source_target_pairs={{0,24},{4,28},{8,16},{12,20},{16,8},{20,12},{24,0},{28,4},{1,25},{... | collective-permute-start | bytes 1769480 | tf_op jit(solution)/shard_map/ppermute | solution.py:800
  31.5 25.8 %collective-permute-start.4 = (bf16[4,192,384]{2,1,0:T(8,128)(2,1)S(1)}, bf16[4,192,384]{2,1,0:T(8,128)(2,1)}, u32[]{:S(2)}, u32[]{:S(2)}) collective-permute-start(bf16[4,192,384]{2,1,0:T(8,128)(2,1)S(1)} %pad_maximum_fusion.5.refs_1_), channel_id=1, source_target_pairs={{0,16},{4,20},{8,24},{12,28},{16,0},{20,4},{24,8},{28,12},{1,17},{... | collective-permute-start | bytes 1769480 | tf_op jit(solution)/shard_map/ppermute | solution.py:800
  32.0 25.4 %collective-permute-start.3 = (bf16[4,192,384]{2,1,0:T(8,128)(2,1)S(1)}, bf16[4,192,384]{2,1,0:T(8,128)(2,1)}, u32[]{:S(2)}, u32[]{:S(2)}) collective-permute-start(bf16[4,192,384]{2,1,0:T(8,128)(2,1)S(1)} %pad_maximum_fusion.5.refs_1_), channel_id=1, source_target_pairs={{0,8},{4,12},{8,0},{12,4},{16,24},{20,28},{24,16},{28,20},{1,9},{5... | collective-permute-start | bytes 1769480 | tf_op jit(solution)/shard_map/ppermute | solution.py:800
  32.6 30.3 %collective-permute-start.6 = (bf16[4,192,384]{2,1,0:T(8,128)(2,1)S(1)}, bf16[4,192,384]{2,1,0:T(8,128)(2,1)}, u32[]{:S(2)}, u32[]{:S(2)}) collective-permute-start(bf16[4,192,384]{2,1,0:T(8,128)(2,1)S(1)} %pad_maximum_fusion.5.refs_1_), channel_id=1, source_target_pairs={{0,4},{4,0},{8,12},{12,8},{16,20},{20,16},{24,28},{28,24},{1,5},{5... | collective-permute-start | bytes 1769480 | tf_op jit(solution)/shard_map/ppermute | solution.py:800
  46.4 16.4 %collective-permute-start.9 = (bf16[4,192,384]{2,1,0:T(8,128)(2,1)}, bf16[4,192,384]{2,1,0:T(8,128)(2,1)}, u32[]{:S(2)}, u32[]{:S(2)}) collective-permute-start(bf16[4,192,384]{2,1,0:T(8,128)(2,1)} %collective-permute-done.5.refs_4_), channel_id=1, source_target_pairs={{0,4},{4,0},{8,12},{12,8},{16,20},{20,16},{24,28},{28,24},{1,5},{5... | collective-permute-start | bytes 1769480 | tf_op jit(solution)/shard_map/ppermute | solution.py:800
  75.2 132.3 %all-gather.11.cloned.1.call-start = ((), (), s32[]{:S(2)}) async-start(), calls=%async_computation.14 | async-start | bytes 5935104 | tf_op jit(solution)/shard_map/all_gather | solution.py:880
  84.3 201.4 %reduce-scatter.7.cloned.1.call-start = ((), (), s32[]{:S(2)}) async-start(), calls=%async_computation.6 | async-start | bytes 1720320 | tf_op jit(solution)/shard_map/reduce_scatter | solution.py:917
  89.0 46.9 %collective-permute-start.11 = (bf16[3,368,896]{2,1,0:T(8,128)(2,1)}, bf16[3,368,896]{2,1,0:T(8,128)(2,1)}, u32[]{:S(2)}, u32[]{:S(2)}) collective-permute-start(bf16[3,368,896]{2,1,0:T(8,128)(2,1)} %pad_maximum_fusion.2), channel_id=1, source_target_pairs={{0,16},{4,20},{8,24},{12,28},{16,0},{20,4},{24,8},{28,12},{1,17},{... | collective-permute-start | bytes 5935112 | tf_op jit(solution)/shard_map/ppermute | solution.py:800
  90.4 46.3 %collective-permute-start.10 = (bf16[3,368,896]{2,1,0:T(8,128)(2,1)}, bf16[3,368,896]{2,1,0:T(8,128)(2,1)}, u32[]{:S(2)}, u32[]{:S(2)}) collective-permute-start(bf16[3,368,896]{2,1,0:T(8,128)(2,1)} %pad_maximum_fusion.2), channel_id=1, source_target_pairs={{0,8},{4,12},{8,0},{12,4},{16,24},{20,28},{24,16},{28,20},{1,9},{5... | collective-permute-start | bytes 5935112 | tf_op jit(solution)/shard_map/ppermute | solution.py:800
  124.1 41.1 %collective-permute-start.14 = (bf16[3,112,1472]{2,1,0:T(8,128)(2,1)}, bf16[3,112,1472]{2,1,0:T(8,128)(2,1)}, u32[]{:S(2)}, u32[]{:S(2)}) collective-permute-start(bf16[3,112,1472]{2,1,0:T(8,128)(2,1)} %pad_maximum_fusion.4), channel_id=1, source_target_pairs={{0,16},{4,20},{8,24},{12,28},{16,0},{20,4},{24,8},{28,12},{1,17},{... | collective-permute-start | bytes 2967560 | tf_op jit(solution)/shard_map/ppermute | solution.py:800
  125.6 39.7 %collective-permute-start.13 = (bf16[3,112,1472]{2,1,0:T(8,128)(2,1)}, bf16[3,112,1472]{2,1,0:T(8,128)(2,1)S(1)}, u32[]{:S(2)}, u32[]{:S(2)}) collective-permute-start(bf16[3,112,1472]{2,1,0:T(8,128)(2,1)} %pad_maximum_fusion.4), channel_id=1, source_target_pairs={{0,8},{4,12},{8,0},{12,4},{16,24},{20,28},{24,16},{28,20},{1,9},{5... | collective-permute-start | bytes 2967560 | tf_op jit(solution)/shard_map/ppermute | solution.py:800
  165.2 13.8 %collective-permute-start.19 = (bf16[3,368,896]{2,1,0:T(8,128)(2,1)}, bf16[3,368,896]{2,1,0:T(8,128)(2,1)}, u32[]{:S(2)}, u32[]{:S(2)}) collective-permute-start(bf16[3,368,896]{2,1,0:T(8,128)(2,1)} %collective-permute-done.10.refs_7_.refs_11_), channel_id=1, source_target_pairs={{0,4},{4,0},{8,12},{12,8},{16,20},{20,16},{24,28},{28,24},{1,5},{5... | collective-permute-start | bytes 5935112 | tf_op jit(solution)/shard_map/ppermute | solution.py:800
  165.3 9.2 %collective-permute-start.12 = (bf16[4,112,1472]{2,1,0:T(8,128)(2,1)}, bf16[4,112,1472]{2,1,0:T(8,128)(2,1)S(1)}, u32[]{:S(2)}, u32[]{:S(2)}) collective-permute-start(bf16[4,112,1472]{2,1,0:T(8,128)(2,1)} %get-tuple-element.151), channel_id=1, source_target_pairs={{0,4},{4,0},{8,12},{12,8},{16,20},{20,16},{24,28},{28,24},{1,5},{5... | collective-permute-start | bytes 3956744 | tf_op jit(solution)/shard_map/ppermute | solution.py:800
  165.8 12.1 %collective-permute-start.20 = (bf16[3,112,1472]{2,1,0:T(8,128)(2,1)S(1)}, bf16[3,112,1472]{2,1,0:T(8,128)(2,1)S(1)}, u32[]{:S(2)}, u32[]{:S(2)}) collective-permute-start(bf16[3,112,1472]{2,1,0:T(8,128)(2,1)S(1)} %collective-permute-done.13.refs_9_.refs_6_), channel_id=1, source_target_pairs={{0,4},{4,0},{8,12},{12,8},{16,20},{20,16},{24,28},{28,24},{1,5},{5... | collective-permute-start | bytes 2967560 | tf_op jit(solution)/shard_map/ppermute | solution.py:800
  167.7 40.5 %collective-permute-start.16 = (bf16[3,112,1472]{2,1,0:T(8,128)(2,1)}, bf16[3,112,1472]{2,1,0:T(8,128)(2,1)}, u32[]{:S(2)}, u32[]{:S(2)}) collective-permute-start(bf16[3,112,1472]{2,1,0:T(8,128)(2,1)} %collective-permute-done.14.refs_9_), channel_id=1, source_target_pairs={{0,4},{4,0},{8,12},{12,8},{16,20},{20,16},{24,28},{28,24},{1,5},{5... | collective-permute-start | bytes 2967560 | tf_op jit(solution)/shard_map/ppermute | solution.py:800
  168.1 39.4 %collective-permute-start.23 = (bf16[3,112,1472]{2,1,0:T(8,128)(2,1)}, bf16[3,112,1472]{2,1,0:T(8,128)(2,1)}, u32[]{:S(2)}, u32[]{:S(2)}) collective-permute-start(bf16[3,112,1472]{2,1,0:T(8,128)(2,1)} %pad_maximum_fusion.4), channel_id=1, source_target_pairs={{0,24},{4,28},{8,16},{12,20},{16,8},{20,12},{24,0},{28,4},{1,25},{... | collective-permute-start | bytes 2967560 | tf_op jit(solution)/shard_map/ppermute | solution.py:800
  174.5 33.9 %collective-permute-start.15 = (bf16[3,368,896]{2,1,0:T(8,128)(2,1)}, bf16[3,368,896]{2,1,0:T(8,128)(2,1)}, u32[]{:S(2)}, u32[]{:S(2)}) collective-permute-start(bf16[3,368,896]{2,1,0:T(8,128)(2,1)} %collective-permute-done.11.refs_7_.refs_15_), channel_id=1, source_target_pairs={{0,4},{4,0},{8,12},{12,8},{16,20},{20,16},{24,28},{28,24},{1,5},{5... | collective-permute-start | bytes 5935112 | tf_op jit(solution)/shard_map/ppermute | solution.py:800
  177.7 117.1 %reduce-scatter.9.cloned.1.call-start = ((), (), s32[]{:S(2)}) async-start(), calls=%async_computation.7 | async-start | bytes 1720320 | tf_op jit(solution)/shard_map/reduce_scatter | solution.py:917
  178.9 58.3 %collective-permute-start.18 = (bf16[1472,896]{1,0:T(8,128)(2,1)}, bf16[1472,896]{1,0:T(8,128)(2,1)S(1)}, u32[]{:S(2)}, u32[]{:S(2)}) collective-permute-start(bf16[1472,896]{1,0:T(8,128)(2,1)} %get-tuple-element.162), channel_id=1, source_target_pairs={{0,4},{4,0},{8,12},{12,8},{16,20},{20,16},{24,28},{28,24},{1,5},{5... | collective-permute-start | bytes 7913480 | tf_op jit(solution)/shard_map/ppermute | solution.py:800
  207.5 42.3 %collective-permute-start.24 = (bf16[3,112,1472]{2,1,0:T(8,128)(2,1)}, bf16[3,112,1472]{2,1,0:T(8,128)(2,1)}, u32[]{:S(2)}, u32[]{:S(2)}) collective-permute-start(bf16[3,112,1472]{2,1,0:T(8,128)(2,1)} %collective-permute-done.23.refs_8_.refs_12_), channel_id=1, source_target_pairs={{0,4},{4,0},{8,12},{12,8},{16,20},{20,16},{24,28},{28,24},{1,5},{5... | collective-permute-start | bytes 2967560 | tf_op jit(solution)/shard_map/ppermute | solution.py:800
  207.9 34.0 %collective-permute-start.22 = (bf16[4,112,1472]{2,1,0:T(8,128)(2,1)}, bf16[4,112,1472]{2,1,0:T(8,128)(2,1)}, u32[]{:S(2)}, u32[]{:S(2)}) collective-permute-start(bf16[4,112,1472]{2,1,0:T(8,128)(2,1)} %get-tuple-element.169), channel_id=1, source_target_pairs={{0,4},{4,0},{8,12},{12,8},{16,20},{20,16},{24,28},{28,24},{1,5},{5... | collective-permute-start | bytes 3956744 | tf_op jit(solution)/shard_map/ppermute | solution.py:800
  208.1 37.0 %collective-permute-start.21 = (bf16[1472,896]{1,0:T(8,128)(2,1)}, bf16[1472,896]{1,0:T(8,128)(2,1)}, u32[]{:S(2)}, u32[]{:S(2)}) collective-permute-start(bf16[1472,896]{1,0:T(8,128)(2,1)} %get-tuple-element.167), channel_id=1, source_target_pairs={{0,4},{4,0},{8,12},{12,8},{16,20},{20,16},{24,28},{28,24},{1,5},{5... | collective-permute-start | bytes 7913480 | tf_op jit(solution)/shard_map/ppermute | solution.py:800
  236.9 41.7 %collective-permute-start.26 = (bf16[4,112,1472]{2,1,0:T(8,128)(2,1)}, bf16[4,112,1472]{2,1,0:T(8,128)(2,1)}, u32[]{:S(2)}, u32[]{:S(2)}) collective-permute-start(bf16[4,112,1472]{2,1,0:T(8,128)(2,1)} %get-tuple-element.179), channel_id=1, source_target_pairs={{0,4},{4,0},{8,12},{12,8},{16,20},{20,16},{24,28},{28,24},{1,5},{5... | collective-permute-start | bytes 3956744 | tf_op jit(solution)/shard_map/ppermute | solution.py:800
  244.8 100.9 %reduce-scatter.11.cloned.1.call-start = ((), (), s32[]{:S(2)}) async-start(), calls=%async_computation.8 | async-start | bytes 3440640 | tf_op jit(solution)/shard_map/reduce_scatter | solution.py:917
  283.8 116.8 %reduce-scatter.13.cloned.1.call-start = ((), (), s32[]{:S(2)}) async-start(), calls=%async_computation.9 | async-start | bytes 3297280 | tf_op jit(solution)/shard_map/reduce_scatter | solution.py:917
  284.2 10.6 %collective-permute-start.25 = (bf16[1472,896]{1,0:T(8,128)(2,1)}, bf16[1472,896]{1,0:T(8,128)(2,1)}, u32[]{:S(2)}, u32[]{:S(2)}) collective-permute-start(bf16[1472,896]{1,0:T(8,128)(2,1)} %get-tuple-element.177), channel_id=1, source_target_pairs={{0,4},{4,0},{8,12},{12,8},{16,20},{20,16},{24,28},{28,24},{1,5},{5... | collective-permute-start | bytes 7913480 | tf_op jit(solution)/shard_map/ppermute | solution.py:800
  285.7 61.2 %collective-permute-start.28 = (bf16[1472,896]{1,0:T(8,128)(2,1)}, bf16[1472,896]{1,0:T(8,128)(2,1)}, u32[]{:S(2)}, u32[]{:S(2)}) collective-permute-start(bf16[1472,896]{1,0:T(8,128)(2,1)} %add_convert_fusion.2), channel_id=1, source_target_pairs={{0,8},{4,12},{8,0},{12,4},{16,24},{20,28},{24,16},{28,20},{1,9},{5... | collective-permute-start | bytes 7913480 | tf_op jit(solution)/shard_map/ppermute | solution.py:800
  293.9 59.7 %collective-permute-start.29 = (bf16[1472,896]{1,0:T(8,128)(2,1)}, bf16[1472,896]{1,0:T(8,128)(2,1)}, u32[]{:S(2)}, u32[]{:S(2)}) collective-permute-start(bf16[1472,896]{1,0:T(8,128)(2,1)} %add_convert_fusion.4), channel_id=1, source_target_pairs={{0,16},{4,20},{8,24},{12,28},{16,0},{20,4},{24,8},{28,12},{1,17},{... | collective-permute-start | bytes 7913480 | tf_op jit(solution)/shard_map/ppermute | solution.py:800
  299.6 158.3 %reduce-scatter.15.cloned.1.call-start = ((), (), s32[]{:S(2)}) async-start(), calls=%async_computation.10 | async-start | bytes 3297280 | tf_op jit(solution)/shard_map/reduce_scatter | solution.py:917
  353.6 27.4 %collective-permute-start.30 = (bf16[112,1472]{1,0:T(8,128)(2,1)}, bf16[112,1472]{1,0:T(8,128)(2,1)}, u32[]{:S(2)}, u32[]{:S(2)}) collective-permute-start(bf16[112,1472]{1,0:T(8,128)(2,1)} %bitcast.145), channel_id=1, source_target_pairs={{0,8},{4,12},{8,0},{12,4},{16,24},{20,28},{24,16},{28,20},{1,9},{5... | collective-permute-start | bytes 989192 | tf_op jit(solution)/shard_map/ppermute | solution.py:800
  355.1 26.0 %collective-permute-start.31 = (bf16[112,1472]{1,0:T(8,128)(2,1)S(1)}, bf16[112,1472]{1,0:T(8,128)(2,1)}, u32[]{:S(2)}, u32[]{:S(2)}) collective-permute-start(bf16[112,1472]{1,0:T(8,128)(2,1)S(1)} %get-tuple-element.201), channel_id=1, source_target_pairs={{0,16},{4,20},{8,24},{12,28},{16,0},{20,4},{24,8},{28,12},{1,17},{... | collective-permute-start | bytes 989192 | tf_op jit(solution)/shard_map/ppermute | solution.py:800
  356.0 25.1 %collective-permute-start.32 = (bf16[112,1472]{1,0:T(8,128)(2,1)S(1)}, bf16[112,1472]{1,0:T(8,128)(2,1)}, u32[]{:S(2)}, u32[]{:S(2)}) collective-permute-start(bf16[112,1472]{1,0:T(8,128)(2,1)S(1)} %get-tuple-element.202), channel_id=1, source_target_pairs={{0,24},{4,28},{8,16},{12,20},{16,8},{20,12},{24,0},{28,4},{1,25},{... | collective-permute-start | bytes 989192 | tf_op jit(solution)/shard_map/ppermute | solution.py:800
  381.0 103.4 %reduce-scatter.17.cloned.1.call-start = ((), (), s32[]{:S(2)}) async-start(), calls=%async_computation.11 | async-start | bytes 737280 | tf_op jit(solution)/shard_map/reduce_scatter | solution.py:917
  382.7 17.8 %collective-permute-start.35 = (bf16[112,1472]{1,0:T(8,128)(2,1)S(1)}, bf16[112,1472]{1,0:T(8,128)(2,1)S(1)}, u32[]{:S(2)}, u32[]{:S(2)}) collective-permute-start(bf16[112,1472]{1,0:T(8,128)(2,1)S(1)} %add_convert_fusion.11), channel_id=1, source_target_pairs={{0,24},{4,28},{8,16},{12,20},{16,8},{20,12},{24,0},{28,4},{1,25},{... | collective-permute-start | bytes 989192 | tf_op jit(solution)/shard_map/ppermute | solution.py:800
  384.6 15.9 %collective-permute-start.34 = (bf16[112,1472]{1,0:T(8,128)(2,1)S(1)}, bf16[112,1472]{1,0:T(8,128)(2,1)S(1)}, u32[]{:S(2)}, u32[]{:S(2)}) collective-permute-start(bf16[112,1472]{1,0:T(8,128)(2,1)S(1)} %add_convert_fusion.11), channel_id=1, source_target_pairs={{0,16},{4,20},{8,24},{12,28},{16,0},{20,4},{24,8},{28,12},{1,17},{... | collective-permute-start | bytes 989192 | tf_op jit(solution)/shard_map/ppermute | solution.py:800
  385.7 14.8 %collective-permute-start.33 = (bf16[112,1472]{1,0:T(8,128)(2,1)S(1)}, bf16[112,1472]{1,0:T(8,128)(2,1)S(1)}, u32[]{:S(2)}, u32[]{:S(2)}) collective-permute-start(bf16[112,1472]{1,0:T(8,128)(2,1)S(1)} %add_convert_fusion.11), channel_id=1, source_target_pairs={{0,8},{4,12},{8,0},{12,4},{16,24},{20,28},{24,16},{28,20},{1,9},{5... | collective-permute-start | bytes 989192 | tf_op jit(solution)/shard_map/ppermute | solution.py:800
  414.6 37.9 %collective-permute-start.38 = (bf16[368,896]{1,0:T(8,128)(2,1)}, bf16[368,896]{1,0:T(8,128)(2,1)}, u32[]{:S(2)}, u32[]{:S(2)}) collective-permute-start(bf16[368,896]{1,0:T(8,128)(2,1)} %bitcast.37), channel_id=1, source_target_pairs={{0,24},{4,28},{8,16},{12,20},{16,8},{20,12},{24,0},{28,4},{1,25},{... | collective-permute-start | bytes 1978376 | tf_op jit(solution)/shard_map/ppermute | solution.py:800
  425.8 26.7 %collective-permute-start.41 = (bf16[4,192,384]{2,1,0:T(8,128)(2,1)}, bf16[4,192,384]{2,1,0:T(8,128)(2,1)}, u32[]{:S(2)}, u32[]{:S(2)}) collective-permute-start(bf16[4,192,384]{2,1,0:T(8,128)(2,1)} %get-tuple-element.256), channel_id=1, source_target_pairs={{0,24},{4,28},{8,16},{12,20},{16,8},{20,12},{24,0},{28,4},{1,25},{... | collective-permute-start | bytes 1769480 | tf_op jit(solution)/shard_map/ppermute | solution.py:800
  427.8 30.1 %collective-permute-start.40 = (bf16[4,192,384]{2,1,0:T(8,128)(2,1)}, bf16[4,192,384]{2,1,0:T(8,128)(2,1)}, u32[]{:S(2)}, u32[]{:S(2)}) collective-permute-start(bf16[4,192,384]{2,1,0:T(8,128)(2,1)} %get-tuple-element.257), channel_id=1, source_target_pairs={{0,16},{4,20},{8,24},{12,28},{16,0},{20,4},{24,8},{28,12},{1,17},{... | collective-permute-start | bytes 1769480 | tf_op jit(solution)/shard_map/ppermute | solution.py:800
  428.7 29.2 %collective-permute-start.39 = (bf16[4,192,384]{2,1,0:T(8,128)(2,1)S(1)}, bf16[4,192,384]{2,1,0:T(8,128)(2,1)S(1)}, u32[]{:S(2)}, u32[]{:S(2)}) collective-permute-start(bf16[4,192,384]{2,1,0:T(8,128)(2,1)S(1)} %get-tuple-element.258), channel_id=1, source_target_pairs={{0,8},{4,12},{8,0},{12,4},{16,24},{20,28},{24,16},{28,20},{1,9},{5... | collective-permute-start | bytes 1769480 | tf_op jit(solution)/shard_map/ppermute | solution.py:800
  462.8 16.8 %collective-permute-start.43 = (bf16[368,896]{1,0:T(8,128)(2,1)S(1)}, bf16[368,896]{1,0:T(8,128)(2,1)S(1)}, u32[]{:S(2)}, u32[]{:S(2)}) collective-permute-start(bf16[368,896]{1,0:T(8,128)(2,1)S(1)} %add_convert_fusion.10), channel_id=1, source_target_pairs={{0,16},{4,20},{8,24},{12,28},{16,0},{20,4},{24,8},{28,12},{1,17},{... | collective-permute-start | bytes 1978376 | tf_op jit(solution)/shard_map/ppermute | solution.py:800
  464.0 16.5 %collective-permute-start.42 = (bf16[368,896]{1,0:T(8,128)(2,1)S(1)}, bf16[368,896]{1,0:T(8,128)(2,1)S(1)}, u32[]{:S(2)}, u32[]{:S(2)}) collective-permute-start(bf16[368,896]{1,0:T(8,128)(2,1)S(1)} %add_convert_fusion.10), channel_id=1, source_target_pairs={{0,8},{4,12},{8,0},{12,4},{16,24},{20,28},{24,16},{28,20},{1,9},{5... | collective-permute-start | bytes 1978376 | tf_op jit(solution)/shard_map/ppermute | solution.py:800
  495.1 19.0 %collective-permute-start.50 = (bf16[4,368,896]{2,1,0:T(8,128)(2,1)}, bf16[4,368,896]{2,1,0:T(8,128)(2,1)S(1)}, u32[]{:S(2)}, u32[]{:S(2)}) collective-permute-start(bf16[4,368,896]{2,1,0:T(8,128)(2,1)} %pad_maximum_fusion.1.refs_0_), channel_id=1, source_target_pairs={{0,4},{4,0},{8,12},{12,8},{16,20},{20,16},{24,28},{28,24},{1,5},{5... | collective-permute-start | bytes 7913480 | tf_op jit(solution)/shard_map/ppermute | solution.py:800
  (38 other events, 197.8 us)
Sparse Core Ops, SparseCore 0:
  29.0 56.7 all-gather.6
  87.9 33.7 all-gather.8
  123.3 55.5 all-gather.10
  181.1 30.8 reduce-scatter.6
  244.9 30.7 reduce-scatter.8
  283.9 52.8 reduce-scatter.10
  339.7 52.3 reduce-scatter.12
  394.9 52.1 reduce-scatter.14
  462.9 21.5 reduce-scatter.16
